TPU v7x, 32 devices: a whole 2x2x4 slice. The times are simulated.
32 devices in a mesh: rep: 4 (over x, core), shard: 8 (over z, y).
Axes of the slice: x: 2, y: 2, z: 4, core: 2. Of those that a mesh axis runs over, the one named last changes fastest.
Arguments:
- hidden: float32 [64, 1024, 768], P(('rep', 'shard')), may hold values from -6 to 6
- lengths: int32 [64], P(('rep', 'shard')), may hold values from 256 to 1024, as said below
- clusters: int32 [64, 12, 1024], P(('rep', 'shard')), may hold values from 0 to 1023, each once within a row
- input_weight: bfloat16 [768, 2304], P('shard'), may hold values from -0.3125 to 0.3125
- query_bias: bfloat16 [768], P('shard'), may hold values from -3 to 3
- value_bias: bfloat16 [768], P('shard'), may hold values from -1.1953125 to 1.1953125
- out_weight: bfloat16 [768, 768], P('shard'), may hold values from -0.875 to 0.875
- out_bias: bfloat16 [768], P('shard'), may hold values from -1.1953125 to 1.1953125
- norm1_gain: bfloat16 [768], P('shard'), may hold values from 0.5 to 1.5
- norm1_bias: bfloat16 [768], P('shard'), may hold values from -1.1953125 to 1.1953125
- up_weight: bfloat16 [768, 3072], P('shard'), may hold values from -0.21875 to 0.21875
- up_bias: bfloat16 [3072], P('shard'), may hold values from -1.796875 to 1.796875
- down_weight: bfloat16 [3072, 768], P('shard'), may hold values from -0.15625 to 0.15625
- down_bias: bfloat16 [768], P('shard'), may hold values from -1.1953125 to 1.1953125
- norm2_gain: bfloat16 [768], P('shard'), may hold values from 0.5 to 1.5
- norm2_bias: bfloat16 [768], P('shard'), may hold values from -1.1953125 to 1.1953125
- cotangent: float32 [64, 1024, 768], P(('rep', 'shard')), may hold values from -6 to 6
Outputs:
- output: float32 [64, 1024, 768], P(('rep', 'shard'))
- input_grad: float32 [64, 1024, 768], P(('rep', 'shard'))
- input_weight_grad: float32 [768, 2304], P('shard')
- query_bias_grad: float32 [768], P('shard')
- value_bias_grad: float32 [768], P('shard')
- out_weight_grad: float32 [768, 768], P('shard')
- out_bias_grad: float32 [768], P('shard')
- norm1_gain_grad: float32 [768], P('shard')
- norm1_bias_grad: float32 [768], P('shard')
- up_weight_grad: float32 [768, 3072], P('shard')
- up_bias_grad: float32 [3072], P('shard')
- down_weight_grad: float32 [3072, 768], P('shard')
- down_bias_grad: float32 [768], P('shard')
- norm2_gain_grad: float32 [768], P('shard')
- norm2_bias_grad: float32 [768], P('shard')
Inputs may be any that keep to these rules, and one draw needn't show every extreme that they name: `lengths`: the longest sequence has 1024 valid tokens and the shortest 256, in every draw. `clusters`: each sequence's ordering for each head names every position once.
All inputs are finite; a program needn't handle non-finite values.
Results may differ from a plain program's by a relative error of at most 0.018.
The roundings to bfloat16 on the way count: a program that leaves them out, or rounds other values in their place, can miss the bound.
Values may be sent and summed in bfloat16 or wider, within the bound.
A program may use at most 256 MiB of HBM per device.

v0:
```python
from functools import partial

import jax
import jax.numpy as jnp
from jax import lax
from jax.sharding import PartitionSpec as P

D = 768
H = 12
DH = 64
CLUSTER = 128
LEN = 1024
MICRO = 2


eps_norm = 1e-12


def inner_rows(left, right):
    return lax.dot_general(
        left, right, (((0,), (0,)), ((), ())), preferred_element_type=jnp.float32
    )


def times_transposed(left, right):
    return lax.dot_general(
        left, right, (((1,), (1,)), ((), ())), preferred_element_type=jnp.float32
    )


def norm_forward(source, gain, shift):
    centre = jnp.mean(source, axis=-1, keepdims=True)
    centred = source - centre
    variance = jnp.mean(centred * centred, axis=-1, keepdims=True)
    scale_inv = lax.rsqrt(variance + eps_norm)
    normed = centred * scale_inv
    return (normed * gain + shift, normed, scale_inv)


def norm_backward(upstream, normed, scale_inv, gain):
    scaled = upstream * gain
    mean_part = jnp.mean(scaled, axis=-1, keepdims=True)
    along_part = jnp.mean(scaled * normed, axis=-1, keepdims=True)
    back_rows = scale_inv * (scaled - mean_part - normed * along_part)
    return (back_rows, jnp.sum(upstream * normed, axis=0), jnp.sum(upstream, axis=0))


def order_table(order):
    positions = jnp.arange(LEN, dtype=jnp.int32)
    return (order[..., None] == positions).astype(jnp.bfloat16)


def to_blocks(source, table):
    seq_count = source.shape[0]
    shaped = source.reshape(seq_count, LEN, H, DH).transpose(0, 2, 1, 3)
    picked = jnp.einsum(
        "shtp,shpd->shtd", table, shaped, preferred_element_type=jnp.float32
    ).astype(jnp.bfloat16)
    return picked.reshape(seq_count, H, LEN // CLUSTER, CLUSTER, DH)


def from_blocks(blocks, table):
    seq_count = blocks.shape[0]
    head_rows = blocks.reshape(seq_count, H, LEN, DH)
    placed = jnp.einsum(
        "shtp,shtd->shpd", table, head_rows, preferred_element_type=jnp.float32
    ).astype(jnp.bfloat16)
    return placed.transpose(0, 2, 1, 3).reshape(seq_count * LEN, D)


def scores_of(query_c, key_c, key_bias):
    product = jnp.einsum("shcqd,shckd->shcqk", query_c, key_c, preferred_element_type=jnp.float32)
    return 0.125 * product + key_bias


def forward_micro(source, seq_lengths, valid, order, weights):
    (
        input_weight,
        query_bias,
        value_bias,
        out_weight,
        out_bias,
        norm1_gain,
        norm1_bias,
        up_weight,
        up_bias,
        down_weight,
        down_bias,
        norm2_gain,
        norm2_bias,
    ) = weights
    seq_count = source.shape[0]
    table = order_table(order)
    flat = source.reshape(seq_count * LEN, D)
    rounded = flat.astype(jnp.bfloat16)
    bias_all = jnp.concatenate([query_bias, jnp.zeros_like(query_bias), value_bias]).astype(
        jnp.float32
    )
    projected = (
        jnp.dot(rounded, input_weight, preferred_element_type=jnp.float32) + bias_all
    ).astype(jnp.bfloat16)
    query_c = to_blocks(projected[:, :D].reshape(seq_count, LEN, D), table)
    key_c = to_blocks(projected[:, D : 2 * D].reshape(seq_count, LEN, D), table)
    value_c = to_blocks(projected[:, 2 * D :].reshape(seq_count, LEN, D), table)
    key_valid = (order < seq_lengths[:, None, None]).astype(jnp.float32)
    key_bias = ((key_valid - 1.0) * 30000.0).reshape(seq_count, H, LEN // CLUSTER, 1, CLUSTER)
    scores = scores_of(query_c, key_c, key_bias)
    top_score = jnp.max(scores, axis=-1, keepdims=True)
    log_total = top_score + jnp.log(jnp.sum(jnp.exp(scores - top_score), axis=-1, keepdims=True))
    probs = jnp.exp(scores - log_total).astype(jnp.bfloat16)
    mixed = jnp.einsum(
        "shcqk,shckd->shcqd", probs, value_c, preferred_element_type=jnp.float32
    ).astype(jnp.bfloat16)
    attended = from_blocks(mixed, table)
    branch = jnp.dot(attended, out_weight, preferred_element_type=jnp.float32) + out_bias.astype(
        jnp.float32
    )
    first_out, normed_one, scale_one = norm_forward(
        flat + branch, norm1_gain.astype(jnp.float32), norm1_bias.astype(jnp.float32)
    )
    first_low = first_out.astype(jnp.bfloat16)
    pre_gelu = jnp.dot(first_low, up_weight, preferred_element_type=jnp.float32) + up_bias.astype(
        jnp.float32
    )
    activated = jax.nn.gelu(pre_gelu, approximate=False).astype(jnp.bfloat16)
    second_sum = (
        first_out
        + jnp.dot(activated, down_weight, preferred_element_type=jnp.float32)
        + down_bias.astype(jnp.float32)
    )
    second_out, normed_two, scale_two = norm_forward(
        second_sum, norm2_gain.astype(jnp.float32), norm2_bias.astype(jnp.float32)
    )
    result = (second_out * valid.reshape(seq_count * LEN, 1)).reshape(seq_count, LEN, D)
    saved = (
        rounded,
        query_c,
        key_c,
        value_c,
        key_bias,
        log_total,
        attended,
        normed_one,
        scale_one,
        first_low,
        pre_gelu,
        activated,
        normed_two,
        scale_two,
    )
    return (result, saved)


def backward_micro(upstream, valid, order, saved, weights):
    (
        input_weight,
        query_bias,
        value_bias,
        out_weight,
        out_bias,
        norm1_gain,
        norm1_bias,
        up_weight,
        up_bias,
        down_weight,
        down_bias,
        norm2_gain,
        norm2_bias,
    ) = weights
    (
        rounded,
        query_c,
        key_c,
        value_c,
        key_bias,
        log_total,
        attended,
        normed_one,
        scale_one,
        first_low,
        pre_gelu,
        activated,
        normed_two,
        scale_two,
    ) = saved
    seq_count = upstream.shape[0]
    table = order_table(order)
    back_out = upstream.reshape(seq_count * LEN, D) * valid.reshape(seq_count * LEN, 1)
    back_second, norm2_gain_grad, norm2_bias_grad = norm_backward(
        back_out, normed_two, scale_two, norm2_gain.astype(jnp.float32)
    )
    down_bias_grad = jnp.sum(back_second, axis=0)
    second_low = back_second.astype(jnp.bfloat16)
    down_weight_grad = inner_rows(activated, second_low)
    back_act = times_transposed(second_low, down_weight)
    gelu_value, gelu_pull = jax.vjp(partial(jax.nn.gelu, approximate=False), pre_gelu)
    back_pre = gelu_pull(back_act)[0]
    up_bias_grad = jnp.sum(back_pre, axis=0)
    pre_low = back_pre.astype(jnp.bfloat16)
    up_weight_grad = inner_rows(first_low, pre_low)
    back_first = times_transposed(pre_low, up_weight) + back_second
    back_sum, norm1_gain_grad, norm1_bias_grad = norm_backward(
        back_first, normed_one, scale_one, norm1_gain.astype(jnp.float32)
    )
    out_bias_grad = jnp.sum(back_sum, axis=0)
    sum_low = back_sum.astype(jnp.bfloat16)
    out_weight_grad = inner_rows(attended, sum_low)
    back_attended = times_transposed(sum_low, out_weight).astype(jnp.bfloat16)
    back_mixed = to_blocks(back_attended.reshape(seq_count, LEN, D), table)
    scores = scores_of(query_c, key_c, key_bias)
    probs = jnp.exp(scores - log_total)
    probs_low = probs.astype(jnp.bfloat16)
    back_probs = jnp.einsum(
        "shcqd,shckd->shcqk", back_mixed, value_c, preferred_element_type=jnp.float32
    )
    row_inner = jnp.sum(back_probs * probs, axis=-1, keepdims=True)
    back_scores = (0.125 * (probs * (back_probs - row_inner))).astype(jnp.bfloat16)
    back_query = jnp.einsum(
        "shcqk,shckd->shcqd", back_scores, key_c, preferred_element_type=jnp.float32
    )
    back_key = jnp.einsum(
        "shcqk,shcqd->shckd", back_scores, query_c, preferred_element_type=jnp.float32
    )
    back_value = jnp.einsum(
        "shcqk,shcqd->shckd", probs_low, back_mixed, preferred_element_type=jnp.float32
    )
    query_bias_grad = jnp.sum(back_query, axis=(0, 2, 3)).reshape(D)
    value_bias_grad = jnp.sum(back_value, axis=(0, 2, 3)).reshape(D)
    projected_low = jnp.concatenate(
        [
            from_blocks(back_query.astype(jnp.bfloat16), table),
            from_blocks(back_key.astype(jnp.bfloat16), table),
            from_blocks(back_value.astype(jnp.bfloat16), table),
        ],
        axis=1,
    )
    input_weight_grad = inner_rows(rounded, projected_low)
    back_input = back_sum + times_transposed(projected_low, input_weight)
    grads = (
        input_weight_grad,
        query_bias_grad,
        value_bias_grad,
        out_weight_grad,
        out_bias_grad,
        norm1_gain_grad,
        norm1_bias_grad,
        up_weight_grad,
        up_bias_grad,
        down_weight_grad,
        down_bias_grad,
        norm2_gain_grad,
        norm2_bias_grad,
    )
    return (back_input.reshape(seq_count, LEN, D), grads)


def local(
    hidden,
    lengths,
    clusters,
    input_weight,
    query_bias,
    value_bias,
    out_weight,
    out_bias,
    norm1_gain,
    norm1_bias,
    up_weight,
    up_bias,
    down_weight,
    down_bias,
    norm2_gain,
    norm2_bias,
    cotangent,
):
    positions = jnp.arange(LEN, dtype=jnp.int32)
    valid_all = (positions[None, :] < lengths[:, None]).astype(jnp.float32)
    per_micro = hidden.shape[0] // MICRO
    results = []
    back_inputs = []
    shares = None
    for micro_index in range(MICRO):
        row_begin = micro_index * per_micro
        row_end = row_begin + per_micro
        gathered = (
            lax.all_gather(input_weight, "shard", axis=0, tiled=True),
            lax.all_gather(query_bias, "shard", axis=0, tiled=True),
            lax.all_gather(value_bias, "shard", axis=0, tiled=True),
            lax.all_gather(out_weight, "shard", axis=0, tiled=True),
            lax.all_gather(out_bias, "shard", axis=0, tiled=True),
            lax.all_gather(norm1_gain, "shard", axis=0, tiled=True),
            lax.all_gather(norm1_bias, "shard", axis=0, tiled=True),
            lax.all_gather(up_weight, "shard", axis=0, tiled=True),
            lax.all_gather(up_bias, "shard", axis=0, tiled=True),
            lax.all_gather(down_weight, "shard", axis=0, tiled=True),
            lax.all_gather(down_bias, "shard", axis=0, tiled=True),
            lax.all_gather(norm2_gain, "shard", axis=0, tiled=True),
            lax.all_gather(norm2_bias, "shard", axis=0, tiled=True),
        )
        valid = valid_all[row_begin:row_end]
        order = clusters[row_begin:row_end]
        result, saved = forward_micro(
            hidden[row_begin:row_end], lengths[row_begin:row_end], valid, order, gathered
        )
        backward_weights = (
            lax.all_gather(input_weight, "shard", axis=0, tiled=True),
            lax.all_gather(query_bias, "shard", axis=0, tiled=True),
            lax.all_gather(value_bias, "shard", axis=0, tiled=True),
            lax.all_gather(out_weight, "shard", axis=0, tiled=True),
            lax.all_gather(out_bias, "shard", axis=0, tiled=True),
            lax.all_gather(norm1_gain, "shard", axis=0, tiled=True),
            lax.all_gather(norm1_bias, "shard", axis=0, tiled=True),
            lax.all_gather(up_weight, "shard", axis=0, tiled=True),
            lax.all_gather(up_bias, "shard", axis=0, tiled=True),
            lax.all_gather(down_weight, "shard", axis=0, tiled=True),
            lax.all_gather(down_bias, "shard", axis=0, tiled=True),
            lax.all_gather(norm2_gain, "shard", axis=0, tiled=True),
            lax.all_gather(norm2_bias, "shard", axis=0, tiled=True),
        )
        back_input, grads = backward_micro(
            cotangent[row_begin:row_end], valid, order, saved, backward_weights
        )
        owned = (
            lax.psum_scatter(
                grads[0].astype(jnp.bfloat16), "shard", scatter_dimension=0, tiled=True
            ).astype(jnp.float32),
            lax.psum_scatter(
                grads[1].astype(jnp.bfloat16), "shard", scatter_dimension=0, tiled=True
            ).astype(jnp.float32),
            lax.psum_scatter(
                grads[2].astype(jnp.bfloat16), "shard", scatter_dimension=0, tiled=True
            ).astype(jnp.float32),
            lax.psum_scatter(
                grads[3].astype(jnp.bfloat16), "shard", scatter_dimension=0, tiled=True
            ).astype(jnp.float32),
            lax.psum_scatter(
                grads[4].astype(jnp.bfloat16), "shard", scatter_dimension=0, tiled=True
            ).astype(jnp.float32),
            lax.psum_scatter(
                grads[5].astype(jnp.bfloat16), "shard", scatter_dimension=0, tiled=True
            ).astype(jnp.float32),
            lax.psum_scatter(
                grads[6].astype(jnp.bfloat16), "shard", scatter_dimension=0, tiled=True
            ).astype(jnp.float32),
            lax.psum_scatter(
                grads[7].astype(jnp.bfloat16), "shard", scatter_dimension=0, tiled=True
            ).astype(jnp.float32),
            lax.psum_scatter(
                grads[8].astype(jnp.bfloat16), "shard", scatter_dimension=0, tiled=True
            ).astype(jnp.float32),
            lax.psum_scatter(
                grads[9].astype(jnp.bfloat16), "shard", scatter_dimension=0, tiled=True
            ).astype(jnp.float32),
            lax.psum_scatter(
                grads[10].astype(jnp.bfloat16), "shard", scatter_dimension=0, tiled=True
            ).astype(jnp.float32),
            lax.psum_scatter(
                grads[11].astype(jnp.bfloat16), "shard", scatter_dimension=0, tiled=True
            ).astype(jnp.float32),
            lax.psum_scatter(
                grads[12].astype(jnp.bfloat16), "shard", scatter_dimension=0, tiled=True
            ).astype(jnp.float32),
        )
        shares = owned if shares is None else jax.tree.map(jnp.add, shares, owned)
        results.append(result)
        back_inputs.append(back_input)
    summed = lax.psum(
        (
            shares[0],
            shares[1],
            shares[2],
            shares[3],
            shares[4],
            shares[5],
            shares[6],
            shares[7],
            shares[8],
            shares[9],
            shares[10],
            shares[11],
            shares[12],
        ),
        "rep",
    )
    return (
        jnp.concatenate(results, axis=0),
        jnp.concatenate(back_inputs, axis=0),
        summed[0],
        summed[1],
        summed[2],
        summed[3],
        summed[4],
        summed[5],
        summed[6],
        summed[7],
        summed[8],
        summed[9],
        summed[10],
        summed[11],
        summed[12],
    )


def solution(mesh):
    return jax.shard_map(
        local,
        mesh=mesh,
        in_specs=(
            P(("rep", "shard"), None, None),
            P(("rep", "shard")),
            P(("rep", "shard"), None, None),
            P("shard", None),
            P("shard"),
            P("shard"),
            P("shard", None),
            P("shard"),
            P("shard"),
            P("shard"),
            P("shard", None),
            P("shard"),
            P("shard", None),
            P("shard"),
            P("shard"),
            P("shard"),
            P(("rep", "shard"), None, None),
        ),
        out_specs=(
            P(("rep", "shard"), None, None),
            P(("rep", "shard"), None, None),
            P("shard", None),
            P("shard"),
            P("shard"),
            P("shard", None),
            P("shard"),
            P("shard"),
            P("shard"),
            P("shard", None),
            P("shard"),
            P("shard", None),
            P("shard"),
            P("shard"),
            P("shard"),
        ),
        check_vma=False,
    )
```

profile of v0, /device:TPU:9, one launch (start us, length us, event | category | flops | bytes accessed | tf_op | source)
XLA Modules:
  0.0 1277.9 jit_solution(8378484310645078386)
XLA Ops:
  12.1 4.9 fusion.252
  17.1 3.8 copy.252
  24.6 28.2 %all-reduce.29 = (bf16[768]{0:T(1024)(128)(2,1)S(1)}, bf16[768]{0:T(1024)(128)(2,1)S(1)}, bf16[768]{0:T(1024)(128)(2,1)S(1)}, bf16[768]{0:T(1024)(128)(2,1)S(1)}...) all-reduce(bf16[768]{0:T(1024)(128)(2,1)S(1)} %dynamic-update-slice, ...), channel_id=1, replica_groups=mesh['rep'=4,'shard'=8] {'shard'}, use_global_device_ids=true, to_apply=%add.1 | all-reduce | flops 5376 | bytes 21504
  56.1 22.6 %all-gather = bf16[8,1,384]{2,1,0:T(2,128)(2,1)S(1)} all-gather(bf16[1,1,384]{2,1,0:T(2,128)(2,1)S(1)} %reshape.591), channel_id=1, replica_groups=mesh['rep'=4,'shard'=8] {'shard'}, dimensions={0}, use_global_device_ids=true | all-gather | bytes 6912 | tf_op jit(solution)/shard_map/all_gather | solution.py:294
  80.5 4.9 fusion.253
  85.4 4.1 copy.256
  91.8 7.0 add_convert_fusion.1
  103.6 12.1 fusion.178
  115.7 12.1 fusion.179
  127.9 4.0 fusion.48
  137.4 12.2 fusion.177
  153.0 11.0 fusion.97
  170.6 4.3 add_convert_fusion
  179.6 12.1 fusion.174
  191.8 12.1 fusion.175
  203.9 4.0 fusion.49
  213.5 12.2 fusion.173
  229.1 10.4 fusion.105
  245.9 7.7 fusion.237
  253.6 4.6 copy-done.10
  258.2 68.2 %multiply_convert_fusion.1 = (bf16[1024,3072]{1,0:T(8,128)(2,1)}, f32[1024,3072]{1,0:T(8,128)}, bf16[1024,3072]{1,0:T(8,128)(2,1)}, f32[1024,3072]{1,0:T(8,128)}, f32[1024,3072]{1,0:T(8,128)}) fusion(f32[3072]{0:T(1024)S(1)} %bitcast.383, f32[1024,3072]{1,0:T(8,128)S(1)} %fusion.237, bf16[768,3072]{1,0:T(8,128)(2,1)S(1)} %copy-done.19, ...), kind=kOutput, calls=%fused_computation.55 | convolution fusion | flops 5247074304 | bytes 69218304 | tf_op jit(solution)/shard_map/dot_general | solution.py:122
  326.6 11.0 fusion.263
  340.6 5.9 fusion.262
  351.6 3.8 fusion.246
  355.4 19.7 %fusion.265 = (bf16[3072]{0:T(1024)(128)(2,1)}, bf16[1024,3072]{1,0:T(8,128)(2,1)}) fusion(f32[1024,3072]{1,0:T(8,128)} %get-tuple-element.139, bf16[3072,768]{1,0:T(8,128)(2,1)} %all-gather.12.cloned.1.call-done, f32[1024,768]{0,1:T(8,128)} %get-tuple-element.131, f32[1024,3072]{1,0:T(8,128)} %get-tuple-element.188, f32[3072]{0:T(1024)S(1)} %bitcast.384), kind=kOutput, calls=%fused_computation.354 | convolution fusion | flops 4882953216 | bytes 39340032 | tf_op jit(solution)/shard_map/dot_general | solution.py:26
  375.2 12.7 multiply_reduce_fusion.5
  391.2 19.9 %fusion.264 = (bf16[3072]{0:T(1024)(128)(2,1)}, bf16[1024,3072]{1,0:T(8,128)(2,1)}) fusion(f32[1024,3072]{1,0:T(8,128)} %get-tuple-element.163, bf16[3072,768]{1,0:T(8,128)(2,1)} %all-gather.12.cloned.1.call-done, f32[1024,768]{0,1:T(8,128)} %get-tuple-element.133, f32[1024,3072]{1,0:T(8,128)} %copy-done.10, f32[3072]{0:T(1024)S(1)} %bitcast.385), kind=kOutput, calls=%fused_computation.353 | convolution fusion | flops 4882953216 | bytes 39340032 | tf_op jit(solution)/shard_map/dot_general | solution.py:26
  411.1 13.8 %fusion.248 = (bf16[768]{0:T(1024)(128)(2,1)}, f32[1024,768]{0,1:T(8,128)S(1)}, bf16[768]{0:T(1024)(128)(2,1)}, f32[1024]{0:T(1024)S(1)}, f32[1024]{0:T(1024)S(1...) fusion(f32[1024]{0:T(1024)S(1)} %broadcast_multiply_fusion.4, f32[1024,768]{0,1:T(8,128)} %copy-done.11, ...), kind=kOutput, calls=%fused_computation.339 | convolution fusion | flops 4845988864 | bytes 29924864 | tf_op jit(solution)/shard_map/dot_general | solution.py:26
  426.3 12.1 fusion.176
  438.5 3.8 fusion.140
  442.4 4.9 fusion.138
  449.7 13.1 %fusion.162 = bf16[12,8,8,8,128]{4,3,2,1,0:T(8,128)(2,1)} fusion(f32[12,8,128,128]{2,3,1,0:T(8,128)} %fusion.140, f32[12,8,128]{2,1,0:T(8,128)S(1)} %copy-done.49, f32[12,8,128]{2,1,0:T(8,128)S(1)} %copy-done.37, f32[12,8,128,128]{2,3,1,0:T(8,128)} %copy-done.1, bf16[12,8,8,8,128]{4,3,2,1,0:T(8,128)(2,1)} %copy-done.30), kind=kOutput, calls=%fused_computation.230 | convolution fusion | flops 219426944 | bytes 15826944 | tf_op jit(solution)/shard_map/shcqk,shcqd->shckd/dot_general | solution.py:221
  462.8 16.2 %convert_bitcast_fusion.2 = (bf16[12,8,8,8,128]{4,3,2,1,0:T(8,128)(2,1)}, bf16[12,64]{1,0:T(8,128)(2,1)S(1)}, bf16[12,64]{1,0:T(8,128)(2,1)S(1)}, bf16[12,8,8,8,128]{4,3,2,1,0:T(8,128)(2,1)}) fusion(f32[12,8,128,64]{2,3,1,0:T(8,128)} %fusion.138, f32[12,8,128,128]{2,3,1,0:T(8,128)} %fusion.140, f32[12,8,128]{2,1,0:T(8,128)S(1)} %copy-done.49, ...), kind=kOutput, calls=%fused_computation.224 | convolution fusion | flops 221784704 | bytes 20548608 | tf_op jit(solution)/shard_map/shcqk,shckd->shcqd/dot_general | solution.py:218
  486.9 11.2 fusion.100
  498.2 10.9 fusion.99
  509.2 10.2 fusion.101
  520.5 8.5 fusion.50
  529.0 5.8 copy.248
  538.5 12.3 fusion.172
  552.0 3.8 fusion.136
  555.8 13.5 %fusion.167 = bf16[12,8,8,8,128]{4,3,2,1,0:T(8,128)(2,1)} fusion(f32[12,8,128,128]{2,3,1,0:T(8,128)} %fusion.136, f32[12,8,128]{2,1,0:T(8,128)S(1)} %copy-done.47, f32[12,8,128]{2,1,0:T(8,128)S(1)} %copy-done.39, f32[12,8,128,128]{2,3,1,0:T(8,128)} %copy-done, bf16[12,8,8,8,128]{4,3,2,1,0:T(8,128)(2,1)} %copy-done.28), kind=kOutput, calls=%fused_computation.231 | convolution fusion | flops 219426944 | bytes 15826944 | tf_op jit(solution)/shard_map/shcqk,shcqd->shckd/dot_general | solution.py:221
  569.3 5.9 fusion.134
  575.2 16.5 %convert_bitcast_fusion = (bf16[12,8,8,8,128]{4,3,2,1,0:T(8,128)(2,1)}, bf16[12,64]{1,0:T(8,128)(2,1)S(1)}, bf16[12,64]{1,0:T(8,128)(2,1)S(1)}, bf16[12,8,8,8,128]{4,3,2,1,0:T(8,128)(2,1)}) fusion(f32[12,8,128,64]{2,3,1,0:T(8,128)} %fusion.134, f32[12,8,128,128]{2,3,1,0:T(8,128)} %fusion.136, f32[12,8,128]{2,1,0:T(8,128)S(1)} %copy-done.47, ...), kind=kOutput, calls=%fused_computation.222 | convolution fusion | flops 221784704 | bytes 20548608 | tf_op jit(solution)/shard_map/shcqk,shckd->shcqd/dot_general | solution.py:218
  591.7 10.6 fusion.108
  602.3 10.2 fusion.107
  612.5 10.2 fusion.109
  623.9 8.7 fusion.51
  632.6 5.8 copy.250
  638.4 9.7 convolution_convert_fusion.1
  648.2 9.7 convolution_convert_fusion
  658.6 9.8 convolution_convert_fusion.3
  668.5 10.1 convolution_convert_fusion.2
  680.9 7.4 add_bitcast_fusion.1
  688.3 3.8 add_bitcast_fusion
  695.5 6.6 copy.232
  702.3 27.4 %all-reduce.28 = (bf16[768]{0:T(1024)(128)(2,1)S(1)}, bf16[768]{0:T(1024)(128)(2,1)S(1)}, bf16[768]{0:T(1024)(128)(2,1)S(1)}, bf16[768]{0:T(1024)(128)(2,1)S(1)}...) all-reduce(bf16[768]{0:T(1024)(128)(2,1)S(1)} %dynamic-update-slice, ...), channel_id=1, replica_groups=mesh['rep'=4,'shard'=8] {'shard'}, use_global_device_ids=true, to_apply=%add.7 | all-reduce | flops 19200 | bytes 76800
  732.8 53.1 %reduce-scatter.27.cloned.1.call-done = bf16[96,2304]{1,0:T(8,128)(2,1)} async-done(((bf16[768,2304]{1,0:T(8,128)(2,1)}), bf16[96,2304]{1,0:T(8,128)(2,1)}) %reduce-scatter.27.cloned.1.call-update) | async-done | bytes 442384
  788.3 96.2 %reduce-scatter.21.cloned.1.call-done = bf16[384,768]{1,0:T(8,128)(2,1)} async-done(((bf16[3072,768]{1,0:T(8,128)(2,1)}), bf16[384,768]{1,0:T(8,128)(2,1)}) %reduce-scatter.21.cloned.1.call-update) | async-done | bytes 589840 | tf_op jit(solution)/shard_map/reduce_scatter | solution.py:351
  884.5 98.5 %reduce-scatter.23.cloned.1.call-done = bf16[384,768]{1,0:T(8,128)(2,1)} async-done(((bf16[3072,768]{1,0:T(8,128)(2,1)}), bf16[384,768]{1,0:T(8,128)(2,1)}) %reduce-scatter.23.cloned.1.call-update) | async-done | bytes 589840 | tf_op jit(solution)/shard_map/reduce_scatter | solution.py:351
  985.5 96.4 %reduce-scatter.17.cloned.1.call-done = bf16[96,3072]{1,0:T(8,128)(2,1)} async-done(((bf16[768,3072]{1,0:T(8,128)(2,1)}), bf16[96,3072]{1,0:T(8,128)(2,1)}) %reduce-scatter.17.cloned.1.call-update) | async-done | bytes 589840 | tf_op jit(solution)/shard_map/reduce_scatter | solution.py:345
  1081.9 98.7 %reduce-scatter.19.cloned.1.call-done = bf16[96,3072]{1,0:T(8,128)(2,1)} async-done(((bf16[768,3072]{1,0:T(8,128)(2,1)}), bf16[96,3072]{1,0:T(8,128)(2,1)}) %reduce-scatter.19.cloned.1.call-update) | async-done | bytes 589840 | tf_op jit(solution)/shard_map/reduce_scatter | solution.py:345
  1189.7 7.0 copy.231
  1197.3 6.5 all-reduce.26
  1203.8 60.7 %all-reduce.32.cloned.1.call-done = (f32[96,2304]{0,1:T(8,128)}, f32[96,768]{1,0:T(8,128)}, f32[96,3072]{1,0:T(8,128)}, f32[384,768]{1,0:T(8,128)}) async-done(((f32[96,2304]{0,1:T(8,128)}, f32[96,768]{1,0:T(8,128)}, f32[96,3072]{1,0:T(8,128)}, f32[384,768]{1,0:T(8,128)}), (f32[96,2304]{0,1:T(8,128)}, f32[96,768]{1,0:T(8,128)}, f32[96,3072]{1,0:T(8,128)}, ...) | async-done | bytes 3538960 | tf_op jit(solution)/shard_map/psum | solution.py:367
  (422 shorter events, 114.0 us)
Async XLA Ops:
  7.2 84.7 %all-gather.6.cloned.1.call-start = ((), (), s32[]{:S(2)}) async-start(), calls=%async_computation.8 | async-start | bytes 3981312 | tf_op jit(solution)/shard_map/all_gather | solution.py:286
  7.9 156.1 %all-gather.8.cloned.1.call-start = ((), (), s32[]{:S(2)}) async-start(), calls=%async_computation.9 | async-start | bytes 1327104 | tf_op jit(solution)/shard_map/all_gather | solution.py:289
  8.7 237.2 %all-gather.10.cloned.1.call-start = ((), (), s32[]{:S(2)}) async-start(), calls=%async_computation.10 | async-start | bytes 5308416 | tf_op jit(solution)/shard_map/all_gather | solution.py:293
  9.4 317.1 %all-gather.12.cloned.1.call-start = ((), (), s32[]{:S(2)}) async-start(), calls=%async_computation.11 | async-start | bytes 5308416 | tf_op jit(solution)/shard_map/all_gather | solution.py:295
  10.0 719.7 %reduce-scatter.13.cloned.1.call-start = ((), (), s32[]{:S(2)}) async-start(), calls=%async_computation.12 | async-start | bytes 1327104 | tf_op jit(solution)/shard_map/reduce_scatter | solution.py:333
  21.0 132.0 %copy-start.66 = (s32[1,12,1024]{2,1,0:T(8,128)}, s32[1,12,1024]{2,1,0:T(8,128)S(1)}, u32[]{:S(2)}) copy-start(s32[1,12,1024]{2,1,0:T(8,128)S(1)} %copy.393) | copy-start | bytes 147460
  21.7 128.0 %copy-start.36 = (f32[12,8,128]{2,1,0:T(8,128)}, f32[12,8,128]{2,1,0:T(8,128)S(1)}, u32[]{:S(2)}) copy-start(f32[12,8,128]{2,1,0:T(8,128)S(1)} %slice.72) | copy-start | bytes 147460
  52.9 192.9 %copy-start.42 = (f32[768]{0:T(1024)}, f32[768]{0:T(1024)S(1)}, u32[]{:S(2)}) copy-start(f32[768]{0:T(1024)S(1)} %convert_element_type.417) | copy-start | bytes 9220
  52.9 192.9 %copy-start.52 = (f32[768]{0:T(1024)}, f32[768]{0:T(1024)S(1)}, u32[]{:S(2)}) copy-start(f32[768]{0:T(1024)S(1)} %convert_element_type.418) | copy-start | bytes 9220
  55.3 173.7 %copy-start.68 = (s32[1,12,1024]{2,1,0:T(8,128)}, s32[1,12,1024]{2,1,0:T(8,128)S(1)}, u32[]{:S(2)}) copy-start(s32[1,12,1024]{2,1,0:T(8,128)S(1)} %copy.392) | copy-start | bytes 147460
  56.1 169.6 %copy-start.38 = (f32[12,8,128]{2,1,0:T(8,128)}, f32[12,8,128]{2,1,0:T(8,128)S(1)}, u32[]{:S(2)}) copy-start(f32[12,8,128]{2,1,0:T(8,128)S(1)} %slice.73) | copy-start | bytes 147460
  103.6 12.2 copy-start.32
  115.7 12.2 copy-start.29
  134.7 15.0 %copy-start.48 = (f32[12,8,128]{2,1,0:T(8,128)}, f32[12,8,128]{2,1,0:T(8,128)S(1)}, u32[]{:S(2)}) copy-start(f32[12,8,128]{2,1,0:T(8,128)S(1)} %log_add_fusion.1) | copy-start | bytes 147460
  134.7 15.0 %slice-start.2 = ((s8[6291456]{0:T(1024)(128)(4,1)}), s8[2097152]{0:T(1024)(128)(4,1)S(1)}, s32[]{:S(2)}) async-start(s8[6291456]{0:T(1024)(128)(4,1)} %bitcast.347), calls=%async_computation.23 | async-start | bytes 4194304
  137.4 12.3 slice-start.3
  167.6 74.0 %copy-start.74 = (f32[1024]{0:T(1024)}, f32[1024]{0:T(1024)S(1)}, u32[]{:S(2)}) copy-start(f32[1024]{0:T(1024)S(1)} %broadcast_multiply_fusion.11) | copy-start | bytes 12292
  170.6 71.0 %copy-start.77 = (f32[1024]{0:T(1024)}, f32[1024]{0:T(1024)S(1)}, u32[]{:S(2)}) copy-start(f32[1024]{0:T(1024)S(1)} %add_rsqrt_fusion.3) | copy-start | bytes 12292
  179.6 12.1 copy-start.34
  191.7 12.2 copy-start.27
  210.7 15.0 %copy-start.46 = (f32[12,8,128]{2,1,0:T(8,128)}, f32[12,8,128]{2,1,0:T(8,128)S(1)}, u32[]{:S(2)}) copy-start(f32[12,8,128]{2,1,0:T(8,128)S(1)} %log_add_fusion) | copy-start | bytes 147460
  210.7 15.0 %slice-start = ((s8[6291456]{0:T(1024)(128)(4,1)}), s8[2097152]{0:T(1024)(128)(4,1)S(1)}, s32[]{:S(2)}) async-start(s8[6291456]{0:T(1024)(128)(4,1)} %bitcast.345), calls=%async_computation.21 | async-start | bytes 4194304
  213.5 12.3 slice-start.1
  245.9 12.3 copy-start.19
  245.9 12.3 copy-start.35
  258.2 68.3 %copy-start.43 = (f32[768]{0:T(1024)S(1)}, f32[768]{0:T(1024)}, u32[]{:S(2)}) copy-start(f32[768]{0:T(1024)} %copy-done.42) | copy-start | bytes 9220
  258.2 68.3 %copy-start.45 = (f32[1024]{0:T(1024)S(1)}, f32[1024]{0:T(1024)}, u32[]{:S(2)}) copy-start(f32[1024]{0:T(1024)} %copy-done.44) | copy-start | bytes 12292
  258.2 68.3 %copy-start.51 = (f32[1024]{0:T(1024)S(1)}, f32[1024]{0:T(1024)}, u32[]{:S(2)}) copy-start(f32[1024]{0:T(1024)} %copy-done.50) | copy-start | bytes 12292
  258.2 68.3 %copy-start.53 = (f32[768]{0:T(1024)S(1)}, f32[768]{0:T(1024)}, u32[]{:S(2)}) copy-start(f32[768]{0:T(1024)} %copy-done.52) | copy-start | bytes 9220
  258.2 68.3 %copy-start.89 = (f32[768]{0:T(1024)S(1)}, f32[768]{0:T(1024)}, u32[]{:S(2)}) copy-start(f32[768]{0:T(1024)} %convert_element_type.422) | copy-start | bytes 9220
  326.5 11.5 slice-start.6
  326.5 11.5 slice-start.8
  326.6 11.5 slice-start.7
  326.6 11.5 slice-start.9
  337.6 50.3 %copy-start.2 = (f32[1024,768]{0,1:T(8,128)}, f32[1024,768]{0,1:T(8,128)S(1)}, u32[]{:S(2)}) copy-start(f32[1024,768]{0,1:T(8,128)S(1)} %get-tuple-element.192) | copy-start | bytes 9437188
  337.6 50.2 %copy-start.55 = (f32[1024]{0:T(1024)}, f32[1024]{0:T(1024)S(1)}, u32[]{:S(2)}) copy-start(f32[1024]{0:T(1024)S(1)} %broadcast_multiply_fusion.8) | copy-start | bytes 12292
  338.1 49.8 %copy-start.62 = (f32[1024]{0:T(1024)}, f32[1024]{0:T(1024)S(1)}, u32[]{:S(2)}) copy-start(f32[1024]{0:T(1024)S(1)} %add_rsqrt_fusion) | copy-start | bytes 12292
  375.2 12.7 copy-start.8
  391.2 19.9 %copy-start.6 = (f32[1024,768]{0,1:T(8,128)S(1)}, f32[1024,768]{0,1:T(8,128)}, u32[]{:S(2)}) copy-start(f32[1024,768]{0,1:T(8,128)} %copy-done.5) | copy-start | bytes 9437188
  411.1 13.8 %copy-start.100 = (bf16[768,768]{1,0:T(8,128)(2,1)S(1)}, bf16[768,768]{1,0:T(8,128)(2,1)}, u32[]{:S(2)}) copy-start(bf16[768,768]{1,0:T(8,128)(2,1)} %all-gather.8.cloned.1.call-done) | copy-start | bytes 3538948
  424.9 22.3 %copy-start.123 = (f32[1024,768]{0,1:T(8,128)}, f32[1024,768]{0,1:T(8,128)S(1)}, u32[]{:S(2)}) copy-start(f32[1024,768]{0,1:T(8,128)S(1)} %get-tuple-element.135) | copy-start | bytes 9437188
  424.9 17.4 %slice-start.4 = ((s8[6291456]{0:T(1024)(128)(4,1)}), s8[4194304]{0:T(1024)(128)(4,1)S(1)}, s32[]{:S(2)}) async-start(s8[6291456]{0:T(1024)(128)(4,1)} %bitcast.349), calls=%async_computation.25 | async-start | bytes 8388608
  426.3 12.2 copy-start.17
  426.3 16.0 %slice-start.5 = ((s8[6291456]{0:T(1024)(128)(4,1)}), s8[2097152]{0:T(1024)(128)(4,1)S(1)}, s32[]{:S(2)}) async-start(s8[6291456]{0:T(1024)(128)(4,1)} %bitcast.349), calls=%async_computation.26 | async-start | bytes 4194304
  479.1 250.6 %reduce-scatter.15.cloned.1.call-start = ((), (), s32[]{:S(2)}) async-start(), calls=%async_computation.13 | async-start | bytes 1327104 | tf_op jit(solution)/shard_map/reduce_scatter | solution.py:333
  498.1 233.3 %reduce-scatter.25.cloned.1.call-start = ((), (), s32[]{:S(2)}) async-start(), calls=%async_computation.18 | async-start | bytes 3981312
  509.2 11.4 copy-start.21
  509.2 11.4 copy-start.112
  534.8 251.0 %reduce-scatter.27.cloned.1.call-start = ((), (), s32[]{:S(2)}) async-start(), calls=%async_computation.19 | async-start | bytes 3981312
  538.5 13.5 %copy-start.15 = (bf16[12,8,8,8,128]{4,3,2,1,0:T(8,128)(2,1)S(1)}, bf16[12,8,8,8,128]{4,3,2,1,0:T(8,128)(2,1)}, u32[]{:S(2)}) copy-start(bf16[12,8,8,8,128]{4,3,2,1,0:T(8,128)(2,1)} %copy-done.14) | copy-start | bytes 4718596
  602.3 20.5 %copy-start.117 = (bf16[12,1024,64]{1,2,0:T(8,128)(2,1)}, bf16[12,1024,64]{1,2,0:T(8,128)(2,1)S(1)}, u32[]{:S(2)}) copy-start(bf16[12,1024,64]{1,2,0:T(8,128)(2,1)S(1)} %fusion.108) | copy-start | bytes 4718596
  638.4 246.2 %reduce-scatter.21.cloned.1.call-start = ((), (), s32[]{:S(2)}) async-start(), calls=%async_computation.16 | async-start | bytes 5308416 | tf_op jit(solution)/shard_map/reduce_scatter | solution.py:351
  648.1 334.9 %reduce-scatter.23.cloned.1.call-start = ((), (), s32[]{:S(2)}) async-start(), calls=%async_computation.17 | async-start | bytes 5308416 | tf_op jit(solution)/shard_map/reduce_scatter | solution.py:351
  657.9 424.0 %reduce-scatter.17.cloned.1.call-start = ((), (), s32[]{:S(2)}) async-start(), calls=%async_computation.14 | async-start | bytes 5308416 | tf_op jit(solution)/shard_map/reduce_scatter | solution.py:345
  668.5 512.1 %reduce-scatter.19.cloned.1.call-start = ((), (), s32[]{:S(2)}) async-start(), calls=%async_computation.15 | async-start | bytes 5308416 | tf_op jit(solution)/shard_map/reduce_scatter | solution.py:345
  678.7 585.8 %all-reduce.32.cloned.1.call-start = ((), (), s32[]{:S(2)}) async-start(), calls=%async_computation.20 | async-start | bytes 7667712 | tf_op jit(solution)/shard_map/psum | solution.py:367
  985.4 197.6 %copy-start.3 = (f32[1024,768]{0,1:T(8,128)S(1)}, f32[1024,768]{0,1:T(8,128)}, u32[]{:S(2)}) copy-start(f32[1024,768]{0,1:T(8,128)} %copy-done.2) | copy-start | bytes 9437188
  985.4 197.6 %copy-start.56 = (f32[1024]{0:T(1024)S(1)}, f32[1024]{0:T(1024)}, u32[]{:S(2)}) copy-start(f32[1024]{0:T(1024)} %copy-done.55) | copy-start | bytes 12292
  985.4 197.6 %copy-start.58 = (f32[768]{0:T(1024)S(1)}, f32[768]{0:T(1024)}, u32[]{:S(2)}) copy-start(f32[768]{0:T(1024)} %convert_element_type.423) | copy-start | bytes 9220
  985.4 197.6 %copy-start.60 = (f32[1024]{0:T(1024)S(1)}, f32[1024]{0:T(1024)}, u32[]{:S(2)}) copy-start(f32[1024]{0:T(1024)} %copy-done.59) | copy-start | bytes 12292
  985.5 197.6 %copy-start.63 = (f32[1024]{0:T(1024)S(1)}, f32[1024]{0:T(1024)}, u32[]{:S(2)}) copy-start(f32[1024]{0:T(1024)} %copy-done.62) | copy-start | bytes 12292
  985.5 197.6 %copy-start.65 = (f32[1,1024]{1,0:T(1,128)S(1)}, f32[1,1024]{1,0:T(1,128)}, u32[]{:S(2)}) copy-start(f32[1,1024]{1,0:T(1,128)} %get-tuple-element.167) | copy-start | bytes 12292
  985.5 197.6 %copy-start.71 = (f32[1024]{0:T(1024)S(1)}, f32[1024]{0:T(1024)}, u32[]{:S(2)}) copy-start(f32[1024]{0:T(1024)} %copy-done.70) | copy-start | bytes 12292
  985.5 197.6 %copy-start.73 = (f32[1,1024]{1,0:T(1,128)S(1)}, f32[1,1024]{1,0:T(1,128)}, u32[]{:S(2)}) copy-start(f32[1,1024]{1,0:T(1,128)} %get-tuple-element.166) | copy-start | bytes 12292
  (86 other events, 437.2 us)
Sparse Core Ops, SparseCore 0:
  10.2 65.9 all-gather.5
  78.4 39.8 all-gather.7
  120.5 77.7 all-gather.9
  200.4 78.3 all-gather.11
  479.2 72.7 reduce-scatter.12
  555.8 63.0 reduce-scatter.14
  622.5 80.1 reduce-scatter.24
  706.3 79.4 reduce-scatter.26
  789.5 94.9 reduce-scatter.20
  888.0 94.9 reduce-scatter.22
  986.7 95.1 reduce-scatter.16
  1085.4 95.1 reduce-scatter.18
  1184.3 80.1 all-reduce.31
where the time goes:
time: 1280 us
  matrix products  527 us (41%)
  waiting for transfers between devices  506 us (40%)
  local copies, waits for them, and re-layouts  98.6 us (8%)
  blocking collectives  84.7 us (7%)
  other arithmetic  41.9 us (3%)
  between operations  18.6 us (1%)
    reduce_scatter x2, waiting for transfers between devices, local(): lax.psum_scatter(grads[7].astype(jnp.bfloat16), 'shard', scatter_dimensio...  195 us
    reduce_scatter x2, waiting for transfers between devices, local(): lax.psum_scatter(grads[9].astype(jnp.bfloat16), 'shard', scatter_dimensio...  195 us
    dot_general x8, matrix products, to_blocks(): jnp.einsum('shtp,shpd->shtd', table, shaped, preferred_element_type=jnp.f...  97.5 us
    dot_general x8, matrix products, from_blocks(): jnp.einsum('shtp,shtd->shpd', table, head_rows, preferred_element_type=jn...  84.6 us
    dot_general x8, matrix products, times_transposed(): lax.dot_general(left, right, (((1,), (1,)), ((), ())), preferred_element_...  82.3 us
    dot_general x2, matrix products, forward_micro(): jnp.dot(first_low, up_weight, preferred_element_type=jnp.float32)  76 us
    unnamed x311, local copies, waits for them, and re-layouts  71.5 us
    dot_general x8, matrix products, inner_rows(): lax.dot_general(left, right, (((0,), (0,)), ((), ())), preferred_element_...  61.4 us
  transfers between devices with their start and end apart: 13, of which 6 were waited for; matrix products, arithmetic and copies ran while one was open for 38% of the time, Pallas kernels for 0%

commit v1 on v0

v1 whole, which is shorter than its diff:
```python
from functools import partial

import jax
import jax.numpy as jnp
from jax import lax
from jax.experimental import pallas as pl
from jax.experimental.pallas import tpu as pltpu
from jax.sharding import PartitionSpec as P

D = 768
H = 12
DH = 64
FF = 3072
CLUSTER = 128
LEN = 1024
PAIRS = H // 2
SLICES = [slice(c * CLUSTER, (c + 1) * CLUSTER) for c in range(LEN // CLUSTER)]
bf = jnp.bfloat16
f32 = jnp.float32
eps_norm = 1e-12


def dot_nn(left, right):
    return lax.dot_general(left, right, (((1,), (0,)), ((), ())), preferred_element_type=f32)


def dot_nt(left, right):
    return lax.dot_general(left, right, (((1,), (1,)), ((), ())), preferred_element_type=f32)


def dot_tn(left, right):
    return lax.dot_general(left, right, (((0,), (0,)), ((), ())), preferred_element_type=f32)


def low_lanes():
    return lax.broadcasted_iota(jnp.int32, (LEN, CLUSTER), 1) < DH


def table_of(order_row):
    positions = lax.broadcasted_iota(jnp.int32, (LEN, LEN), 0)
    return jnp.where(jnp.broadcast_to(order_row, (LEN, LEN)) == positions, 1.0, 0.0).astype(bf)


def half_roll(source):
    return pltpu.roll(source.astype(f32), DH, 1).astype(bf)


def softmax_rows(scores):
    top = jnp.max(scores, axis=-1, keepdims=True)
    grown = jnp.exp(scores - top)
    return grown * (1.0 / jnp.sum(grown, axis=-1, keepdims=True))


def attention_forward_body(
    len_ref, x_ref, w_ref, b_ref, row_ref, att_ref, proj_ref, t0, t1, s0, s1, m0, m1
):
    count = len_ref[pl.program_id(0)]
    proj = (dot_nn(x_ref[...], w_ref[...]) + b_ref[0]).astype(bf)
    proj_ref[...] = proj
    low = low_lanes()
    tables, scores, mixed = (t0, t1), (s0, s1), (m0, m1)
    rows = [row_ref[0, 0, e : e + 1, :] for e in range(2)]
    for e in range(2):
        tables[e][...] = table_of(rows[e])
    picked = [
        dot_tn(tables[e][...], proj[:, 128 * e : 128 * e + 256]).astype(bf) for e in range(2)
    ]
    for e in range(2):
        qk = picked[e][:, 128 * e : 128 * e + 128]
        key_low = jnp.where(low, half_roll(qk), jnp.zeros((), bf))
        bias = jnp.where(rows[e] < count, 0.0, -30000.0)
        for sl in SLICES:
            scores[e][sl, :] = 0.125 * dot_nt(qk[sl], key_low[sl]) + bias[:, sl]
    for e in range(2):
        values = picked[e][:, 128 - 128 * e : 256 - 128 * e]
        for sl in SLICES:
            probs = softmax_rows(scores[e][sl, :]).astype(bf)
            mixed[e][sl, :] = dot_nn(probs, values[sl]).astype(bf)
    placed = [dot_nn(tables[e][...], mixed[e][...]) for e in range(2)]
    att_ref[...] = jnp.where(low, placed[0], placed[1]).astype(bf)


def attention_forward(lengths, rounded, weight, bias, rows):
    seqs = rows.shape[0]
    tokens = seqs * LEN
    return pl.pallas_call(
        attention_forward_body,
        grid_spec=pltpu.PrefetchScalarGridSpec(
            num_scalar_prefetch=1,
            grid=(seqs, PAIRS),
            in_specs=[
                pl.BlockSpec((LEN, D), lambda s, h, n: (s, 0)),
                pl.BlockSpec((D, 384), lambda s, h, n: (0, h)),
                pl.BlockSpec((1, 1, 384), lambda s, h, n: (h, 0, 0)),
                pl.BlockSpec((1, 1, 2, LEN), lambda s, h, n: (s, h, 0, 0)),
            ],
            out_specs=[
                pl.BlockSpec((LEN, 128), lambda s, h, n: (s, h)),
                pl.BlockSpec((LEN, 384), lambda s, h, n: (s, h)),
            ],
            scratch_shapes=[pltpu.VMEM((LEN, LEN), bf)] * 2
            + [pltpu.VMEM((LEN, 128), f32)] * 2
            + [pltpu.VMEM((LEN, 128), bf)] * 2,
        ),
        out_shape=[
            jax.ShapeDtypeStruct((tokens, D), bf),
            jax.ShapeDtypeStruct((tokens, 3 * D), bf),
        ],
        compiler_params=pltpu.CompilerParams(vmem_limit_bytes=50 << 20),
        cost_estimate=pl.CostEstimate(
            flops=44_000_000_000, bytes_accessed=24_000_000, transcendentals=0
        ),
        name="attention_forward",
    )(lengths, rounded, weight, bias, rows)


def attention_backward_body(
    len_ref,
    x_ref,
    proj_ref,
    datt_ref,
    row_ref,
    dproj_ref,
    dw_ref,
    db_ref,
    t0,
    t1,
    s0,
    s1,
    d0,
    d1,
    p0,
    p1,
    e0,
    e1,
    total,
):
    seq = pl.program_id(1)
    count = len_ref[seq]
    low = low_lanes()
    zero = jnp.zeros((), bf)
    tables, scores, back_probs, probs_low, backs = (t0, t1), (s0, s1), (d0, d1), (p0, p1), (e0, e1)
    rows = [row_ref[0, 0, e : e + 1, :] for e in range(2)]
    for e in range(2):
        tables[e][...] = table_of(rows[e])
    datt = datt_ref[...]
    swapped = half_roll(proj_ref[:, 128:256])
    middle = [jnp.where(low, datt, swapped), jnp.where(low, swapped, datt)]
    sources = [
        jnp.concatenate([proj_ref[:, 256 * e : 256 * e + 128], middle[e]], axis=1)
        for e in range(2)
    ]
    picked = [dot_tn(tables[e][...], sources[e]).astype(bf) for e in range(2)]
    for e in range(2):
        qk, dv = picked[e][:, 0:128], picked[e][:, 128:256]
        key_low = jnp.where(low, half_roll(qk), zero)
        turned = half_roll(dv)
        value_only = jnp.where(low, turned, zero) if e == 0 else jnp.where(low, zero, turned)
        bias = jnp.where(rows[e] < count, 0.0, -30000.0)
        for sl in SLICES:
            scores[e][sl, :] = 0.125 * dot_nt(qk[sl], key_low[sl]) + bias[:, sl]
            back_probs[e][sl, :] = dot_nt(dv[sl], value_only[sl])
    for e in range(2):
        for sl in SLICES:
            probs = softmax_rows(scores[e][sl, :])
            back = back_probs[e][sl, :]
            probs_low[e][sl, :] = probs.astype(bf)
            inner = jnp.sum(back * probs, axis=-1, keepdims=True)
            backs[e][sl, :] = (0.125 * (probs * (back - inner))).astype(bf)
    placed = []
    for e in range(2):
        qk, dv = picked[e][:, 0:128], picked[e][:, 128:256]
        queries, keys, values = [], [], []
        for sl in SLICES:
            back = backs[e][sl, :]
            queries.append(dot_nn(back, qk[sl]))
            keys.append(dot_tn(back, qk[sl]))
            values.append(dot_tn(probs_low[e][sl, :], dv[sl]))
        key_query = jnp.where(low, jnp.concatenate(keys, 0), jnp.concatenate(queries, 0))
        value = jnp.concatenate(values, 0)
        db_ref[0, 0, e : e + 1, :] = jnp.sum(key_query, axis=0, keepdims=True)
        db_ref[0, 0, 2 + e : 3 + e, :] = jnp.sum(value, axis=0, keepdims=True)
        parts = [half_roll(key_query), value.astype(bf)]
        placed.append(
            dot_nn(tables[e][...], jnp.concatenate(parts if e == 0 else parts[::-1], axis=1))
        )
    out = jnp.concatenate(
        [
            placed[0][:, 0:128],
            jnp.where(low, placed[0][:, 128:256], placed[1][:, 0:128]),
            placed[1][:, 128:256],
        ],
        axis=1,
    ).astype(bf)
    dproj_ref[...] = out
    part = dot_tn(x_ref[...], out)

    @pl.when(seq == 0)
    def _():
        total[...] = part

    @pl.when(seq != 0)
    def _():
        total[...] += part

    dw_ref[...] = total[...].astype(bf)


def attention_backward(lengths, rounded, proj, datt, rows):
    seqs = rows.shape[0]
    tokens = seqs * LEN
    return pl.pallas_call(
        attention_backward_body,
        grid_spec=pltpu.PrefetchScalarGridSpec(
            num_scalar_prefetch=1,
            grid=(PAIRS, seqs),
            in_specs=[
                pl.BlockSpec((LEN, D), lambda h, s, n: (s, 0)),
                pl.BlockSpec((LEN, 384), lambda h, s, n: (s, h)),
                pl.BlockSpec((LEN, 128), lambda h, s, n: (s, h)),
                pl.BlockSpec((1, 1, 2, LEN), lambda h, s, n: (s, h, 0, 0)),
            ],
            out_specs=[
                pl.BlockSpec((LEN, 384), lambda h, s, n: (s, h)),
                pl.BlockSpec((D, 384), lambda h, s, n: (0, h)),
                pl.BlockSpec((1, 1, 4, 128), lambda h, s, n: (s, h, 0, 0)),
            ],
            scratch_shapes=[pltpu.VMEM((LEN, LEN), bf)] * 2
            + [pltpu.VMEM((LEN, 128), f32)] * 4
            + [pltpu.VMEM((LEN, 128), bf)] * 4
            + [pltpu.VMEM((D, 384), f32)],
        ),
        out_shape=[
            jax.ShapeDtypeStruct((tokens, 3 * D), bf),
            jax.ShapeDtypeStruct((D, 3 * D), bf),
            jax.ShapeDtypeStruct((seqs, PAIRS, 4, 128), f32),
        ],
        compiler_params=pltpu.CompilerParams(vmem_limit_bytes=50 << 20),
        cost_estimate=pl.CostEstimate(
            flops=70_000_000_000, bytes_accessed=30_000_000, transcendentals=0
        ),
        name="attention_backward",
    )(lengths, rounded, proj, datt, rows)


def to_pairs(weight):
    parts = weight.reshape(weight.shape[:-1] + (3, PAIRS, 2, DH))
    query, key, value = parts[..., 0, :, :, :], parts[..., 1, :, :, :], parts[..., 2, :, :, :]
    a, b = 0, 1
    joined = jnp.concatenate(
        [
            query[..., a, :],
            key[..., a, :],
            value[..., a, :],
            value[..., b, :],
            query[..., b, :],
            key[..., b, :],
        ],
        axis=-1,
    )
    return joined.reshape(weight.shape)


def from_pairs(weight):
    parts = weight.reshape(weight.shape[:-1] + (PAIRS, 6, DH))
    query = jnp.stack([parts[..., 0, :], parts[..., 4, :]], axis=-2)
    key = jnp.stack([parts[..., 1, :], parts[..., 5, :]], axis=-2)
    value = jnp.stack([parts[..., 2, :], parts[..., 3, :]], axis=-2)
    lead = weight.shape[:-1]
    return jnp.concatenate([t.reshape(lead + (D,)) for t in (query, key, value)], axis=-1)


def norm_forward(source, gain, shift):
    centre = jnp.mean(source, axis=-1, keepdims=True)
    centred = source - centre
    variance = jnp.mean(centred * centred, axis=-1, keepdims=True)
    scale_inv = lax.rsqrt(variance + eps_norm)
    normed = centred * scale_inv
    return (normed * gain + shift, normed, scale_inv)


def norm_backward(upstream, normed, scale_inv, gain):
    scaled = upstream * gain
    mean_part = jnp.mean(scaled, axis=-1, keepdims=True)
    along_part = jnp.mean(scaled * normed, axis=-1, keepdims=True)
    back_rows = scale_inv * (scaled - mean_part - normed * along_part)
    return (back_rows, jnp.sum(upstream * normed, axis=0), jnp.sum(upstream, axis=0))


def local(
    hidden,
    lengths,
    clusters,
    input_weight,
    query_bias,
    value_bias,
    out_weight,
    out_bias,
    norm1_gain,
    norm1_bias,
    up_weight,
    up_bias,
    down_weight,
    down_bias,
    norm2_gain,
    norm2_bias,
    cotangent,
):
    seqs = hidden.shape[0]
    tokens = seqs * LEN
    gather = partial(lax.all_gather, axis_name="shard", axis=0, tiled=True)
    vectors = (
        query_bias,
        value_bias,
        out_bias,
        norm1_gain,
        norm1_bias,
        down_bias,
        norm2_gain,
        norm2_bias,
        up_bias,
    )
    widths = [v.shape[0] for v in vectors]
    marks = [sum(widths[:i]) for i in range(len(widths) + 1)]
    packed = lax.all_gather(jnp.concatenate(vectors)[None], "shard", axis=0, tiled=True)
    query_b, value_b, out_b, gain1, shift1, down_b, gain2, shift2, up_b = [
        packed[:, marks[i] : marks[i + 1]].reshape(-1).astype(f32) for i in range(len(widths))
    ]
    in_w = gather(to_pairs(input_weight))
    out_w = gather(out_weight)
    up_w = gather(up_weight)
    down_w = gather(down_weight)

    flat = hidden.reshape(tokens, D)
    rounded = flat.astype(bf)
    rows = clusters.reshape(seqs, PAIRS, 2, LEN)
    bias_pairs = to_pairs(jnp.concatenate([query_b, jnp.zeros_like(query_b), value_b]))
    attended, proj = attention_forward(
        lengths, rounded, in_w, bias_pairs.reshape(PAIRS, 1, 384), rows
    )
    positions = jnp.arange(LEN, dtype=jnp.int32)
    valid = (positions[None, :] < lengths[:, None]).astype(f32).reshape(tokens, 1)
    first_out, normed_one, scale_one = norm_forward(
        flat + dot_nn(attended, out_w) + out_b, gain1, shift1
    )
    first_low = first_out.astype(bf)
    pre_gelu = dot_nn(first_low, up_w) + up_b
    activated = jax.nn.gelu(pre_gelu, approximate=False).astype(bf)
    second_sum = first_out + dot_nn(activated, down_w) + down_b
    second_out, normed_two, scale_two = norm_forward(second_sum, gain2, shift2)
    result = (second_out * valid).reshape(seqs, LEN, D)

    back_out = cotangent.reshape(tokens, D) * valid
    back_second, gain2_grad, shift2_grad = norm_backward(back_out, normed_two, scale_two, gain2)
    down_b_grad = jnp.sum(back_second, axis=0)
    second_low = back_second.astype(bf)
    down_w_grad = dot_tn(activated, second_low).astype(bf)
    back_act = dot_nt(second_low, down_w)
    back_pre = jax.vjp(partial(jax.nn.gelu, approximate=False), pre_gelu)[1](back_act)[0]
    up_b_grad = jnp.sum(back_pre, axis=0)
    pre_low = back_pre.astype(bf)
    up_w_grad = dot_tn(first_low, pre_low).astype(bf)
    back_first = dot_nt(pre_low, up_w) + back_second
    back_sum, gain1_grad, shift1_grad = norm_backward(back_first, normed_one, scale_one, gain1)
    out_b_grad = jnp.sum(back_sum, axis=0)
    sum_low = back_sum.astype(bf)
    out_w_grad = dot_tn(attended, sum_low).astype(bf)
    back_attended = dot_nt(sum_low, out_w).astype(bf)
    dproj, in_w_grad, db = attention_backward(lengths, rounded, proj, back_attended, rows)
    db = jnp.sum(db, axis=0)
    query_b_grad = db[:, 0:2, DH:].reshape(D)
    value_b_grad = jnp.concatenate([db[:, 2, :DH], db[:, 3, DH:]], axis=1).reshape(D)
    back_input = (back_sum + dot_nt(dproj, in_w)).reshape(seqs, LEN, D)

    def scatter(grad):
        part = lax.psum_scatter(grad, "shard", scatter_dimension=0, tiled=True)
        return lax.psum(part.astype(f32), "rep")

    shards = packed.shape[0]
    small = jnp.concatenate(
        [
            g.reshape(shards, -1)
            for g in (
                query_b_grad,
                value_b_grad,
                out_b_grad,
                gain1_grad,
                shift1_grad,
                down_b_grad,
                gain2_grad,
                shift2_grad,
                up_b_grad,
            )
        ],
        axis=1,
    )
    small = lax.psum(small, ("rep", "shard"))
    mine = lax.dynamic_index_in_dim(small, lax.axis_index("shard"), 0, keepdims=False)
    small = [mine[marks[i] : marks[i + 1]] for i in range(len(widths))]
    return (
        result,
        back_input,
        from_pairs(scatter(in_w_grad)),
        small[0],
        small[1],
        scatter(out_w_grad),
        small[2],
        small[3],
        small[4],
        scatter(up_w_grad),
        small[8],
        scatter(down_w_grad),
        small[5],
        small[6],
        small[7],
    )


def solution(mesh):
    tokens = P(("rep", "shard"), None, None)
    matrix, vector = P("shard", None), P("shard")
    params = (
        matrix,
        vector,
        vector,
        matrix,
        vector,
        vector,
        vector,
        matrix,
        vector,
        matrix,
        vector,
        vector,
        vector,
    )
    return jax.shard_map(
        local,
        mesh=mesh,
        in_specs=(tokens, P(("rep", "shard")), tokens) + params + (tokens,),
        out_specs=(tokens, tokens) + params,
        check_vma=False,
    )
```

time: 1280 us -> 915 us (0.71)
  matrix products: 527 us -> 205 us
  Pallas kernels: 0 us -> 154 us
  waiting for transfers between devices: 506 us -> 376 us
  local copies, waits for them, and re-layouts: 98.6 us -> 16 us
  blocking collectives: 84.7 us -> 114 us
  other arithmetic: 41.9 us -> 27.1 us
    dot_general x52 -> x10, matrix products: 527 us -> 205 us  [the longest x3 93.1 us: dot_nn(): lax.dot_general(left, right, (((1,), (0,)), ((), ())), preferred_element_...]
    pallas_call x0 -> x2, Pallas kernels: none -> 154 us  [the longest x1 94.4 us: attention_backward(): pl.pallas_call(attention_backward_body, grid_spec=pltpu.PrefetchScalarGri...]
    reduce_scatter x6 -> x4, waiting for transfers between devices: 390 us -> 267 us  [scatter(): part = lax.psum_scatter(grad, 'shard', scatter_dimension=0, tiled=True)]
    all_gather x4, waiting for transfers between devices: 0.06 us -> 92.2 us  [the longest x1 52.9 us: local(): up_w = gather(up_weight)]
    psum x1 -> x2, blocking collectives: 6.51 us -> 91.2 us  [the longest x1 52.3 us: scatter(): return lax.psum(part.astype(f32), 'rep')]
    unnamed x311 -> x77, local copies, waits for them, and re-layouts: 71.5 us -> 5.61 us
    unnamed x2 -> x0, blocking collectives: 55.6 us -> none
    unnamed x15 -> x9, waiting for transfers between devices: 55.8 us -> 2 us
  transfers between devices with their start and end apart: 13 -> 9, of which waited for: 6 -> 7; matrix products, arithmetic and copies ran while one was open for 38% -> 17% of each run, Pallas kernels for 0% -> 7%
where the time goes in v1:
time: 915 us; the launch traced here: 907 us
  waiting for transfers between devices  376 us (41%)
  matrix products  205 us (22%)
  Pallas kernels  154 us (17%)
  blocking collectives  114 us (12%)
  other arithmetic  27.1 us (3%)
  local copies, waits for them, and re-layouts  16 us (2%)
  between operations  14.7 us (2%)
    reduce_scatter x4, waiting for transfers between devices, scatter(): part = lax.psum_scatter(grad, 'shard', scatter_dimension=0, tiled=True)  267 us
    pallas_call x1, Pallas kernels, attention_backward(): pl.pallas_call(attention_backward_body, grid_spec=pltpu.PrefetchScalarGri...  94.4 us
    dot_general x3, matrix products, dot_nn(): lax.dot_general(left, right, (((1,), (0,)), ((), ())), preferred_element_...  93.1 us
    dot_general x4, matrix products, dot_nt(): lax.dot_general(left, right, (((1,), (1,)), ((), ())), preferred_element_...  70.8 us
    pallas_call x1, Pallas kernels, attention_forward(): pl.pallas_call(attention_forward_body, grid_spec=pltpu.PrefetchScalarGrid...  59.2 us
    all_gather x1, waiting for transfers between devices, local(): up_w = gather(up_weight)  52.9 us
    psum x1, blocking collectives, scatter(): return lax.psum(part.astype(f32), 'rep')  52.3 us
    dot_general x3, matrix products, dot_tn(): lax.dot_general(left, right, (((0,), (0,)), ((), ())), preferred_element_...  41.3 us
  transfers between devices with their start and end apart: 9, of which 7 were waited for; matrix products, arithmetic and copies ran while one was open for 17% of the time, Pallas kernels for 7%

profile of v1, /device:TPU:9, one launch (start us, length us, event | category | flops | bytes accessed | tf_op | source)
XLA Modules:
  0.0 906.5 jit_solution(1256733016815241294)
XLA Ops:
  7.3 1.3 copy.51
  8.9 1.0 copy.65
  10.0 0.7 all-gather.9.cloned.1.call-update
  10.7 0.7 all-gather.11.cloned.1.call-update
  11.5 0.5 all-gather.13.cloned.1.call-update
  12.1 0.1 concatenate.20
  12.2 22.6 %all-gather.1 = bf16[8,1,1152]{2,1,0:T(2,128)(2,1)S(1)} all-gather(bf16[1,1,1152]{2,1,0:T(2,128)(2,1)S(1)} %reshape.273), channel_id=2, replica_groups=mesh['rep'=4,'shard'=8] {'shard'}, dimensions={0}, use_global_device_ids=true | all-gather | bytes 20736 | tf_op jit(solution)/shard_map/all_gather | solution.py:325
  34.8 0.1 slice_convert_fusion.2
  34.9 0.1 reshape.262
  35.0 0.1 reshape.263
  35.1 0.1 concatenate.21
  35.2 4.7 bitcast_convert_fusion.x_ref
  40.0 0.1 reshape.264
  40.1 0.1 reshape.265
  40.1 0.1 reshape.266
  40.2 0.7 reshape.268
  40.9 0.1 reshape.269
  41.0 0.1 compare_convert_fusion
  41.0 4.1 multiply_reduce_fusion.7
  45.1 0.7 reshape.270
  45.8 0.6 copy_bitcast_fusion.3
  46.4 29.5 %all-gather.7.cloned.1.call-done.w_ref = bf16[768,2304]{1,0:T(8,128)(2,1)} async-done(((bf16[96,2304]{1,0:T(8,128)(2,1)}), bf16[768,2304]{1,0:T(8,128)(2,1)}) %all-gather.7.cloned.1.call-update) | async-done | bytes 3538960 | tf_op jit(solution)/shard_map/all_gather | solution.py:329
  75.9 59.2 %attention_forward.1 = (bf16[2048,768]{1,0:T(8,128)(2,1)S(1)}, bf16[2048,2304]{1,0:T(8,128)(2,1)}) custom-call(s32[2]{0:T(128)S(1)} %copy-done.1, bf16[2048,768]{1,0:T(8,128)(2,1)} %bitcast_convert_fusion.x_ref, bf16[768,2304]{1,0:T(8,128)(2,1)} %all-gather.7.cloned.1.call-done.w_ref, f32[6,1,384]{2,1,0:T(1,128)S(1)} %reshape_reshape.9.b_ref, ...), custom_call_target="tpu_custom_call" | custom-call | flops 44000002048 | bytes 24000000 | tf_op jit(solution)/shard_map/attention_forward/pallas_call | solution.py:86
  135.1 6.5 fusion.44
  141.7 2.7 copy-done.5
  144.4 0.8 multiply_reduce_fusion.6
  145.2 52.9 %all-gather.11.cloned.1.call-done = bf16[768,3072]{1,0:T(8,128)(2,1)} async-done(((bf16[96,3072]{1,0:T(8,128)(2,1)}), bf16[768,3072]{1,0:T(8,128)(2,1)}) %all-gather.11.cloned.1.call-update) | async-done | bytes 4718608 | tf_op jit(solution)/shard_map/all_gather | solution.py:331
  198.1 70.4 %multiply_convert_fusion = (bf16[2048,3072]{1,0:T(8,128)(2,1)}, f32[2048,3072]{1,0:T(8,128)}, f32[2048,3072]{1,0:T(8,128)}) fusion(f32[3072]{0:T(1024)S(1)} %reshape.267, bf16[768,3072]{1,0:T(8,128)(2,1)} %all-gather.11.cloned.1.call-done, f32[2048,768]{1,0:T(8,128)} %copy-done.5, f32[768]{0:T(1024)S(1)} %reshape.266, f32[768]{0:T(1024)S(1)} %reshape.265, ...), kind=kOutput, calls=%fused_computation.3 | convolution fusion | flops 10086776832 | bytes 73959424 | tf_op jit(solution)/shard_map/dot_general | solution.py:24
  268.5 9.7 %all-gather.13.cloned.1.call-done = bf16[3072,768]{1,0:T(8,128)(2,1)} async-done(((bf16[384,768]{1,0:T(8,128)(2,1)}), bf16[3072,768]{1,0:T(8,128)(2,1)}) %all-gather.13.cloned.1.call-update) | async-done | bytes 4718608 | tf_op jit(solution)/shard_map/all_gather | solution.py:332
  278.2 16.2 %fusion.45 = (f32[2048]{0:T(1024)S(1)}, f32[2048,768]{1,0:T(8,128)S(1)}) fusion(f32[768]{0:T(1024)S(1)} %copy-done.20, bf16[2048,3072]{1,0:T(8,128)(2,1)} %get-tuple-element.70, bf16[3072,768]{1,0:T(8,128)(2,1)} %all-gather.13.cloned.1.call-done, f32[768]{0:T(1024)S(1)} %reshape.266, f32[768]{0:T(1024)S(1)} %reshape.265, f32[2048]{0:T(1024)S(1)} %add_rsqrt_fusion.1, ...), kind=kOutput, calls=%fused_computation.118 | convolution fusion | flops 9674684416 | bytes 29918208 | tf_op jit(solution)/shard_map/dot_general | solution.py:24
  294.4 0.8 multiply_reduce_fusion.5
  295.4 3.4 multiply_reduce_fusion
  298.8 6.7 fusion.37
  305.5 32.3 %fusion.46 = (f32[3072]{0:T(1024)}, bf16[2048,3072]{1,0:T(8,128)(2,1)}) fusion(f32[2048,3072]{1,0:T(8,128)} %get-tuple-element.71, bf16[3072,768]{1,0:T(8,128)(2,1)} %all-gather.13.cloned.1.call-done, f32[2048,768]{1,0:T(8,128)} %get-tuple-element.67, f32[2048,3072]{1,0:T(8,128)} %get-tuple-element.106, f32[3072]{0:T(1024)S(1)} %reshape.267), kind=kOutput, calls=%fused_computation.119 | convolution fusion | flops 9765909504 | bytes 73949184 | tf_op jit(solution)/shard_map/dot_general | solution.py:28
  337.8 20.5 %multiply_reduce_fusion.1 = (f32[768]{0:T(1024)S(1)}, f32[2048]{0:T(1024)S(1)}, f32[2048]{0:T(1024)S(1)}, f32[768]{0:T(1024)S(1)}, f32[2048,768]{1,0:T(8,128)}) fusion(f32[2048,768]{1,0:T(8,128)} %copy-done.5, f32[2048]{0:T(1024)S(1)} %add_rsqrt_fusion.1, f32[2048]{0:T(1024)S(1)} %broadcast_multiply_fusion.4, f32[768]{0:T(1024)S(1)} %reshape.265, ...), kind=kOutput, calls=%fused_computation.22 | convolution fusion | flops 9679398912 | bytes 36217856 | tf_op jit(solution)/shard_map/dot_general | solution.py:28
  358.3 6.1 fusion.38
  364.4 4.1 convolution_convert_fusion.1.datt_ref
  368.6 0.1 copy-done.6
  368.7 94.4 %attention_backward.1 = (bf16[2048,2304]{1,0:T(8,128)(2,1)}, bf16[768,2304]{1,0:T(8,128)(2,1)}, f32[2,6,4,128]{3,2,1,0:T(4,128)S(1)}) custom-call(s32[2]{0:T(128)S(1)} %copy-done.2, bf16[2048,768]{1,0:T(8,128)(2,1)S(1)} %copy-done, bf16[2048,2304]{1,0:T(8,128)(2,1)} %get-tuple-element.21.proj_ref, bf16[2048,768]{1,0:T(8,128)(2,1)} %convolution_convert_fusion.1.datt_ref, ...), custom_call_target="tpu_custom_call" | custom-call | flops 70000001024 | bytes 30000000 | tf_op jit(solution)/shard_map/attention_backward/pallas_call | solution.py:212
  463.1 6.6 fusion.24
  469.8 72.7 %reduce-scatter.5.cloned.1.call-done = bf16[96,2304]{1,0:T(8,128)(2,1)} async-done(((bf16[768,2304]{1,0:T(8,128)(2,1)}), bf16[96,2304]{1,0:T(8,128)(2,1)}) %reduce-scatter.5.cloned.1.call-update) | async-done | bytes 442384 | tf_op jit(solution)/shard_map/reduce_scatter | solution.py:376
  542.4 2.3 copy.62
  544.8 16.7 %convolution_convert_fusion = bf16[3072,768]{1,0:T(8,128)(2,1)} fusion(bf16[2048,3072]{1,0:T(8,128)(2,1)} %get-tuple-element.70, f32[2048,768]{1,0:T(8,128)} %get-tuple-element.67), kind=kOutput, calls=%fused_computation.43 | convolution fusion | flops 9667608576 | bytes 23592960 | tf_op jit(solution)/shard_map/dot_general | solution.py:32
  561.6 18.1 %fusion.13 = bf16[768,3072]{1,0:T(8,128)(2,1)} fusion(bf16[2048,3072]{1,0:T(8,128)(2,1)} %get-tuple-element.111, f32[2048,768]{1,0:T(8,128)} %copy-done.5, f32[768]{0:T(1024)S(1)} %copy-done.19, f32[768]{0:T(1024)S(1)} %reshape.265, f32[2048]{0:T(1024)S(1)} %add_rsqrt_fusion.1, f32[2048]{0:T(1024)S(1)} %broadcast_multiply_fusion.4), kind=kOutput, calls=%fused_computation.44 | convolution fusion | flops 9673900032 | bytes 23615488 | tf_op jit(solution)/shard_map/dot_general | solution.py:32
  579.7 0.1 reshape.260
  579.8 0.1 slice.225
  579.9 0.1 fusion.41
  579.9 0.1 pad_maximum_fusion.3
  580.0 0.1 reshape_reshape.11
  580.1 0.1 reshape_reshape.10
  580.4 0.1 reshape.258
  580.6 0.1 concatenate.24
  580.6 39.0 %psum.36 = f32[8,1152]{1,0:T(8,128)S(1)} all-reduce(f32[8,1152]{1,0:T(8,128)S(1)} %concatenate.24), channel_id=1, replica_groups=mesh['rep'=4,'shard'=8] {'rep','shard'}, use_global_device_ids=true, to_apply=%region_18.19 | all-reduce | flops 9216 | bytes 73728 | tf_op jit(solution)/shard_map/psum | solution.py:397
  619.6 0.7 dynamic-slice_reduce_fusion
  620.3 0.6 dynamic-slice_bitcast_fusion
  620.9 13.8 %convolution_add_fusion = f32[2048,768]{1,0:T(8,128)} fusion(f32[2048,768]{1,0:T(8,128)} %copy-done.6, bf16[2048,2304]{1,0:T(8,128)(2,1)} %get-tuple-element.22, bf16[768,2304]{1,0:T(8,128)(2,1)} %all-gather.7.cloned.1.call-done.w_ref), kind=kOutput, calls=%fused_computation.47 | convolution fusion | flops 7249330176 | bytes 25559040 | tf_op jit(solution)/shard_map/dot_general | solution.py:28
  634.7 14.9 %all-reduce.4.cloned.1.call-done = f32[96,6,6,64]{0,3,2,1:T(8,128)} async-done(((f32[96,6,6,64]{0,3,2,1:T(8,128)}), f32[96,6,6,64]{0,3,2,1:T(8,128)}) %all-reduce.4.cloned.1.call-update) | async-done | bytes 884752 | tf_op jit(solution)/shard_map/psum | solution.py:377
  649.6 1.0 stack.12
  650.6 1.3 fusion.40
  652.0 0.1 pad_maximum_fusion
  652.1 1.3 copy.64
  653.4 95.5 %reduce-scatter.11.cloned.1.call-done = bf16[384,768]{1,0:T(8,128)(2,1)} async-done(((bf16[3072,768]{1,0:T(8,128)(2,1)}), bf16[384,768]{1,0:T(8,128)(2,1)}) %reduce-scatter.11.cloned.1.call-update) | async-done | bytes 589840 | tf_op jit(solution)/shard_map/reduce_scatter | solution.py:376
  748.8 98.7 %reduce-scatter.9.cloned.1.call-done = bf16[96,3072]{1,0:T(8,128)(2,1)} async-done(((bf16[768,3072]{1,0:T(8,128)(2,1)}), bf16[96,3072]{1,0:T(8,128)(2,1)}) %reduce-scatter.9.cloned.1.call-update) | async-done | bytes 589840 | tf_op jit(solution)/shard_map/reduce_scatter | solution.py:376
  847.5 52.3 %all-reduce.5 = (f32[96,768]{1,0:T(8,128)}, f32[96,3072]{1,0:T(8,128)}, f32[384,768]{1,0:T(8,128)}) all-reduce(bf16[96,768]{1,0:T(8,128)(2,1)S(1)} %copy-done.7, bf16[96,3072]{1,0:T(8,128)(2,1)} %reduce-scatter.9.cloned.1.call-done, bf16[384,768]{1,0:T(8,128)(2,1)} %reduce-scatter.11.cloned.1.call-done), channel_id=1, replica_groups=mesh['rep'=4,'shard'=8] {'rep'}, use_global_device_ids=true, to_apply=%region_20.21 | all-reduce | flops 663552 | bytes 3981312 | tf_op jit(solution)/shard_map/psum | solution.py:377
  (119 shorter events, 1.3 us)
Async XLA Ops:
  7.2 4.9 copy-start.22
  7.2 4.9 copy-start.23
  7.2 4.9 copy-start.24
  7.2 4.9 copy-start.25
  7.2 4.9 copy-start.26
  7.2 4.9 copy-start.21
  7.2 4.9 copy-start.27
  7.3 4.9 copy-start.28
  7.3 4.9 copy-start.29
  7.3 68.6 %all-gather.7.cloned.1.call-start = ((), (), s32[]{:S(2)}) async-start(), calls=%async_computation.4 | async-start | bytes 3981312 | tf_op jit(solution)/shard_map/all_gather | solution.py:329
  8.9 31.1 %copy-start.8 = (s32[2,12,1024]{2,0,1:T(2,128)S(1)}, s32[2,12,1024]{2,0,1:T(2,128)}, u32[]{:S(2)}) copy-start(s32[2,12,1024]{2,0,1:T(2,128)} %param.19) | copy-start | bytes 294916
  8.9 32.1 %copy-start.1 = (s32[2]{0:T(128)S(1)}, s32[2]{0:T(128)}, u32[]{:S(2)}) copy-start(s32[2]{0:T(128)} %len_ref.3) | copy-start | bytes 28
  9.9 125.2 %all-gather.9.cloned.1.call-start = ((), (), s32[]{:S(2)}) async-start(), calls=%async_computation.5 | async-start | bytes 1327104 | tf_op jit(solution)/shard_map/all_gather | solution.py:330
  10.7 187.4 %all-gather.11.cloned.1.call-start = ((), (), s32[]{:S(2)}) async-start(), calls=%async_computation.6 | async-start | bytes 5308416 | tf_op jit(solution)/shard_map/all_gather | solution.py:331
  11.4 266.8 %all-gather.13.cloned.1.call-start = ((), (), s32[]{:S(2)}) async-start(), calls=%async_computation.7 | async-start | bytes 5308416 | tf_op jit(solution)/shard_map/all_gather | solution.py:332
  12.0 530.4 %reduce-scatter.5.cloned.1.call-start = ((), (), s32[]{:S(2)}) async-start(), calls=%async_computation.8 | async-start | bytes 3981312 | tf_op jit(solution)/shard_map/reduce_scatter | solution.py:376
  40.2 238.0 %copy-start.18 = (f32[768]{0:T(1024)}, f32[768]{0:T(1024)S(1)}, u32[]{:S(2)}) copy-start(f32[768]{0:T(1024)S(1)} %reshape.266) | copy-start | bytes 9220
  41.0 94.1 %copy-start.10 = (f32[768]{0:T(1024)}, f32[768]{0:T(1024)S(1)}, u32[]{:S(2)}) copy-start(f32[768]{0:T(1024)S(1)} %reshape.269) | copy-start | bytes 9220
  135.1 6.6 copy-start.3
  141.7 2.7 copy-start.5
  198.1 80.1 %copy-start.20 = (f32[768]{0:T(1024)S(1)}, f32[768]{0:T(1024)}, u32[]{:S(2)}) copy-start(f32[768]{0:T(1024)} %reshape.268) | copy-start | bytes 9220
  278.2 17.1 %slice-start = ((s8[6291456]{0:T(1024)(128)(4,1)}), s8[4194304]{0:T(1024)(128)(4,1)S(1)}, s32[]{:S(2)}) async-start(s8[6291456]{0:T(1024)(128)(4,1)} %bitcast.113), calls=%async_computation.13 | async-start | bytes 8388608
  278.2 17.1 %slice-start.1 = ((s8[6291456]{0:T(1024)(128)(4,1)}), s8[2097152]{0:T(1024)(128)(4,1)S(1)}, s32[]{:S(2)}) async-start(s8[6291456]{0:T(1024)(128)(4,1)} %bitcast.113), calls=%async_computation.14 | async-start | bytes 4194304
  294.4 0.9 copy-start.9
  294.4 0.9 copy-start.11
  295.4 3.5 copy-start.12
  295.4 3.4 copy-start.16
  358.3 6.1 copy-start.30
  364.4 4.3 copy-start.6
  364.4 4.2 copy-start
  364.4 4.2 copy-start.2
  368.7 94.5 %copy-start.4 = (bf16[2048,768]{1,0:T(8,128)(2,1)S(1)}, bf16[2048,768]{1,0:T(8,128)(2,1)}, u32[]{:S(2)}) copy-start(bf16[2048,768]{1,0:T(8,128)(2,1)} %copy-done.3) | copy-start | bytes 9437188
  463.1 171.7 %reduce-scatter.7.cloned.1.call-start = ((), (), s32[]{:S(2)}) async-start(), calls=%async_computation.10 | async-start | bytes 1327104 | tf_op jit(solution)/shard_map/reduce_scatter | solution.py:376
  469.7 179.9 %all-reduce.4.cloned.1.call-start = ((), (), s32[]{:S(2)}) async-start(), calls=%async_computation.9 | async-start | bytes 2359296 | tf_op jit(solution)/shard_map/psum | solution.py:377
  544.7 16.9 %copy-start.19 = (f32[768]{0:T(1024)S(1)}, f32[768]{0:T(1024)}, u32[]{:S(2)}) copy-start(f32[768]{0:T(1024)} %copy-done.18) | copy-start | bytes 9220
  544.7 204.1 %reduce-scatter.11.cloned.1.call-start = ((), (), s32[]{:S(2)}) async-start(), calls=%async_computation.12 | async-start | bytes 5308416 | tf_op jit(solution)/shard_map/reduce_scatter | solution.py:376
  561.5 18.2 %copy-start.15 = (f32[768]{0:T(1024)S(1)}, f32[768]{0:T(1024)}, u32[]{:S(2)}) copy-start(f32[768]{0:T(1024)} %get-tuple-element.59) | copy-start | bytes 9220
  561.5 18.9 %copy-start.17 = (f32[3072]{0:T(1024)S(1)}, f32[3072]{0:T(1024)}, u32[]{:S(2)}) copy-start(f32[3072]{0:T(1024)} %get-tuple-element.110) | copy-start | bytes 36868
  561.5 18.9 %copy-start.14 = (f32[768]{0:T(1024)S(1)}, f32[768]{0:T(1024)}, u32[]{:S(2)}) copy-start(f32[768]{0:T(1024)} %get-tuple-element.66) | copy-start | bytes 9220
  561.5 19.0 %copy-start.13 = (f32[768]{0:T(1024)S(1)}, f32[768]{0:T(1024)}, u32[]{:S(2)}) copy-start(f32[768]{0:T(1024)} %get-tuple-element.55) | copy-start | bytes 9220
  561.5 286.0 %reduce-scatter.9.cloned.1.call-start = ((), (), s32[]{:S(2)}) async-start(), calls=%async_computation.11 | async-start | bytes 5308416 | tf_op jit(solution)/shard_map/reduce_scatter | solution.py:376
  634.7 212.8 %copy-start.7 = (bf16[96,768]{1,0:T(8,128)(2,1)S(1)}, bf16[96,768]{1,0:T(8,128)(2,1)}, u32[]{:S(2)}) copy-start(bf16[96,768]{1,0:T(8,128)(2,1)} %reduce-scatter.7.cloned.1.call-done) | copy-start | bytes 442372
Sparse Core Ops, SparseCore 0:
  10.9 65.0 all-gather.6
  78.1 39.6 all-gather.8
  120.0 78.0 all-gather.10
  200.1 78.0 all-gather.12
  463.2 79.2 reduce-scatter.4
  546.3 61.7 reduce-scatter.6
  611.0 38.5 all-reduce.3
  653.2 95.5 reduce-scatter.10
  752.5 94.9 reduce-scatter.8

commit v2 on v1

--- a/solution.py
+++ b/solution.py
@@ -270,21 +270,373 @@
     return jnp.concatenate([t.reshape(lead + (D,)) for t in (query, key, value)], axis=-1)
 
 
-def norm_forward(source, gain, shift):
-    centre = jnp.mean(source, axis=-1, keepdims=True)
-    centred = source - centre
-    variance = jnp.mean(centred * centred, axis=-1, keepdims=True)
-    scale_inv = lax.rsqrt(variance + eps_norm)
-    normed = centred * scale_inv
-    return (normed * gain + shift, normed, scale_inv)
-
-
-def norm_backward(upstream, normed, scale_inv, gain):
-    scaled = upstream * gain
-    mean_part = jnp.mean(scaled, axis=-1, keepdims=True)
-    along_part = jnp.mean(scaled * normed, axis=-1, keepdims=True)
-    back_rows = scale_inv * (scaled - mean_part - normed * along_part)
-    return (back_rows, jnp.sum(upstream * normed, axis=0), jnp.sum(upstream, axis=0))
+ROWS = 4
+MESH=pl.DeviceIdType.MESH
+
+def when(cond,do):
+    if cond is None: do()
+    else: pl.when(cond)(do)
+
+class Place:
+    def __init__(self,shards,reps):
+        self.Y=shards//ROWS; self.S=shards; self.X=reps//2
+        self.s=lax.axis_index("shard"); self.r=lax.axis_index("rep")
+        self.z=self.s//self.Y; self.y=lax.rem(self.s,self.Y)
+        self.core=lax.rem(self.r,2); self.x=self.r//2
+    def near_z(self,step): return {"shard":self.s+step*self.Y}
+    def other_y(self,k): return {"shard":self.z*self.Y+lax.rem(self.y+k,self.Y)}
+    def other_core(self): return {"rep":self.r+1-2*self.core}
+    def other_x(self,k): return {"rep":2*lax.rem(self.x+k,self.X)+self.core}
+
+def meet(place,with_x):
+    sem=pltpu.get_barrier_semaphore()
+    def tell(dev): pl.semaphore_signal(sem,inc=1,device_id=dev,device_id_type=MESH)
+    pl.when(place.z>0)(lambda: tell(place.near_z(-1)))
+    pl.when(place.z<ROWS-1)(lambda: tell(place.near_z(1)))
+    for k in range(1,place.Y): tell(place.other_y(k))
+    tell(place.other_core())
+    if with_x:
+        for k in range(1,place.X): tell(place.other_x(k))
+    others=place.Y+(place.X-1 if with_x else 0)
+    inner=jnp.logical_and(place.z>0,place.z<ROWS-1)
+    pl.when(inner)(lambda: pl.semaphore_wait(sem,others+2))
+    pl.when(jnp.logical_not(inner))(lambda: pl.semaphore_wait(sem,others+1))
+
+def gather_semaphores(count,shards):
+    Y=shards//ROWS
+    return [pltpu.SemaphoreType.DMA((count,2,ROWS)),pltpu.SemaphoreType.DMA((count,2,ROWS)),
+            pltpu.SemaphoreType.DMA((count,ROWS,Y)),pltpu.SemaphoreType.DMA((count,ROWS,Y)),
+            pltpu.SemaphoreType.DMA((count,shards)),pltpu.SemaphoreType.DMA((count,shards)),
+            pltpu.SemaphoreType.DMA((count,))]
+
+class Gather:
+    def __init__(self,place,ins,outs,sems):
+        self.p=place; self.ins=ins; self.outs=outs
+        self.line_s,self.line_r,self.y_s,self.y_r,self.core_s,self.core_r,self.own=sems
+        self.sent=[]
+    def half(self,ref,shard=None):
+        n=ref.shape[-1]//2
+        cols=pl.ds(pl.multiple_of(self.p.core*n,128),n)
+        return ref.at[:,cols] if shard is None else ref.at[shard,:,cols]
+    def other_half(self,ref,shard):
+        n=ref.shape[-1]//2
+        return ref.at[shard,:,pl.ds(pl.multiple_of((1-self.p.core)*n,128),n)]
+    def send(self,cond,desc):
+        when(cond,desc.start); self.sent.append((cond,desc))
+    def copy(self,src,dst,ss,rs,dev):
+        return pltpu.make_async_remote_copy(src_ref=src,dst_ref=dst,send_sem=ss,recv_sem=rs,device_id=dev,device_id_type=MESH)
+    def pass_on(self,cond,zz,own,direction):
+        p=self.p; shard=zz*p.Y+p.y
+        for a,(i,o) in enumerate(zip(self.ins,self.outs)):
+            src=self.half(i) if own else self.half(o,shard); dst=self.half(o,shard)
+            for d in direction:
+                edge=(p.z<ROWS-1) if d==0 else (p.z>0)
+                c=edge if cond is None else jnp.logical_and(cond,edge)
+                self.send(c,self.copy(src,dst,self.line_s.at[a,d,zz],self.line_r.at[a,d,zz],p.near_z(1 if d==0 else -1)))
+            for k in range(1,p.Y):
+                self.send(cond,self.copy(src,dst,self.y_s.at[a,zz,k],self.y_r.at[a,zz,k],p.other_y(k)))
+            if not own:
+                self.send(cond,self.copy(src,dst,self.core_s.at[a,shard],self.core_r.at[a,shard],p.other_core()))
+    def begin(self):
+        for a,(i,o) in enumerate(zip(self.ins,self.outs)):
+            pltpu.make_async_copy(i,o.at[self.p.s],self.own.at[a]).start()
+        self.pass_on(None,self.p.z,True,(0,1))
+    def wave(self,w):
+        p=self.p
+        for d in (0,1):
+            zz=p.z-w if d==0 else p.z+w
+            cond=p.z>=w if d==0 else p.z+w<ROWS
+            for a,o in enumerate(self.outs):
+                ref=self.half(o,jnp.clip(zz,0,ROWS-1)*p.Y+p.y);
+                desc=self.copy(ref,ref,self.line_s.at[a,d,jnp.clip(zz,0,ROWS-1)],self.line_r.at[a,d,jnp.clip(zz,0,ROWS-1)],p.near_z(0))
+                when(cond,desc.wait_recv)
+            self.pass_on(cond,jnp.clip(zz,0,ROWS-1),False,(d,))
+    def across(self,w):
+        p=self.p
+        for zz,cond in (((p.z,None),) if w==0 else ((p.z-w,p.z>=w),(p.z+w,p.z+w<ROWS))):
+            zz=jnp.clip(zz,0,ROWS-1)
+            for k in range(1,p.Y):
+                shard=zz*p.Y+lax.rem(p.y-k+p.Y,p.Y)
+                for a,o in enumerate(self.outs):
+                    ref=self.half(o,shard)
+                    desc=self.copy(ref,ref,self.y_s.at[a,zz,k],self.y_r.at[a,zz,k],p.other_y(k))
+                    when(cond,desc.wait_recv)
+                    self.send(cond,self.copy(ref,ref,self.core_s.at[a,shard],self.core_r.at[a,shard],p.other_core()))
+    def finish(self):
+        p=self.p
+        for a,(i,o) in enumerate(zip(self.ins,self.outs)):
+            for k in range(1,p.S):
+                shard=lax.rem(p.s+k,p.S)
+                ref=self.other_half(o,shard)
+                self.copy(ref,ref,self.core_s.at[a,shard],self.core_r.at[a,shard],p.other_core()).wait_recv()
+            pltpu.make_async_copy(i,o.at[p.s],self.own.at[a]).wait()
+        for cond,desc in self.sent: when(cond,desc.wait_send)
+    def steps(self):
+        return [self.begin,lambda: self.wave(1),lambda: self.across(0),lambda: self.wave(2),lambda: self.across(1),lambda: self.wave(3),lambda: self.across(2),lambda: self.across(3),self.finish]
+
+def gather_body(shards,reps,count,*refs):
+    ins,outs,sems=refs[:count],refs[count:2*count],refs[2*count:]
+    place=Place(shards,reps)
+    meet(place,False)
+    for step in Gather(place,ins,outs,sems).steps(): step()
+
+def gather_now(arrays,shards,reps,collective_id):
+    count=len(arrays)
+    return pl.pallas_call(partial(gather_body,shards,reps,count),
+        in_specs=[pl.BlockSpec(memory_space=pltpu.VMEM)]*count,
+        out_specs=[pl.BlockSpec(memory_space=pl.ANY)]*count,
+        out_shape=[jax.ShapeDtypeStruct((shards,)+a.shape,a.dtype) for a in arrays],
+        scratch_shapes=gather_semaphores(count,shards),
+        compiler_params=pltpu.CompilerParams(collective_id=collective_id,has_side_effects=True,vmem_limit_bytes=16<<20),
+        name="gather_weights")(*arrays)
+
+ORDER=(3,0,2,1)
+def reduce_scratch(shapes,shards,reps,store=True):
+    S=shards; Y=S//ROWS; X=reps//2; A=len(shapes)
+    out=[]
+    for r,c in shapes:
+        n=c//2
+        out+=[pltpu.VMEM((S,r,n),bf),pltpu.VMEM((S,r,n),bf),pltpu.VMEM((max(Y-1,1),ROWS,r,n),bf),
+              pltpu.VMEM((2,ROWS,r,n),bf),pltpu.VMEM((X,r,n),bf)]
+    dma=pltpu.SemaphoreType.DMA
+    return out+[dma((A,S)),dma((A,S)),dma((A,S)),dma((A,Y,ROWS)),dma((A,Y,ROWS)),dma((A,2,ROWS)),dma((A,2,ROWS)),dma((A,X)),dma((A,X)),dma((A,)),dma((A,))]
+class Reduce:
+    def __init__(self,place,ins,outs,scratch):
+        self.p=place; self.ins=ins; self.outs=outs; A=len(ins); self.A=range(A)
+        self.bufs=[scratch[5*a:5*a+5] for a in range(A)]
+        (self.own,self.core_s,self.core_r,self.y_s,self.y_r,self.line_s,self.line_r,self.x_s,self.x_r,self.end_s,self.end_r)=scratch[5*A:]
+        self.sent=[]
+    def copy(self,src,dst,ss,rs,dev):
+        return pltpu.make_async_remote_copy(src_ref=src,dst_ref=dst,send_sem=ss,recv_sem=rs,device_id=dev,device_id_type=MESH)
+    def send(self,cond,desc):
+        when(cond,desc.start); self.sent.append((cond,desc))
+    def half(self,a,shard,core):
+        n=self.ins[a].shape[-1]//2
+        return self.ins[a].at[shard,:,pl.ds(pl.multiple_of(core*n,128),n)]
+    def add(self,dst,others):
+        rows=dst.shape[0]; step=48 if rows%48==0 else 16
+        def body(i,_):
+            at=pl.ds(pl.multiple_of(i*step,16),step)
+            value=dst[at,:].astype(f32)
+            for o in others: value=value+o[at,:].astype(f32)
+            dst[at,:]=value.astype(bf)
+            return 0
+        lax.fori_loop(0,rows//step,body,0)
+    def begin(self):
+        p=self.p
+        for k in list(range(1,p.Y))+[0]:
+            for d in ORDER:
+                shard=d*p.Y+lax.rem(p.y+k,p.Y)
+                for a in self.A:
+                    H,Rc=self.bufs[a][0:2]
+                    self.send(None,self.copy(self.half(a,shard,1-p.core),Rc.at[shard],self.core_s.at[a,shard],self.core_r.at[a,shard],p.other_core()))
+                    pltpu.make_async_copy(self.half(a,shard,p.core),H.at[shard],self.own.at[a,shard]).start()
+    def join_core(self,shard):
+        p=self.p
+        for a in self.A:
+            H,Rc=self.bufs[a][0:2]
+            pltpu.make_async_copy(self.half(a,shard,p.core),H.at[shard],self.own.at[a,shard]).wait()
+            self.copy(Rc.at[shard],Rc.at[shard],self.core_s.at[a,shard],self.core_r.at[a,shard],p.other_core()).wait_recv()
+            self.add(H.at[shard],[Rc.at[shard]])
+    def to_y(self,d):
+        p=self.p
+        for k in range(1,p.Y):
+            shard=d*p.Y+lax.rem(p.y+k,p.Y)
+            self.join_core(shard)
+            for a in self.A:
+                H,_,Ry=self.bufs[a][0:3]
+                self.send(None,self.copy(H.at[shard],Ry.at[k-1,d],self.y_s.at[a,k,d],self.y_r.at[a,k,d],p.other_y(k)))
+    def own_y(self,d):
+        self.join_core(d*self.p.Y+self.p.y)
+    def line(self,d):
+        p=self.p; shard=d*p.Y+p.y
+        for a in self.A:
+            H,_,Ry,Rl=self.bufs[a][0:4]
+            for k in range(1,p.Y):
+                self.copy(Ry.at[k-1,d],Ry.at[k-1,d],self.y_s.at[a,k,d],self.y_r.at[a,k,d],p.other_y(k)).wait_recv()
+            self.add(H.at[shard],[Ry.at[k-1,d] for k in range(1,p.Y)])
+        for up in (0,1):
+            passes=(p.z<d) if up==0 else (p.z>d)
+            inner=(p.z>0) if up==0 else (p.z<ROWS-1)
+            def add_in(up=up):
+                for a in self.A:
+                    H,Rl=self.bufs[a][0],self.bufs[a][3]
+                    self.copy(Rl.at[up,d],Rl.at[up,d],self.line_s.at[a,up,d],self.line_r.at[a,up,d],p.near_z(0)).wait_recv()
+                    self.add(H.at[shard],[Rl.at[up,d]])
+            pl.when(jnp.logical_and(passes,inner))(add_in)
+            for a in self.A:
+                H,Rl=self.bufs[a][0],self.bufs[a][3]
+                self.send(passes,self.copy(H.at[shard],Rl.at[up,d],self.line_s.at[a,up,d],self.line_r.at[a,up,d],p.near_z(1 if up==0 else -1)))
+    def to_x(self):
+        p=self.p
+        for up in (0,1):
+            def add_in(up=up):
+                for a in self.A:
+                    H,Rl=self.bufs[a][0],self.bufs[a][3]
+                    self.copy(Rl.at[up,p.z],Rl.at[up,p.z],self.line_s.at[a,up,p.z],self.line_r.at[a,up,p.z],p.near_z(0)).wait_recv()
+                    self.add(H.at[p.s],[Rl.at[up,p.z]])
+            pl.when((p.z>0) if up==0 else (p.z<ROWS-1))(add_in)
+        for a in self.A:
+            H,Rx=self.bufs[a][0],self.bufs[a][4]
+            for k in range(1,p.X):
+                self.send(None,self.copy(H.at[p.s],Rx.at[p.x],self.x_s.at[a,k],self.x_r.at[a,p.x],p.other_x(k)))
+    def to_core(self):
+        p=self.p
+        for a in self.A:
+            H,Rx=self.bufs[a][0],self.bufs[a][4]; out=self.outs[a]
+            for k in range(1,p.X):
+                src=lax.rem(p.x-k+p.X,p.X)
+                self.copy(Rx.at[src],Rx.at[src],self.x_s.at[a,k],self.x_r.at[a,src],p.other_x(k)).wait_recv()
+            rows=H.shape[1]; step=48 if rows%48==0 else 16
+            def body(i,_):
+                at=pl.ds(pl.multiple_of(i*step,16),step)
+                own=H[p.s,at,:].astype(f32)
+                value=jnp.zeros_like(own)
+                for q in range(p.X):
+                    value=value+jnp.where(p.x==q,own,Rx[q,at,:].astype(f32))
+                out[p.core,at,:]=value
+                return 0
+            lax.fori_loop(0,rows//step,body,0)
+        for a in self.A:
+            out=self.outs[a]
+            self.send(None,self.copy(out.at[p.core],out.at[p.core],self.end_s.at[a],self.end_r.at[a],p.other_core()))
+    def finish(self):
+        p=self.p
+        for a in self.A:
+            ref=self.outs[a].at[1-p.core]
+            self.copy(ref,ref,self.end_s.at[a],self.end_r.at[a],p.other_core()).wait_recv()
+        for cond,desc in self.sent: when(cond,desc.wait_send)
+    def steps(self):
+        part=lambda f,d: (lambda: f(d))
+        return [self.begin]+[part(self.to_y,d) for d in ORDER]+[part(self.own_y,d) for d in ORDER]+[part(self.line,d) for d in ORDER]+[self.to_x,self.to_core,self.finish]
+def reduce_body(shards,reps,count,*refs):
+    ins,outs,scratch=refs[:count],refs[count:2*count],refs[2*count:]
+    place=Place(shards,reps)
+    meet(place,True)
+    for step in Reduce(place,ins,outs,scratch).steps(): step()
+def reduce_now(arrays,shards,reps,collective_id):
+    count=len(arrays)
+    return pl.pallas_call(partial(reduce_body,shards,reps,count),
+        in_specs=[pl.BlockSpec(memory_space=pl.ANY)]*count,
+        out_specs=[pl.BlockSpec(memory_space=pltpu.VMEM)]*count,
+        out_shape=[jax.ShapeDtypeStruct((2,a.shape[1],a.shape[2]//2),f32) for a in arrays],
+        scratch_shapes=reduce_scratch([a.shape[1:] for a in arrays],shards,reps),
+        compiler_params=pltpu.CompilerParams(collective_id=collective_id,has_side_effects=True,vmem_limit_bytes=50<<20),
+        name="reduce_grads")(*arrays)
+
+
+def norm_stats(x):
+    c=jnp.mean(x,axis=-1,keepdims=True)
+    xc=x-c
+    r=lax.rsqrt(jnp.mean(xc*xc,axis=-1,keepdims=True)+eps_norm)
+    return xc*r,r
+
+def norm_back(up,normed,r,gain):
+    g=up*gain
+    return r*(g-jnp.mean(g,axis=-1,keepdims=True)-normed*jnp.mean(g*normed,axis=-1,keepdims=True))
+
+def colsum(x): return jnp.sum(x,axis=0,keepdims=True)
+
+def gelu_parts(u):
+    cdf=0.5+0.5*lax.erf(u*0.7071067811865476)
+    pdf=jnp.exp(-0.5*u*u)*0.3989422804014327
+    return u*cdf,cdf+u*pdf
+
+def middle_body(len_ref,h_ref,a_ref,ct_ref,ow_ref,uw_ref,dw_ref,vec_ref,ub_ref,
+               out_ref,bs_ref,ba_ref,act,pl_,low_ref,d2_ref,sl_ref,small_ref,ubg_ref,
+               gp,n1_ref,*,T,sub_rows,chunk):
+    i=pl.program_id(0)
+    per=LEN//T
+    count=len_ref[i//per]
+    @pl.when(i==0)
+    def _():
+        small_ref[...]=jnp.zeros_like(small_ref); ubg_ref[...]=jnp.zeros_like(ubg_ref)
+    out_b,g1,b1,down_b,g2,b2=[vec_ref[j:j+1,:] for j in range(6)]
+    parts=[slice(k,k+sub_rows) for k in range(0,T,sub_rows)]
+    r1s=[];sums=[]
+    xs=[dot_nn(a_ref[p,:],ow_ref[...]) for p in parts]
+    for p,x in zip(parts,xs):
+        n1,r1=norm_stats(h_ref[p,:]+x+out_b)
+        n1_ref[p,:]=n1; r1s.append(r1)
+        low_ref[p,:]=(n1*g1+b1).astype(bf)
+    for j in range(0,FF,chunk):
+        sl=slice(j,j+chunk)
+        for p in parts:
+            u=dot_nn(low_ref[p,:],uw_ref[:,sl])+ub_ref[:,sl]
+            a,g=gelu_parts(u)
+            act[p,sl]=a.astype(bf); gp[p,sl]=g.astype(gp.dtype)
+    ys=[dot_nn(act[p,:],dw_ref[...]) for p in parts]
+    for p,y in zip(parts,ys):
+        pos=lax.broadcasted_iota(jnp.int32,(sub_rows,1),0)+(i%per)*T+p.start
+        valid=jnp.where(pos<count,1.0,0.0)
+        second=n1_ref[p,:]*g1+b1+y+down_b
+        n2,r2=norm_stats(second)
+        out_ref[p,:]=valid*(n2*g2+b2)
+        up=valid*ct_ref[p,:]
+        b2nd=norm_back(up,n2,r2,g2)
+        d2_ref[p,:]=b2nd.astype(bf)
+        bs_ref[p,:]=b2nd
+        sums.append(jnp.concatenate([colsum(b2nd),colsum(up*n2),colsum(up)],axis=0))
+    small_ref[3:6,:]+=sum(sums[1:],sums[0])
+    for j in range(0,FF,chunk):
+        sl=slice(j,j+chunk)
+        cs=[]
+        for p in parts:
+            bp=dot_nt(d2_ref[p,:],dw_ref[sl,:])*gp[p,sl].astype(f32)
+            cs.append(colsum(bp))
+            pl_[p,sl]=bp.astype(bf)
+        ubg_ref[:,sl]+=sum(cs[1:],cs[0])
+    zs=[dot_nt(pl_[p,:],uw_ref[...]) for p in parts]
+    sums=[]
+    for p,z,r1 in zip(parts,zs,r1s):
+        bfirst=z+bs_ref[p,:]
+        n1=n1_ref[p,:]
+        bsum=norm_back(bfirst,n1,r1,g1)
+        bs_ref[p,:]=bsum
+        sl_ref[p,:]=bsum.astype(bf)
+        sums.append(jnp.concatenate([colsum(bsum),colsum(bfirst*n1),colsum(bfirst)],axis=0))
+    small_ref[0:3,:]+=sum(sums[1:],sums[0])
+    for p in parts:
+        ba_ref[p,:]=dot_nt(sl_ref[p,:],ow_ref[...]).astype(bf)
+
+def middle(lengths,hidden,att,ct,ow,uw,dw,vec,ub,T=512,chunk=768,gpt=f32,sub_rows=256):
+    tokens=hidden.shape[0]
+    tile=lambda n=D: pl.BlockSpec((T,n),lambda i,l:(i,0))
+    const=lambda shape: pl.BlockSpec(shape,lambda i,l:(0,0),pipeline_mode=pl.Buffered(1))
+    whole=lambda shape: pl.BlockSpec(shape,lambda i,l:(0,0))
+    sd=lambda n,dt: jax.ShapeDtypeStruct((tokens,n),dt)
+    return pl.pallas_call(
+        partial(middle_body,T=T,chunk=chunk,sub_rows=sub_rows),
+        grid_spec=pltpu.PrefetchScalarGridSpec(num_scalar_prefetch=1,grid=(tokens//T,),
+          in_specs=[tile(),tile(),tile(),const((D,D)),const((D,FF)),const((FF,D)),whole((8,D)),whole((1,FF))],
+          out_specs=[tile(),tile(),tile(),tile(FF),tile(FF),tile(),tile(),tile(),whole((8,D)),whole((1,FF))],
+          scratch_shapes=[pltpu.VMEM((T,FF),gpt),pltpu.VMEM((T,D),f32)]),
+        out_shape=[sd(D,f32),sd(D,f32),sd(D,bf),sd(FF,bf),sd(FF,bf),sd(D,bf),sd(D,bf),sd(D,bf),jax.ShapeDtypeStruct((8,D),f32),jax.ShapeDtypeStruct((1,FF),f32)],
+        compiler_params=pltpu.CompilerParams(vmem_limit_bytes=63<<20),
+        name="middle")(lengths,hidden,att,ct,ow,uw,dw,vec,ub)
+
+
+def weight_grad_body(l_ref,r_ref,out_ref):
+    out_ref[...]=dot_tn(l_ref[...],r_ref[...]).astype(bf)
+def weight_grad(left,right,block,name,columns=False):
+    K,M=left.shape; N=right.shape[1]
+    if columns:
+        grid,lb,rb,ob,li,ri,oi=(N//block,),(K,M),(K,block),(M,block),(lambda i:(0,0)),(lambda i:(0,i)),(lambda i:(0,i))
+    else:
+        grid,lb,rb,ob,li,ri,oi=(M//block,),(K,block),(K,N),(block,N),(lambda i:(0,i)),(lambda i:(0,0)),(lambda i:(i,0))
+    return pl.pallas_call(weight_grad_body,grid=grid,
+        in_specs=[pl.BlockSpec(lb,li),pl.BlockSpec(rb,ri)],out_specs=pl.BlockSpec(ob,oi),
+        out_shape=jax.ShapeDtypeStruct((M,N),bf),
+        cost_estimate=pl.CostEstimate(flops=2*K*M*N,bytes_accessed=2*(K*M+K*N+M*N),transcendentals=0),
+        compiler_params=pltpu.CompilerParams(vmem_limit_bytes=60<<20),name=name)(left,right)
+
+
+WIDE = 4096
+
+
+def shard_vectors(vectors):
+    row = jnp.concatenate(vectors)
+    return jnp.pad(row, (0, WIDE - row.shape[0])).reshape(16, 256)
 
 
 def local(
@@ -305,114 +657,108 @@
     norm2_gain,
     norm2_bias,
     cotangent,
+    *,
+    shards,
+    reps,
 ):
     seqs = hidden.shape[0]
     tokens = seqs * LEN
-    gather = partial(lax.all_gather, axis_name="shard", axis=0, tiled=True)
-    vectors = (
-        query_bias,
-        value_bias,
-        out_bias,
-        norm1_gain,
-        norm1_bias,
-        down_bias,
-        norm2_gain,
-        norm2_bias,
-        up_bias,
+    part = D // shards
+    vectors = shard_vectors(
+        (
+            query_bias,
+            value_bias,
+            out_bias,
+            norm1_gain,
+            norm1_bias,
+            down_bias,
+            norm2_gain,
+            norm2_bias,
+            up_bias,
+        )
     )
-    widths = [v.shape[0] for v in vectors]
-    marks = [sum(widths[:i]) for i in range(len(widths) + 1)]
-    packed = lax.all_gather(jnp.concatenate(vectors)[None], "shard", axis=0, tiled=True)
-    query_b, value_b, out_b, gain1, shift1, down_b, gain2, shift2, up_b = [
-        packed[:, marks[i] : marks[i + 1]].reshape(-1).astype(f32) for i in range(len(widths))
-    ]
-    in_w = gather(to_pairs(input_weight))
-    out_w = gather(out_weight)
-    up_w = gather(up_weight)
-    down_w = gather(down_weight)
+    in_w, vectors = gather_now((to_pairs(input_weight), vectors), shards, reps, 1)
+    out_w, up_w, down_w = gather_now((out_weight, up_weight, down_weight), shards, reps, 2)
+    in_w, out_w, up_w, down_w = [w.reshape(-1, w.shape[-1]) for w in (in_w, out_w, up_w, down_w)]
+    vectors = vectors.reshape(shards, WIDE).astype(f32)
+    table = vectors[:, : 8 * part].reshape(shards, 8, part).transpose(1, 0, 2).reshape(8, D)
+    bias_pairs = to_pairs(
+        jnp.concatenate([table[0], jnp.zeros((D,), f32), table[1]])
+    ).reshape(PAIRS, 1, 384)
+    norm_rows = jnp.concatenate([table[2:], table[:2]])
+    up_b = vectors[:, 8 * part : 8 * part + FF // shards].reshape(1, FF)
 
     flat = hidden.reshape(tokens, D)
     rounded = flat.astype(bf)
     rows = clusters.reshape(seqs, PAIRS, 2, LEN)
-    bias_pairs = to_pairs(jnp.concatenate([query_b, jnp.zeros_like(query_b), value_b]))
-    attended, proj = attention_forward(
-        lengths, rounded, in_w, bias_pairs.reshape(PAIRS, 1, 384), rows
+    attended, proj = attention_forward(lengths, rounded, in_w, bias_pairs, rows)
+    (
+        result,
+        back_sum,
+        back_attended,
+        activated,
+        pre_low,
+        first_low,
+        second_low,
+        sum_low,
+        norm_sums,
+        up_b_sum,
+    ) = middle(
+        lengths,
+        flat,
+        attended,
+        cotangent.reshape(tokens, D),
+        out_w,
+        up_w,
+        down_w,
+        norm_rows,
+        up_b,
     )
-    positions = jnp.arange(LEN, dtype=jnp.int32)
-    valid = (positions[None, :] < lengths[:, None]).astype(f32).reshape(tokens, 1)
-    first_out, normed_one, scale_one = norm_forward(
-        flat + dot_nn(attended, out_w) + out_b, gain1, shift1
+    down_g = weight_grad(activated, second_low, D, "down_weight_grad")
+    up_g = weight_grad(first_low, pre_low, D, "up_weight_grad", True)
+    out_g = weight_grad(attended, sum_low, D // 2, "out_weight_grad")
+    dproj, in_g, bias_sums = attention_backward(lengths, rounded, proj, back_attended, rows)
+    down_s, up_s, out_s = reduce_now(
+        [g.reshape(shards, -1, g.shape[-1]) for g in (down_g, up_g, out_g)], shards, reps, 3
     )
-    first_low = first_out.astype(bf)
-    pre_gelu = dot_nn(first_low, up_w) + up_b
-    activated = jax.nn.gelu(pre_gelu, approximate=False).astype(bf)
-    second_sum = first_out + dot_nn(activated, down_w) + down_b
-    second_out, normed_two, scale_two = norm_forward(second_sum, gain2, shift2)
-    result = (second_out * valid).reshape(seqs, LEN, D)
-
-    back_out = cotangent.reshape(tokens, D) * valid
-    back_second, gain2_grad, shift2_grad = norm_backward(back_out, normed_two, scale_two, gain2)
-    down_b_grad = jnp.sum(back_second, axis=0)
-    second_low = back_second.astype(bf)
-    down_w_grad = dot_tn(activated, second_low).astype(bf)
-    back_act = dot_nt(second_low, down_w)
-    back_pre = jax.vjp(partial(jax.nn.gelu, approximate=False), pre_gelu)[1](back_act)[0]
-    up_b_grad = jnp.sum(back_pre, axis=0)
-    pre_low = back_pre.astype(bf)
-    up_w_grad = dot_tn(first_low, pre_low).astype(bf)
-    back_first = dot_nt(pre_low, up_w) + back_second
-    back_sum, gain1_grad, shift1_grad = norm_backward(back_first, normed_one, scale_one, gain1)
-    out_b_grad = jnp.sum(back_sum, axis=0)
-    sum_low = back_sum.astype(bf)
-    out_w_grad = dot_tn(attended, sum_low).astype(bf)
-    back_attended = dot_nt(sum_low, out_w).astype(bf)
-    dproj, in_w_grad, db = attention_backward(lengths, rounded, proj, back_attended, rows)
-    db = jnp.sum(db, axis=0)
-    query_b_grad = db[:, 0:2, DH:].reshape(D)
-    value_b_grad = jnp.concatenate([db[:, 2, :DH], db[:, 3, DH:]], axis=1).reshape(D)
-    back_input = (back_sum + dot_nt(dproj, in_w)).reshape(seqs, LEN, D)
-
-    def scatter(grad):
-        part = lax.psum_scatter(grad, "shard", scatter_dimension=0, tiled=True)
-        return lax.psum(part.astype(f32), "rep")
-
-    shards = packed.shape[0]
+    bias_sums = jnp.sum(bias_sums, axis=0)
+    query_sum = bias_sums[:, 0:2, DH:].reshape(D)
+    value_sum = jnp.concatenate([bias_sums[:, 2, :DH], bias_sums[:, 3, DH:]], axis=1).reshape(D)
+    table = jnp.concatenate([query_sum[None], value_sum[None], norm_sums[:6]])
     small = jnp.concatenate(
         [
-            g.reshape(shards, -1)
-            for g in (
-                query_b_grad,
-                value_b_grad,
-                out_b_grad,
-                gain1_grad,
-                shift1_grad,
-                down_b_grad,
-                gain2_grad,
-                shift2_grad,
-                up_b_grad,
-            )
+            table.reshape(8, shards, part).transpose(1, 0, 2).reshape(shards, 8 * part),
+            up_b_sum.reshape(shards, FF // shards),
         ],
         axis=1,
+    ).astype(bf)
+    small = jnp.pad(small, ((0, 0), (0, WIDE - small.shape[1]))).reshape(shards, 16, 256)
+    in_s, small_s = reduce_now(
+        [in_g.reshape(shards, part, 3 * D), small], shards, reps, 4
     )
-    small = lax.psum(small, ("rep", "shard"))
-    mine = lax.dynamic_index_in_dim(small, lax.axis_index("shard"), 0, keepdims=False)
-    small = [mine[marks[i] : marks[i + 1]] for i in range(len(widths))]
+    back_input = (back_sum + dot_nt(dproj, in_w)).reshape(seqs, LEN, D)
+
+    def whole(halves):
+        return jnp.concatenate([halves[0], halves[1]], axis=1)
+
+    small_s = whole(small_s).reshape(WIDE)
+    vec = [small_s[i * part : (i + 1) * part] for i in range(8)]
     return (
-        result,
+        result.reshape(seqs, LEN, D),
         back_input,
-        from_pairs(scatter(in_w_grad)),
-        small[0],
-        small[1],
-        scatter(out_w_grad),
-        small[2],
-        small[3],
-        small[4],
-        scatter(up_w_grad),
-        small[8],
-        scatter(down_w_grad),
-        small[5],
-        small[6],
-        small[7],
+        from_pairs(whole(in_s)),
+        vec[0],
+        vec[1],
+        whole(out_s),
+        vec[2],
+        vec[3],
+        vec[4],
+        whole(up_s),
+        small_s[8 * part : 8 * part + FF // shards],
+        whole(down_s),
+        vec[5],
+        vec[6],
+        vec[7],
     )
 
 
@@ -435,7 +781,7 @@
         vector,
     )
     return jax.shard_map(
-        local,
+        partial(local, shards=mesh.shape["shard"], reps=mesh.shape["rep"]),
         mesh=mesh,
         in_specs=(tokens, P(("rep", "shard")), tokens) + params + (tokens,),
         out_specs=(tokens, tokens) + params,

time: 915 us -> 549 us (0.60)
  waiting for transfers between devices: 376 us -> 0 us
  Pallas kernels: 154 us -> 498 us
  matrix products: 205 us -> 11.7 us
  blocking collectives: 114 us -> 0 us
  other arithmetic: 27.1 us -> 8.73 us
  between operations: 14.7 us -> 1.55 us
    pallas_call x0 -> x8, Pallas kernels: none -> 345 us  [the longest x2 154 us: reduce_now(): pl.pallas_call(partial(reduce_body, shards, reps, count), in_specs=[pl.Bl...]
    reduce_scatter x4 -> x0, waiting for transfers between devices: 267 us -> none  [scatter(): part = lax.psum_scatter(grad, 'shard', scatter_dimension=0, tiled=True)]
    dot_general x6 -> x0, matrix products: 134 us -> none  [the longest x3 93.1 us: dot_nn(): lax.dot_general(left, right, (((1,), (0,)), ((), ())), preferred_element_...]
    all_gather x4 -> x0, waiting for transfers between devices: 92.2 us -> none  [the longest x1 52.9 us: local(): up_w = gather(up_weight)]
    psum x2 -> x0, blocking collectives: 91.2 us -> none  [the longest x1 52.3 us: scatter(): return lax.psum(part.astype(f32), 'rep')]
    dot_general x4 -> x1, matrix products: 70.8 us -> 11.7 us  [dot_nt(): lax.dot_general(left, right, (((1,), (1,)), ((), ())), preferred_element_...]
    all_gather x1 -> x0, blocking collectives: 22.6 us -> none  [local(): lax.all_gather(jnp.concatenate(vectors)[None], 'shard', axis=0, tiled=True)]
    reduce_sum x7 -> x1, other arithmetic: 22 us -> 0.01 us  [local(): bias_sums = jnp.sum(bias_sums, axis=0)]
  transfers between devices with their start and end apart: 9 -> 0, of which waited for: 7 -> 0; matrix products, arithmetic and copies ran while one was open for 17% -> 0% of each run, Pallas kernels for 7% -> 0%
where the time goes in v2:
time: 549 us; the launch traced here: 543 us
  Pallas kernels  498 us (91%)
  local copies, waits for them, and re-layouts  22.6 us (4%)
  matrix products  11.7 us (2%)
  other arithmetic  8.73 us (2%)
    pallas_call x2, Pallas kernels, reduce_now(): pl.pallas_call(partial(reduce_body, shards, reps, count), in_specs=[pl.Bl...  154 us
    pallas_call x1, Pallas kernels, attention_backward(): pl.pallas_call(attention_backward_body, grid_spec=pltpu.PrefetchScalarGri...  94.3 us
    pallas_call x2, Pallas kernels, gather_now(): pl.pallas_call(partial(gather_body, shards, reps, count), in_specs=[pl.Bl...  92.8 us
    pallas_call x1, Pallas kernels, middle(): pl.pallas_call(partial(middle_body, T=T, chunk=chunk, sub_rows=sub_rows),...  62.1 us
    pallas_call x1, Pallas kernels, attention_forward(): pl.pallas_call(attention_forward_body, grid_spec=pltpu.PrefetchScalarGrid...  59.2 us
    pallas_call x3, Pallas kernels, weight_grad(): pl.pallas_call(weight_grad_body, grid=grid, in_specs=[pl.BlockSpec(lb, li...  35.4 us
    unnamed x50, local copies, waits for them, and re-layouts  12.2 us
    dot_general x1, matrix products, dot_nt(): lax.dot_general(left, right, (((1,), (1,)), ((), ())), preferred_element_...  11.7 us

profile of v2, /device:TPU:9, one launch (start us, length us, event | category | flops | bytes accessed | tf_op | source)
XLA Modules:
  0.0 542.8 jit_solution(866135938369151322)
XLA Ops:
  0.6 6.1 %concatenate.56 = bf16[1152]{0:T(1024)(128)(2,1)S(1)} concatenate(bf16[96]{0:T(256)(128)(2,1)} %param.21, bf16[96]{0:T(256)(128)(2,1)} %param.22, bf16[96]{0:T(256)(128)(2,1)} %param.24, bf16[96]{0:T(256)(128)(2,1)} %param.25, bf16[96]{0:T(256)(128)(2,1)} %param.26, bf16[96]{0:T(256)(128)(2,1)} %param.30, bf16[96]{0:T(256)(128)(2,1)} %param.31, bf16[96]{0:T(256)(128)(2,1)} %param.32, ...), dimensions={0} | concatenate | bytes 4608 | tf_op jit(solution)/shard_map/concatenate | solution.py:638
  6.8 0.9 copy.117.row_ref
  7.7 1.3 copy.108
  9.3 0.2 copy.125.refs_0_
  9.5 0.0 copy-start.6
  9.5 0.0 copy-start.7
  9.5 0.0 copy-start.8
  9.5 0.0 copy-start.9
  9.6 4.8 bitcast_convert_fusion.x_ref
  14.4 25.9 %gather_weights.2 = (bf16[8,96,2304]{2,1,0:T(8,128)(2,1)S(1)}, bf16[8,16,256]{2,1,0:T(8,128)(2,1)S(1)}) custom-call(bf16[96,2304]{1,0:T(8,128)(2,1)S(1)} %copy.125.refs_0_, bf16[16,256]{1,0:T(8,128)(2,1)S(1)} %reshape.143.refs_1_), custom_call_target="tpu_custom_call" | custom-call | tf_op jit(solution)/shard_map/gather_weights/pallas_call | solution.py:385
  40.3 0.0 copy-start.11
  40.3 1.7 copy-done.11
  42.0 0.1 copy.135
  42.2 0.6 copy.136
  42.8 0.1 reshape.145
  42.9 0.1 slice.180
  43.0 0.1 slice.178
  43.1 0.6 pad_maximum_fusion.5.vec_ref
  43.7 0.1 squeeze.98
  43.8 0.1 squeeze.95
  43.9 0.1 concatenate.57
  44.0 0.0 copy-done.6
  44.0 0.0 copy-done.7
  44.0 0.0 copy-done.8
  44.0 66.9 %gather_weights.3 = (bf16[8,96,768]{2,1,0:T(8,128)(2,1)S(1)}, bf16[8,96,3072]{2,1,0:T(8,128)(2,1)S(1)}, bf16[8,384,768]{2,1,0:T(8,128)(2,1)S(1)}) custom-call(bf16[96,768]{1,0:T(8,128)(2,1)S(1)} %copy-done.8, bf16[96,3072]{1,0:T(8,128)(2,1)S(1)} %copy-done.6, bf16[384,768]{1,0:T(8,128)(2,1)S(1)} %copy-done.7), custom_call_target="tpu_custom_call" | custom-call | tf_op jit(solution)/shard_map/gather_weights/pallas_call | solution.py:385
  110.9 2.2 copy-done
  113.1 2.1 copy-done.1
  115.3 1.0 copy-done.4
  116.3 59.2 %attention_forward.1 = (bf16[2048,768]{1,0:T(8,128)(2,1)S(1)}, bf16[2048,2304]{1,0:T(8,128)(2,1)}) custom-call(s32[2]{0:T(128)S(1)} %copy-done.9, bf16[2048,768]{1,0:T(8,128)(2,1)} %bitcast_convert_fusion.x_ref, bf16[768,2304]{1,0:T(8,128)(2,1)} %bitcast.111, f32[6,1,384]{2,1,0:T(1,128)S(1)} %reshape_reshape.3.b_ref, s32[2,6,2,1024]{3,2,1,0:T(2,128)S(1)} %copy.117.row_ref), custom_call_target="tpu_custom_call" | custom-call | flops 44000002048 | bytes 24000000 | tf_op jit(solution)/shard_map/attention_forward/pallas_call | solution.py:86
  175.5 1.7 copy-done.2
  177.2 62.1 %middle.1 = (f32[2048,768]{1,0:T(8,128)}, f32[2048,768]{1,0:T(8,128)}, bf16[2048,768]{1,0:T(8,128)(2,1)}, bf16[2048,3072]{1,0:T(8,128)(2,1)}, bf16[2048,3072]{1,...) custom-call(s32[2]{0:T(128)} %len_ref.5, ...), custom_call_target="tpu_custom_call" | custom-call | tf_op jit(solution)/shard_map/middle/pallas_call | solution.py:608
  239.3 0.0 copy-start.13
  239.3 0.0 copy-start.14
  239.3 0.0 copy-start.10
  239.3 6.2 %out_weight_grad.1 = bf16[768,768]{1,0:T(8,128)(2,1)} custom-call(bf16[2048,768]{1,0:T(8,128)(2,1)} %copy-done.2, bf16[2048,768]{1,0:T(8,128)(2,1)} %get-tuple-element.61.r_ref), custom_call_target="tpu_custom_call" | custom-call | flops 2415919104 | bytes 7471104 | tf_op jit(solution)/shard_map/out_weight_grad/pallas_call | solution.py:627
  245.6 0.0 copy-done.14
  245.6 0.1 concatenate.62
  245.8 0.0 copy-start.15
  245.8 94.3 %attention_backward.1 = (bf16[2048,2304]{1,0:T(8,128)(2,1)}, bf16[768,2304]{1,0:T(8,128)(2,1)}, f32[2,6,4,128]{3,2,1,0:T(4,128)S(1)}) custom-call(s32[2]{0:T(128)S(1)} %copy-done.10, bf16[2048,768]{1,0:T(8,128)(2,1)S(1)} %copy-done.3, bf16[2048,2304]{1,0:T(8,128)(2,1)} %get-tuple-element.48.proj_ref, bf16[2048,768]{1,0:T(8,128)(2,1)} %get-tuple-element.49.datt_ref, ...), custom_call_target="tpu_custom_call" | custom-call | flops 70000001024 | bytes 30000000 | tf_op jit(solution)/shard_map/attention_backward/pallas_call | solution.py:212
  340.1 0.0 copy-done.15
  340.1 11.7 %convolution_add_fusion = f32[2048,768]{1,0:T(8,128)} fusion(f32[2048,768]{1,0:T(8,128)S(1)} %copy-done.15, bf16[2048,2304]{1,0:T(8,128)(2,1)} %get-tuple-element.50, bf16[768,2304]{1,0:T(8,128)(2,1)S(1)} %bitcast.112), kind=kOutput, calls=%fused_computation | convolution fusion | flops 7249330176 | bytes 25559040 | tf_op jit(solution)/shard_map/dot_general | solution.py:28
  351.8 0.1 slice.228
  351.9 0.1 concatenate.59
  352.0 0.1 fusion.13
  352.1 0.1 pad_maximum_fusion.6
  352.2 0.1 concatenate.61
  352.3 0.1 reshape.155
  352.4 46.1 %reduce_grads.2 = (f32[2,96,1152]{2,1,0:T(8,128)S(1)}, f32[2,16,128]{2,1,0:T(8,128)S(1)}) custom-call(bf16[8,96,2304]{2,1,0:T(8,128)(2,1)} %bitcast.117, bf16[8,16,256]{2,1,0:T(8,128)(2,1)S(1)} %bitcast.110), custom_call_target="tpu_custom_call" | custom-call | tf_op jit(solution)/shard_map/reduce_grads/pallas_call | solution.py:519
  398.5 0.1 fusion.11
  398.7 0.6 slice.237
  399.2 0.6 fusion.12
  399.8 0.2 copy.122
  400.1 0.2 copy.123
  400.3 0.1 fusion.1
  400.4 0.1 pad_maximum_fusion
  400.5 1.3 copy.124
  401.8 14.5 %down_weight_grad.1 = bf16[3072,768]{1,0:T(8,128)(2,1)} custom-call(bf16[2048,3072]{1,0:T(8,128)(2,1)} %get-tuple-element.57.l_ref, bf16[2048,768]{1,0:T(8,128)(2,1)} %get-tuple-element.58.r_ref), custom_call_target="tpu_custom_call" | custom-call | flops 9663676416 | bytes 20447232 | tf_op jit(solution)/shard_map/down_weight_grad/pallas_call | solution.py:627
  416.3 14.6 %up_weight_grad.1 = bf16[768,3072]{1,0:T(8,128)(2,1)} custom-call(bf16[2048,768]{1,0:T(8,128)(2,1)} %get-tuple-element.59.l_ref, bf16[2048,3072]{1,0:T(8,128)(2,1)} %get-tuple-element.60.r_ref), custom_call_target="tpu_custom_call" | custom-call | flops 9663676416 | bytes 20447232 | tf_op jit(solution)/shard_map/up_weight_grad/pallas_call | solution.py:627
  431.0 108.3 %reduce_grads.3 = (f32[2,384,384]{2,1,0:T(8,128)S(1)}, f32[2,96,1536]{2,1,0:T(8,128)S(1)}, f32[2,96,384]{2,1,0:T(8,128)S(1)}) custom-call(bf16[8,384,768]{2,1,0:T(8,128)(2,1)} %bitcast.115, bf16[8,96,3072]{2,1,0:T(8,128)(2,1)} %bitcast.116, bf16[8,96,768]{2,1,0:T(8,128)(2,1)S(1)} %bitcast.109), custom_call_target="tpu_custom_call" | custom-call | tf_op jit(solution)/shard_map/reduce_grads/pallas_call | solution.py:519
  539.3 0.7 pad_maximum_fusion.4
  540.0 0.1 slice_bitcast_fusion.3
  540.1 1.1 pad_maximum_fusion.1
  541.2 0.1 slice_bitcast_fusion.1
  541.3 1.1 pad_maximum_fusion.2
  (53 shorter events, 0.5 us)
Async XLA Ops:
  9.5 34.5 %copy-start.6 = (bf16[96,3072]{1,0:T(8,128)(2,1)S(1)}, bf16[96,3072]{1,0:T(8,128)(2,1)}, u32[]{:S(2)}) copy-start(bf16[96,3072]{1,0:T(8,128)(2,1)} %refs_1_.1) | copy-start | bytes 1769476
  9.5 34.5 %copy-start.7 = (bf16[384,768]{1,0:T(8,128)(2,1)S(1)}, bf16[384,768]{1,0:T(8,128)(2,1)}, u32[]{:S(2)}) copy-start(bf16[384,768]{1,0:T(8,128)(2,1)} %refs_2_.1) | copy-start | bytes 1769476
  9.5 34.5 %copy-start.8 = (bf16[96,768]{1,0:T(8,128)(2,1)S(1)}, bf16[96,768]{1,0:T(8,128)(2,1)}, u32[]{:S(2)}) copy-start(bf16[96,768]{1,0:T(8,128)(2,1)} %refs_0_.1) | copy-start | bytes 442372
  9.5 106.7 %copy-start.9 = (s32[2]{0:T(128)S(1)}, s32[2]{0:T(128)}, u32[]{:S(2)}) copy-start(s32[2]{0:T(128)} %len_ref.5) | copy-start | bytes 28
  40.3 1.8 copy-start.11
  110.9 2.2 copy-start
  113.1 2.1 copy-start.1
  115.3 1.0 copy-start.4
  175.5 1.7 copy-start.2
  239.3 6.3 %copy-start.13 = (f32[1,3072]{1,0:T(1,128)S(1)}, f32[1,3072]{1,0:T(1,128)}, u32[]{:S(2)}) copy-start(f32[1,3072]{1,0:T(1,128)} %get-tuple-element.54) | copy-start | bytes 36868
  239.3 6.3 %copy-start.14 = (f32[8,768]{1,0:T(8,128)S(1)}, f32[8,768]{1,0:T(8,128)}, u32[]{:S(2)}) copy-start(f32[8,768]{1,0:T(8,128)} %get-tuple-element.53) | copy-start | bytes 73732
  239.3 6.4 %copy-start.3 = (bf16[2048,768]{1,0:T(8,128)(2,1)S(1)}, bf16[2048,768]{1,0:T(8,128)(2,1)}, u32[]{:S(2)}) copy-start(bf16[2048,768]{1,0:T(8,128)(2,1)} %bitcast_convert_fusion.x_ref) | copy-start | bytes 9437188
  239.3 6.4 %copy-start.10 = (s32[2]{0:T(128)S(1)}, s32[2]{0:T(128)}, u32[]{:S(2)}) copy-start(s32[2]{0:T(128)} %len_ref.5) | copy-start | bytes 28
  245.8 94.3 %copy-start.12 = (bf16[8,96,2304]{2,1,0:T(8,128)(2,1)S(1)}, bf16[8,96,2304]{2,1,0:T(8,128)(2,1)}, u32[]{:S(2)}) copy-start(bf16[8,96,2304]{2,1,0:T(8,128)(2,1)} %copy-done.11) | copy-start | bytes 10616836
  245.8 94.3 %copy-start.15 = (f32[2048,768]{1,0:T(8,128)S(1)}, f32[2048,768]{1,0:T(8,128)}, u32[]{:S(2)}) copy-start(f32[2048,768]{1,0:T(8,128)} %get-tuple-element.47) | copy-start | bytes 18874372
  416.3 14.6 %copy-start.5 = (bf16[768,768]{1,0:T(8,128)(2,1)S(1)}, bf16[768,768]{1,0:T(8,128)(2,1)}, u32[]{:S(2)}) copy-start(bf16[768,768]{1,0:T(8,128)(2,1)} %out_weight_grad.1) | copy-start | bytes 3538948

commit v3 on v2

v3 whole, which is shorter than its diff:
```python
from functools import partial

import jax
import jax.numpy as jnp
from jax import lax
from jax.experimental import pallas as pl
from jax.experimental.pallas import tpu as pltpu
from jax.sharding import PartitionSpec as P

D = 768
H = 12
DH = 64
FF = 3072
CLUSTER = 128
LEN = 1024
PAIRS = H // 2
SLICES = [slice(c * CLUSTER, (c + 1) * CLUSTER) for c in range(LEN // CLUSTER)]
bf = jnp.bfloat16
f32 = jnp.float32
eps_norm = 1e-12


def dot_nn(left, right):
    return lax.dot_general(left, right, (((1,), (0,)), ((), ())), preferred_element_type=f32)


def dot_nt(left, right):
    return lax.dot_general(left, right, (((1,), (1,)), ((), ())), preferred_element_type=f32)


def dot_tn(left, right):
    return lax.dot_general(left, right, (((0,), (0,)), ((), ())), preferred_element_type=f32)


ROWS = 4
MESH=pl.DeviceIdType.MESH

def when(cond,do):
    if cond is None: do()
    else: pl.when(cond)(do)

class Place:
    def __init__(self,shards,reps):
        self.Y=shards//ROWS; self.S=shards; self.X=reps//2
        self.s=lax.axis_index("shard"); self.r=lax.axis_index("rep")
        self.z=self.s//self.Y; self.y=lax.rem(self.s,self.Y)
        self.core=lax.rem(self.r,2); self.x=self.r//2
    def near_z(self,step): return {"shard":self.s+step*self.Y}
    def other_y(self,k): return {"shard":self.z*self.Y+lax.rem(self.y+k,self.Y)}
    def other_core(self): return {"rep":self.r+1-2*self.core}
    def other_x(self,k): return {"rep":2*lax.rem(self.x+k,self.X)+self.core}

def meet(place,with_x):
    sem=pltpu.get_barrier_semaphore()
    def tell(dev): pl.semaphore_signal(sem,inc=1,device_id=dev,device_id_type=MESH)
    pl.when(place.z>0)(lambda: tell(place.near_z(-1)))
    pl.when(place.z<ROWS-1)(lambda: tell(place.near_z(1)))
    for k in range(1,place.Y): tell(place.other_y(k))
    tell(place.other_core())
    if with_x:
        for k in range(1,place.X): tell(place.other_x(k))
    others=place.Y+(place.X-1 if with_x else 0)
    inner=jnp.logical_and(place.z>0,place.z<ROWS-1)
    pl.when(inner)(lambda: pl.semaphore_wait(sem,others+2))
    pl.when(jnp.logical_not(inner))(lambda: pl.semaphore_wait(sem,others+1))

def gather_semaphores(count,shards):
    Y=shards//ROWS
    return [pltpu.SemaphoreType.DMA((count,2,ROWS)),pltpu.SemaphoreType.DMA((count,2,ROWS)),
            pltpu.SemaphoreType.DMA((count,ROWS,Y)),pltpu.SemaphoreType.DMA((count,ROWS,Y)),
            pltpu.SemaphoreType.DMA((count,shards)),pltpu.SemaphoreType.DMA((count,shards)),
            pltpu.SemaphoreType.DMA((count,))]

class Gather:
    def __init__(self,place,ins,outs,sems):
        self.p=place; self.ins=ins; self.outs=outs
        self.line_s,self.line_r,self.y_s,self.y_r,self.core_s,self.core_r,self.own=sems
        self.sent=[]
    def half(self,ref,shard=None):
        n=ref.shape[-1]//2
        cols=pl.ds(pl.multiple_of(self.p.core*n,128),n)
        return ref.at[:,cols] if shard is None else ref.at[shard,:,cols]
    def other_half(self,ref,shard):
        n=ref.shape[-1]//2
        return ref.at[shard,:,pl.ds(pl.multiple_of((1-self.p.core)*n,128),n)]
    def send(self,make):
        cond,desc=make()
        when(cond,desc.start); self.sent.append(make)
    def copy(self,src,dst,ss,rs,dev):
        return pltpu.make_async_remote_copy(src_ref=src,dst_ref=dst,send_sem=ss,recv_sem=rs,device_id=dev,device_id_type=MESH)
    def at(self,places):
        zz=self.p.z+places
        if places==0: return None,zz
        return jnp.logical_and(zz>=0,zz<ROWS),jnp.clip(zz,0,ROWS-1)
    def to_line(self,a,places,d):
        p=self.p; i,o=self.ins[a],self.outs[a]
        def make():
            cond,zz=self.at(places); shard=zz*p.Y+p.y
            edge=(p.z<ROWS-1) if d==0 else (p.z>0)
            src=self.half(i) if places==0 else self.half(o,shard)
            return (edge if cond is None else jnp.logical_and(cond,edge)),self.copy(src,self.half(o,shard),self.line_s.at[a,d,zz],self.line_r.at[a,d,zz],p.near_z(1 if d==0 else -1))
        self.send(make)
    def to_y(self,a,places,k):
        p=self.p; i,o=self.ins[a],self.outs[a]
        def make():
            cond,zz=self.at(places); shard=zz*p.Y+p.y
            src=self.half(i) if places==0 else self.half(o,shard)
            return cond,self.copy(src,self.half(o,shard),self.y_s.at[a,zz,k],self.y_r.at[a,zz,k],p.other_y(k))
        self.send(make)
    def to_core(self,a,places,k):
        p=self.p; o=self.outs[a]
        def make():
            cond,zz=self.at(places); shard=zz*p.Y+lax.rem(p.y-k+p.Y,p.Y)
            ref=self.half(o,shard)
            return cond,self.copy(ref,ref,self.core_s.at[a,shard],self.core_r.at[a,shard],p.other_core())
        self.send(make)
    def begin(self):
        for a,(i,o) in enumerate(zip(self.ins,self.outs)):
            for d in (0,1): self.to_line(a,0,d)
            for k in range(1,self.p.Y): self.to_y(a,0,k)
            pltpu.make_async_copy(i,o.at[self.p.s],self.own.at[a]).start()
    def wave(self,w):
        p=self.p
        for d in (0,1):
            places=-w if d==0 else w
            for a,o in enumerate(self.outs):
                cond,zz=self.at(places); ref=self.half(o,zz*p.Y+p.y)
                when(cond,self.copy(ref,ref,self.line_s.at[a,d,zz],self.line_r.at[a,d,zz],p.near_z(0)).wait_recv)
                self.to_line(a,places,d)
                for k in range(1,p.Y): self.to_y(a,places,k)
                self.to_core(a,places,0)
    def across(self,w):
        p=self.p
        for places in ((0,) if w==0 else (-w,w)):
            for k in range(1,p.Y):
                for a,o in enumerate(self.outs):
                    cond,zz=self.at(places); shard=zz*p.Y+lax.rem(p.y-k+p.Y,p.Y)
                    ref=self.half(o,shard)
                    when(cond,self.copy(ref,ref,self.y_s.at[a,zz,k],self.y_r.at[a,zz,k],p.other_y(k)).wait_recv)
                    self.to_core(a,places,k)
    def finish(self):
        p=self.p
        for a,(i,o) in enumerate(zip(self.ins,self.outs)):
            for k in range(1,p.S):
                shard=lax.rem(p.s+k,p.S)
                ref=self.other_half(o,shard)
                self.copy(ref,ref,self.core_s.at[a,shard],self.core_r.at[a,shard],p.other_core()).wait_recv()
            pltpu.make_async_copy(i,o.at[p.s],self.own.at[a]).wait()
        for make in self.sent:
            cond,desc=make()
            when(cond,desc.wait_send)
    def steps(self):
        return [self.begin,lambda: self.wave(1),lambda: self.across(0),lambda: self.wave(2),lambda: self.across(1),lambda: self.wave(3),lambda: self.across(2),lambda: self.across(3),self.finish]

def gather_body(shards,reps,count,*refs):
    ins,outs,sems=refs[:count],refs[count:2*count],refs[2*count:]
    place=Place(shards,reps)
    meet(place,False)
    for step in Gather(place,ins,outs,sems).steps(): step()

def gather_now(arrays,shards,reps,collective_id):
    count=len(arrays)
    return pl.pallas_call(partial(gather_body,shards,reps,count),
        in_specs=[pl.BlockSpec(memory_space=pltpu.VMEM)]*count,
        out_specs=[pl.BlockSpec(memory_space=pl.ANY)]*count,
        out_shape=[jax.ShapeDtypeStruct((shards,)+a.shape,a.dtype) for a in arrays],
        scratch_shapes=gather_semaphores(count,shards),
        compiler_params=pltpu.CompilerParams(collective_id=collective_id,has_side_effects=True,vmem_limit_bytes=16<<20),
        name="gather_weights")(*arrays)

ORDER=(3,0,2,1)
def reduce_scratch(shapes,shards,reps,store=True):
    S=shards; Y=S//ROWS; X=reps//2; A=len(shapes)
    out=[]
    for r,c in shapes:
        n=c//2
        out+=[pltpu.VMEM((S,r,n),bf),pltpu.VMEM((S,r,n),bf),pltpu.VMEM((max(Y-1,1),ROWS,r,n),bf),
              pltpu.VMEM((2,ROWS,r,n),bf),pltpu.VMEM((X,r,n),bf)]
    dma=pltpu.SemaphoreType.DMA
    return out+[dma((A,S)),dma((A,S)),dma((A,S)),dma((A,Y,ROWS)),dma((A,Y,ROWS)),dma((A,2,ROWS)),dma((A,2,ROWS)),dma((A,X)),dma((A,X)),dma((A,)),dma((A,))]
class Reduce:
    def __init__(self,place,ins,outs,scratch):
        self.p=place; self.ins=ins; self.outs=outs; A=len(ins); self.A=range(A)
        self.bufs=[scratch[5*a:5*a+5] for a in range(A)]
        (self.own,self.core_s,self.core_r,self.y_s,self.y_r,self.line_s,self.line_r,self.x_s,self.x_r,self.end_s,self.end_r)=scratch[5*A:]
        self.sent=[]
    def copy(self,src,dst,ss,rs,dev):
        return pltpu.make_async_remote_copy(src_ref=src,dst_ref=dst,send_sem=ss,recv_sem=rs,device_id=dev,device_id_type=MESH)
    def send(self,make):
        cond,desc=make()
        when(cond,desc.start); self.sent.append(make)
    def half(self,a,shard,core):
        n=self.ins[a].shape[-1]//2
        return self.ins[a].at[shard,:,pl.ds(pl.multiple_of(core*n,128),n)]
    def add(self,dst,others):
        rows=dst.shape[0]; step=48 if rows%48==0 else 16
        def body(i,_):
            at=pl.ds(pl.multiple_of(i*step,16),step)
            value=dst[at,:].astype(f32)
            for o in others: value=value+o[at,:].astype(f32)
            dst[at,:]=value.astype(bf)
            return 0
        lax.fori_loop(0,rows//step,body,0)
    def begin(self):
        p=self.p
        for k in list(range(1,p.Y))+[0]:
            for d in ORDER:
                shard=d*p.Y+lax.rem(p.y+k,p.Y)
                for a in self.A:
                    H,Rc=self.bufs[a][0:2]
                    self.send(lambda a=a,Rc=Rc,shard=shard: (None,self.copy(self.half(a,shard,1-p.core),Rc.at[shard],self.core_s.at[a,shard],self.core_r.at[a,shard],p.other_core())))
                    pltpu.make_async_copy(self.half(a,shard,p.core),H.at[shard],self.own.at[a,shard]).start()
    def join_core(self,shard):
        p=self.p
        for a in self.A:
            H,Rc=self.bufs[a][0:2]
            pltpu.make_async_copy(self.half(a,shard,p.core),H.at[shard],self.own.at[a,shard]).wait()
            self.copy(Rc.at[shard],Rc.at[shard],self.core_s.at[a,shard],self.core_r.at[a,shard],p.other_core()).wait_recv()
            self.add(H.at[shard],[Rc.at[shard]])
    def to_y(self,d):
        p=self.p
        for k in range(1,p.Y):
            shard=d*p.Y+lax.rem(p.y+k,p.Y)
            self.join_core(shard)
            for a in self.A:
                H,_,Ry=self.bufs[a][0:3]
                self.send(lambda a=a,H=H,Ry=Ry,k=k,shard=shard: (None,self.copy(H.at[shard],Ry.at[k-1,d],self.y_s.at[a,k,d],self.y_r.at[a,k,d],p.other_y(k))))
    def own_y(self,d):
        self.join_core(d*self.p.Y+self.p.y)
    def line(self,d):
        p=self.p; shard=d*p.Y+p.y
        for a in self.A:
            H,_,Ry,Rl=self.bufs[a][0:4]
            for k in range(1,p.Y):
                self.copy(Ry.at[k-1,d],Ry.at[k-1,d],self.y_s.at[a,k,d],self.y_r.at[a,k,d],p.other_y(k)).wait_recv()
            self.add(H.at[shard],[Ry.at[k-1,d] for k in range(1,p.Y)])
        for up in (0,1):
            passes=(p.z<d) if up==0 else (p.z>d)
            inner=(p.z>0) if up==0 else (p.z<ROWS-1)
            def add_in(up=up):
                for a in self.A:
                    H,Rl=self.bufs[a][0],self.bufs[a][3]
                    self.copy(Rl.at[up,d],Rl.at[up,d],self.line_s.at[a,up,d],self.line_r.at[a,up,d],p.near_z(0)).wait_recv()
                    self.add(H.at[shard],[Rl.at[up,d]])
            pl.when(jnp.logical_and(passes,inner))(add_in)
            for a in self.A:
                H,Rl=self.bufs[a][0],self.bufs[a][3]
                self.send(lambda a=a,H=H,Rl=Rl,up=up,passes=passes: (passes,self.copy(H.at[shard],Rl.at[up,d],self.line_s.at[a,up,d],self.line_r.at[a,up,d],p.near_z(1 if up==0 else -1))))
    def to_x(self):
        p=self.p
        for up in (0,1):
            def add_in(up=up):
                for a in self.A:
                    H,Rl=self.bufs[a][0],self.bufs[a][3]
                    self.copy(Rl.at[up,p.z],Rl.at[up,p.z],self.line_s.at[a,up,p.z],self.line_r.at[a,up,p.z],p.near_z(0)).wait_recv()
                    self.add(H.at[p.s],[Rl.at[up,p.z]])
            pl.when((p.z>0) if up==0 else (p.z<ROWS-1))(add_in)
        for a in self.A:
            H,Rx=self.bufs[a][0],self.bufs[a][4]
            for k in range(1,p.X):
                self.send(lambda a=a,H=H,Rx=Rx,k=k: (None,self.copy(H.at[p.s],Rx.at[p.x],self.x_s.at[a,k],self.x_r.at[a,p.x],p.other_x(k))))
    def to_core(self):
        p=self.p
        for a in self.A:
            H,Rx=self.bufs[a][0],self.bufs[a][4]; out=self.outs[a]
            for k in range(1,p.X):
                src=lax.rem(p.x-k+p.X,p.X)
                self.copy(Rx.at[src],Rx.at[src],self.x_s.at[a,k],self.x_r.at[a,src],p.other_x(k)).wait_recv()
            rows=H.shape[1]; step=48 if rows%48==0 else 16
            def body(i,_):
                at=pl.ds(pl.multiple_of(i*step,16),step)
                own=H[p.s,at,:].astype(f32)
                value=jnp.zeros_like(own)
                for q in range(p.X):
                    value=value+jnp.where(p.x==q,own,Rx[q,at,:].astype(f32))
                out[p.core,at,:]=value
                return 0
            lax.fori_loop(0,rows//step,body,0)
        for a in self.A:
            out=self.outs[a]
            self.send(lambda a=a,out=out: (None,self.copy(out.at[p.core],out.at[p.core],self.end_s.at[a],self.end_r.at[a],p.other_core())))
    def finish(self):
        p=self.p
        for a in self.A:
            ref=self.outs[a].at[1-p.core]
            self.copy(ref,ref,self.end_s.at[a],self.end_r.at[a],p.other_core()).wait_recv()
        for make in self.sent:
            cond,desc=make()
            when(cond,desc.wait_send)
    def steps(self):
        part=lambda f,d: (lambda: f(d))
        return [self.begin]+[part(self.to_y,d) for d in ORDER]+[part(self.own_y,d) for d in ORDER]+[part(self.line,d) for d in ORDER]+[self.to_x,self.to_core,self.finish]
def reduce_body(shards,reps,count,*refs):
    ins,outs,scratch=refs[:count],refs[count:2*count],refs[2*count:]
    place=Place(shards,reps)
    meet(place,True)
    for step in Reduce(place,ins,outs,scratch).steps(): step()
def reduce_now(arrays,shards,reps,collective_id):
    count=len(arrays)
    return pl.pallas_call(partial(reduce_body,shards,reps,count),
        in_specs=[pl.BlockSpec(memory_space=pl.ANY)]*count,
        out_specs=[pl.BlockSpec(memory_space=pltpu.VMEM)]*count,
        out_shape=[jax.ShapeDtypeStruct((2,a.shape[1],a.shape[2]//2),f32) for a in arrays],
        scratch_shapes=reduce_scratch([a.shape[1:] for a in arrays],shards,reps),
        compiler_params=pltpu.CompilerParams(collective_id=collective_id,has_side_effects=True,vmem_limit_bytes=50<<20),
        name="reduce_grads")(*arrays)

GATHER_PLAN = {
    0: (("u", 0), ("d", 0)),
    2: (("u", 1),),
    3: (("d", 1), ("u", 2)),
    4: (("d", 2),),
    5: (("u", 3), ("u", 4)),
    6: (("d", 3), ("d", 4)),
    8: (("u", 5), ("u", 6)),
    9: (("d", 5), ("d", 6)),
    11: (("u", 7),),
    100: (("d", 7), ("u", 8), ("d", 8)),
}


def low_lanes():
    return lax.broadcasted_iota(jnp.int32, (LEN, CLUSTER), 1) < DH


def table_of(order_row):
    positions = lax.broadcasted_iota(jnp.int32, (LEN, LEN), 0)
    return jnp.where(jnp.broadcast_to(order_row, (LEN, LEN)) == positions, 1.0, 0.0).astype(bf)


def half_roll(source):
    return pltpu.roll(source.astype(f32), DH, 1).astype(bf)


def softmax_rows(scores):
    top = jnp.max(scores, axis=-1, keepdims=True)
    grown = jnp.exp(scores - top)
    return grown * (1.0 / jnp.sum(grown, axis=-1, keepdims=True))


def attention_forward_body(
    shards, reps, len_ref, x_ref, wq_ref, wk_ref, wv_ref, bq_ref, bk_ref, bv_ref, row_ref, *rest
):
    ins, (att_ref, proj_ref), outs = rest[:3], rest[3:5], rest[5:8]
    tables, scores, mixed = rest[8:10], rest[10:12], rest[12:14]
    sems = rest[14:]
    step = pl.program_id(0) * PAIRS + pl.program_id(1)
    place = Place(shards, reps)
    up, down = [
        Gather(place, [ins[a] for a in which], [outs[a] for a in which], sems[7 * k : 7 * k + 7])
        for k, which in enumerate(((0,), (1, 2)))
    ]
    u, d = up.steps(), down.steps()
    plan = GATHER_PLAN

    def run(at):
        for name, k in plan.get(at, ()):
            (u if name == "u" else d)[k]()

    def first():
        meet(place, False)
        run(0)

    pl.when(step == 0)(first)
    for at in sorted(plan):
        if 0 < at < 100:
            pl.when(step == at)(partial(run, at))

    count = len_ref[pl.program_id(0)]
    weight = jnp.concatenate([wq_ref[...], wk_ref[...], wv_ref[...]], axis=1)
    bias = jnp.concatenate([bq_ref[...], bk_ref[...], bv_ref[...]], axis=1)
    proj = (dot_nn(x_ref[...], weight) + bias).astype(bf)
    low = low_lanes()
    query, key, value = proj[:, 0:128], proj[:, 128:256], proj[:, 256:384]
    pairs = [jnp.where(low, query, half_roll(key)), jnp.where(low, half_roll(query), key)]
    proj_ref[...] = jnp.concatenate([pairs[0], value, pairs[1]], axis=1)
    rows = [row_ref[0, 0, e : e + 1, :] for e in range(2)]
    for e in range(2):
        tables[e][...] = table_of(rows[e])
    picked = [
        dot_tn(tables[e][...], jnp.concatenate([pairs[e], value], axis=1)).astype(bf)
        for e in range(2)
    ]
    for e in range(2):
        qk = picked[e][:, 0:128]
        key_low = jnp.where(low, half_roll(qk), jnp.zeros((), bf))
        bias = jnp.where(rows[e] < count, 0.0, -30000.0)
        for sl in SLICES:
            scores[e][sl, :] = 0.125 * dot_nt(qk[sl], key_low[sl]) + bias[:, sl]
    for e in range(2):
        values = picked[e][:, 128:256]
        for sl in SLICES:
            probs = softmax_rows(scores[e][sl, :]).astype(bf)
            mixed[e][sl, :] = dot_nn(probs, values[sl]).astype(bf)
    placed = [dot_nn(tables[e][...], mixed[e][...]) for e in range(2)]
    att_ref[...] = jnp.where(low, placed[0], placed[1]).astype(bf)
    pl.when(step == pl.num_programs(0) * PAIRS - 1)(partial(run, 100))


def attention_forward(lengths, rounded, weight, bias, rows, arrays, shards, reps, collective_id):
    seqs = rows.shape[0]
    tokens = seqs * LEN
    column = lambda part: pl.BlockSpec((D, 128), lambda s, h, n: (0, part * PAIRS + h))
    column_b = lambda part: pl.BlockSpec((1, 128), lambda s, h, n: (0, part * PAIRS + h))
    return pl.pallas_call(
        partial(attention_forward_body, shards, reps),
        grid_spec=pltpu.PrefetchScalarGridSpec(
            num_scalar_prefetch=1,
            grid=(seqs, PAIRS),
            in_specs=[pl.BlockSpec((LEN, D), lambda s, h, n: (s, 0))]
            + [column(part) for part in range(3)]
            + [column_b(part) for part in range(3)]
            + [pl.BlockSpec((1, 1, 2, LEN), lambda s, h, n: (s, h, 0, 0))]
            + [pl.BlockSpec(memory_space=pltpu.VMEM)] * 3,
            out_specs=[
                pl.BlockSpec((LEN, 128), lambda s, h, n: (s, h)),
                pl.BlockSpec((LEN, 384), lambda s, h, n: (s, h)),
            ]
            + [pl.BlockSpec(memory_space=pl.ANY)] * 3,
            scratch_shapes=[pltpu.VMEM((LEN, LEN), bf)] * 2
            + [pltpu.VMEM((LEN, 128), f32)] * 2
            + [pltpu.VMEM((LEN, 128), bf)] * 2
            + gather_semaphores(1, shards)
            + gather_semaphores(2, shards),
        ),
        out_shape=[
            jax.ShapeDtypeStruct((tokens, D), bf),
            jax.ShapeDtypeStruct((tokens, 3 * D), bf),
        ]
        + [jax.ShapeDtypeStruct((shards,) + a.shape, bf) for a in arrays],
        compiler_params=pltpu.CompilerParams(
            vmem_limit_bytes=50 << 20, collective_id=collective_id, has_side_effects=True
        ),
        name="attention_forward",
    )(lengths, rounded, weight, weight, weight, bias, bias, bias, rows, *arrays)


def attention_backward_body(
    len_ref,
    x_ref,
    proj_ref,
    datt_ref,
    row_ref,
    dq_ref,
    dk_ref,
    dv_ref,
    dw_ref,
    db_ref,
    t0,
    t1,
    s0,
    s1,
    d0,
    d1,
    p0,
    p1,
    e0,
    e1,
    total,
):
    seq = pl.program_id(1)
    count = len_ref[seq]
    low = low_lanes()
    zero = jnp.zeros((), bf)
    tables, scores, back_probs, probs_low, backs = (t0, t1), (s0, s1), (d0, d1), (p0, p1), (e0, e1)
    rows = [row_ref[0, 0, e : e + 1, :] for e in range(2)]
    for e in range(2):
        tables[e][...] = table_of(rows[e])
    datt = datt_ref[...]
    swapped = half_roll(proj_ref[:, 128:256])
    middle = [jnp.where(low, datt, swapped), jnp.where(low, swapped, datt)]
    sources = [
        jnp.concatenate([proj_ref[:, 256 * e : 256 * e + 128], middle[e]], axis=1)
        for e in range(2)
    ]
    picked = [dot_tn(tables[e][...], sources[e]).astype(bf) for e in range(2)]
    for e in range(2):
        qk, dv = picked[e][:, 0:128], picked[e][:, 128:256]
        key_low = jnp.where(low, half_roll(qk), zero)
        turned = half_roll(dv)
        value_only = jnp.where(low, turned, zero) if e == 0 else jnp.where(low, zero, turned)
        bias = jnp.where(rows[e] < count, 0.0, -30000.0)
        for sl in SLICES:
            scores[e][sl, :] = 0.125 * dot_nt(qk[sl], key_low[sl]) + bias[:, sl]
            back_probs[e][sl, :] = dot_nt(dv[sl], value_only[sl])
    for e in range(2):
        for sl in SLICES:
            probs = softmax_rows(scores[e][sl, :])
            back = back_probs[e][sl, :]
            probs_low[e][sl, :] = probs.astype(bf)
            inner = jnp.sum(back * probs, axis=-1, keepdims=True)
            backs[e][sl, :] = (0.125 * (probs * (back - inner))).astype(bf)
    placed = []
    for e in range(2):
        qk, dv = picked[e][:, 0:128], picked[e][:, 128:256]
        queries, keys, values = [], [], []
        for sl in SLICES:
            back = backs[e][sl, :]
            queries.append(dot_nn(back, qk[sl]))
            keys.append(dot_tn(back, qk[sl]))
            values.append(dot_tn(probs_low[e][sl, :], dv[sl]))
        key_query = jnp.where(low, jnp.concatenate(keys, 0), jnp.concatenate(queries, 0))
        value = jnp.concatenate(values, 0)
        db_ref[0, 0, e : e + 1, :] = jnp.sum(key_query, axis=0, keepdims=True)
        db_ref[0, 0, 2 + e : 3 + e, :] = jnp.sum(value, axis=0, keepdims=True)
        parts = [key_query.astype(bf), value.astype(bf)]
        placed.append(
            dot_nn(tables[e][...], jnp.concatenate(parts, axis=1))
        )
    key_queries = [placed[e][:, 0:128] for e in range(2)]
    turned = [pltpu.roll(t, DH, 1) for t in key_queries]
    query = jnp.where(low, turned[0], key_queries[1]).astype(bf)
    key = jnp.where(low, key_queries[0], turned[1]).astype(bf)
    value = jnp.where(low, placed[0][:, 128:256], placed[1][:, 128:256]).astype(bf)
    dq_ref[...] = query
    dk_ref[...] = key
    dv_ref[...] = value
    out = jnp.concatenate([query, key, value], axis=1)
    part = dot_tn(x_ref[...], out)

    @pl.when(seq == 0)
    def _():
        total[...] = part

    @pl.when(seq != 0)
    def _():
        total[...] += part

    dw_ref[0] = total[...].astype(bf)


def pair_at(i):
    return (i % 2) * (PAIRS // 2) + i // 2


def attention_backward(lengths, rounded, proj, datt, rows):
    seqs = rows.shape[0]
    tokens = seqs * LEN
    own = lambda width: pl.BlockSpec((LEN, width), lambda i, s, n: (s, pair_at(i)))
    return pl.pallas_call(
        attention_backward_body,
        grid_spec=pltpu.PrefetchScalarGridSpec(
            num_scalar_prefetch=1,
            grid=(PAIRS, seqs),
            in_specs=[
                pl.BlockSpec((LEN, D), lambda i, s, n: (s, 0)),
                own(384),
                own(128),
                pl.BlockSpec((1, 1, 2, LEN), lambda i, s, n: (s, pair_at(i), 0, 0)),
            ],
            out_specs=[own(128)] * 3
            + [
                pl.BlockSpec((1, D, 384), lambda i, s, n: (i // 2, 0, i % 2)),
                pl.BlockSpec((1, 1, 4, 128), lambda i, s, n: (s, pair_at(i), 0, 0)),
            ],
            scratch_shapes=[pltpu.VMEM((LEN, LEN), bf)] * 2
            + [pltpu.VMEM((LEN, 128), f32)] * 4
            + [pltpu.VMEM((LEN, 128), bf)] * 4
            + [pltpu.VMEM((D, 384), f32)],
        ),
        out_shape=[jax.ShapeDtypeStruct((tokens, D), bf)] * 3
        + [
            jax.ShapeDtypeStruct((PAIRS // 2, D, D), bf),
            jax.ShapeDtypeStruct((seqs, PAIRS, 4, 128), f32),
        ],
        compiler_params=pltpu.CompilerParams(vmem_limit_bytes=50 << 20),
        cost_estimate=pl.CostEstimate(
            flops=70_000_000_000, bytes_accessed=30_000_000, transcendentals=0
        ),
        name="attention_backward",
    )(lengths, rounded, proj, datt, rows)


def norm_stats(x):
    c=jnp.mean(x,axis=-1,keepdims=True)
    xc=x-c
    r=lax.rsqrt(jnp.mean(xc*xc,axis=-1,keepdims=True)+eps_norm)
    return xc*r,r

def norm_back(up,normed,r,gain):
    g=up*gain
    return r*(g-jnp.mean(g,axis=-1,keepdims=True)-normed*jnp.mean(g*normed,axis=-1,keepdims=True))

def colsum(x): return jnp.sum(x,axis=0,keepdims=True)

def gelu_parts(u):
    cdf=0.5+0.5*lax.erf(u*0.7071067811865476)
    pdf=jnp.exp(-0.5*u*u)*0.3989422804014327
    return u*cdf,cdf+u*pdf

def middle_body(len_ref,h_ref,a_ref,ct_ref,ow_ref,uw_ref,dw_ref,vec_ref,ub_ref,
               out_ref,bs_ref,ba_ref,act,pl_,low_ref,d2_ref,sl_ref,small_ref,ubg_ref,
               gp,n1_ref,*,T,sub_rows,chunk):
    i=pl.program_id(0)
    per=LEN//T
    count=len_ref[i//per]
    @pl.when(i==0)
    def _():
        small_ref[...]=jnp.zeros_like(small_ref); ubg_ref[...]=jnp.zeros_like(ubg_ref)
    out_b,g1,b1,down_b,g2,b2=[vec_ref[j:j+1,:] for j in range(6)]
    parts=[slice(k,k+sub_rows) for k in range(0,T,sub_rows)]
    r1s=[];sums=[]
    xs=[dot_nn(a_ref[p,:],ow_ref[...]) for p in parts]
    for p,x in zip(parts,xs):
        n1,r1=norm_stats(h_ref[p,:]+x+out_b)
        n1_ref[p,:]=n1; r1s.append(r1)
        low_ref[p,:]=(n1*g1+b1).astype(bf)
    for j in range(0,FF,chunk):
        sl=slice(j,j+chunk)
        for p in parts:
            u=dot_nn(low_ref[p,:],uw_ref[:,sl])+ub_ref[:,sl]
            a,g=gelu_parts(u)
            act[p,sl]=a.astype(bf); gp[p,sl]=g.astype(gp.dtype)
    ys=[dot_nn(act[p,:],dw_ref[...]) for p in parts]
    for p,y in zip(parts,ys):
        pos=lax.broadcasted_iota(jnp.int32,(sub_rows,1),0)+(i%per)*T+p.start
        valid=jnp.where(pos<count,1.0,0.0)
        second=n1_ref[p,:]*g1+b1+y+down_b
        n2,r2=norm_stats(second)
        out_ref[p,:]=valid*(n2*g2+b2)
        up=valid*ct_ref[p,:]
        b2nd=norm_back(up,n2,r2,g2)
        d2_ref[p,:]=b2nd.astype(bf)
        bs_ref[p,:]=b2nd
        sums.append(jnp.concatenate([colsum(b2nd),colsum(up*n2),colsum(up)],axis=0))
    small_ref[3:6,:]+=sum(sums[1:],sums[0])
    for j in range(0,FF,chunk):
        sl=slice(j,j+chunk)
        cs=[]
        for p in parts:
            bp=dot_nt(d2_ref[p,:],dw_ref[sl,:])*gp[p,sl].astype(f32)
            cs.append(colsum(bp))
            pl_[p,sl]=bp.astype(bf)
        ubg_ref[:,sl]+=sum(cs[1:],cs[0])
    zs=[dot_nt(pl_[p,:],uw_ref[...]) for p in parts]
    sums=[]
    for p,z,r1 in zip(parts,zs,r1s):
        bfirst=z+bs_ref[p,:]
        n1=n1_ref[p,:]
        bsum=norm_back(bfirst,n1,r1,g1)
        bs_ref[p,:]=bsum
        sl_ref[p,:]=bsum.astype(bf)
        sums.append(jnp.concatenate([colsum(bsum),colsum(bfirst*n1),colsum(bfirst)],axis=0))
    small_ref[0:3,:]+=sum(sums[1:],sums[0])
    for p in parts:
        ba_ref[p,:]=dot_nt(sl_ref[p,:],ow_ref[...]).astype(bf)

def middle(lengths,hidden,att,ct,ow,uw,dw,vec,ub,T=512,chunk=768,gpt=f32,sub_rows=256):
    tokens=hidden.shape[0]
    tile=lambda n=D: pl.BlockSpec((T,n),lambda i,l:(i,0))
    const=lambda shape: pl.BlockSpec(shape,lambda i,l:(0,0),pipeline_mode=pl.Buffered(1))
    whole=lambda shape: pl.BlockSpec(shape,lambda i,l:(0,0))
    sd=lambda n,dt: jax.ShapeDtypeStruct((tokens,n),dt)
    return pl.pallas_call(
        partial(middle_body,T=T,chunk=chunk,sub_rows=sub_rows),
        grid_spec=pltpu.PrefetchScalarGridSpec(num_scalar_prefetch=1,grid=(tokens//T,),
          in_specs=[tile(),tile(),tile(),const((D,D)),const((D,FF)),const((FF,D)),whole((8,D)),whole((1,FF))],
          out_specs=[tile(),tile(),tile(),tile(FF),tile(FF),tile(),tile(),tile(),whole((8,D)),whole((1,FF))],
          scratch_shapes=[pltpu.VMEM((T,FF),gpt),pltpu.VMEM((T,D),f32)]),
        out_shape=[sd(D,f32),sd(D,f32),sd(D,bf),sd(FF,bf),sd(FF,bf),sd(D,bf),sd(D,bf),sd(D,bf),jax.ShapeDtypeStruct((8,D),f32),jax.ShapeDtypeStruct((1,FF),f32)],
        compiler_params=pltpu.CompilerParams(vmem_limit_bytes=63<<20),
        name="middle")(lengths,hidden,att,ct,ow,uw,dw,vec,ub)


def weight_grad_body(l_ref,r_ref,out_ref):
    out_ref[...]=dot_tn(l_ref[...],r_ref[...]).astype(bf)
def weight_grad(left,right,block,name,columns=False):
    K,M=left.shape; N=right.shape[1]
    if columns:
        grid,lb,rb,ob,li,ri,oi=(N//block,),(K,M),(K,block),(M,block),(lambda i:(0,0)),(lambda i:(0,i)),(lambda i:(0,i))
    else:
        grid,lb,rb,ob,li,ri,oi=(M//block,),(K,block),(K,N),(block,N),(lambda i:(0,i)),(lambda i:(0,0)),(lambda i:(i,0))
    return pl.pallas_call(weight_grad_body,grid=grid,
        in_specs=[pl.BlockSpec(lb,li),pl.BlockSpec(rb,ri)],out_specs=pl.BlockSpec(ob,oi),
        out_shape=jax.ShapeDtypeStruct((M,N),bf),
        cost_estimate=pl.CostEstimate(flops=2*K*M*N,bytes_accessed=2*(K*M+K*N+M*N),transcendentals=0),
        compiler_params=pltpu.CompilerParams(vmem_limit_bytes=60<<20),name=name)(left,right)


def input_grad_body(bs_ref,dq_ref,dk_ref,dv_ref,w_ref,out_ref):
    out_ref[...]=bs_ref[...]+dot_nt(dq_ref[...],w_ref[:,0:D])+dot_nt(dk_ref[...],w_ref[:,D:2*D])+dot_nt(dv_ref[...],w_ref[:,2*D:3*D])
def input_grad(back_sum,dq,dk,dv,weight,rows=512):
    tile=pl.BlockSpec((rows,D),lambda i:(i,0))
    return pl.pallas_call(input_grad_body,grid=(back_sum.shape[0]//rows,),
        in_specs=[tile]*4+[pl.BlockSpec((D,3*D),lambda i:(0,0),pipeline_mode=pl.Buffered(1))],out_specs=tile,
        out_shape=jax.ShapeDtypeStruct(back_sum.shape,f32),
        compiler_params=pltpu.CompilerParams(vmem_limit_bytes=50<<20),name="input_grad")(back_sum,dq,dk,dv,weight)


WIDE = 4096


def shard_vectors(vectors):
    row = jnp.concatenate(vectors)
    return jnp.pad(row, (0, WIDE - row.shape[0])).reshape(16, 256)


def local(
    hidden,
    lengths,
    clusters,
    input_weight,
    query_bias,
    value_bias,
    out_weight,
    out_bias,
    norm1_gain,
    norm1_bias,
    up_weight,
    up_bias,
    down_weight,
    down_bias,
    norm2_gain,
    norm2_bias,
    cotangent,
    *,
    shards,
    reps,
):
    seqs = hidden.shape[0]
    tokens = seqs * LEN
    part = D // shards
    vectors = shard_vectors(
        (
            query_bias,
            value_bias,
            out_bias,
            norm1_gain,
            norm1_bias,
            down_bias,
            norm2_gain,
            norm2_bias,
            up_bias,
        )
    )
    in_w, vectors = gather_now((input_weight, vectors), shards, reps, 1)
    in_w = in_w.reshape(D, 3 * D)
    vectors = vectors.reshape(shards, WIDE).astype(f32)
    table = vectors[:, : 8 * part].reshape(shards, 8, part).transpose(1, 0, 2).reshape(8, D)
    bias_all = jnp.concatenate([table[0], jnp.zeros((D,), f32), table[1]])[None]
    norm_rows = jnp.concatenate([table[2:], table[:2]])
    up_b = vectors[:, 8 * part : 8 * part + FF // shards].reshape(1, FF)

    flat = hidden.reshape(tokens, D)
    rounded = flat.astype(bf)
    rows = clusters.reshape(seqs, PAIRS, 2, LEN)
    attended, proj, up_w, down_w, out_w = attention_forward(
        lengths,
        rounded,
        in_w,
        bias_all,
        rows,
        (up_weight, down_weight, out_weight),
        shards,
        reps,
        2,
    )
    out_w, up_w, down_w = [w.reshape(-1, w.shape[-1]) for w in (out_w, up_w, down_w)]
    (
        result,
        back_sum,
        back_attended,
        activated,
        pre_low,
        first_low,
        second_low,
        sum_low,
        norm_sums,
        up_b_sum,
    ) = middle(
        lengths,
        flat,
        attended,
        cotangent.reshape(tokens, D),
        out_w,
        up_w,
        down_w,
        norm_rows,
        up_b,
    )
    down_g = weight_grad(activated, second_low, D, "down_weight_grad")
    up_g = weight_grad(first_low, pre_low, D, "up_weight_grad", True)
    out_g = weight_grad(attended, sum_low, D // 2, "out_weight_grad")
    dq, dk, dv, in_g, bias_sums = attention_backward(lengths, rounded, proj, back_attended, rows)
    down_s, up_s, out_s = reduce_now(
        [g.reshape(shards, -1, g.shape[-1]) for g in (down_g, up_g, out_g)], shards, reps, 3
    )
    bias_sums = jnp.sum(bias_sums, axis=0)
    query_sum = bias_sums[:, 0:2, DH:].reshape(D)
    value_sum = jnp.concatenate([bias_sums[:, 2, :DH], bias_sums[:, 3, DH:]], axis=1).reshape(D)
    table = jnp.concatenate([query_sum[None], value_sum[None], norm_sums[:6]])
    small = jnp.concatenate(
        [
            table.reshape(8, shards, part).transpose(1, 0, 2).reshape(shards, 8 * part),
            up_b_sum.reshape(shards, FF // shards),
        ],
        axis=1,
    ).astype(bf)
    small = jnp.pad(small, ((0, 0), (0, WIDE - small.shape[1]))).reshape(shards, 16, 256)
    *in_s, small_s = reduce_now(
        [in_g[g].reshape(shards, part, D) for g in range(PAIRS // 2)] + [small], shards, reps, 4
    )
    back_input = input_grad(back_sum, dq, dk, dv, in_w).reshape(seqs, LEN, D)
    in_s = jnp.concatenate(
        [
            in_s[g][c, :, 128 * t : 128 * t + 128]
            for t in range(3)
            for c in range(2)
            for g in range(PAIRS // 2)
        ],
        axis=1,
    )

    def whole(halves):
        return jnp.concatenate([halves[0], halves[1]], axis=1)

    small_s = whole(small_s).reshape(WIDE)
    vec = [small_s[i * part : (i + 1) * part] for i in range(8)]
    return (
        result.reshape(seqs, LEN, D),
        back_input,
        in_s,
        vec[0],
        vec[1],
        whole(out_s),
        vec[2],
        vec[3],
        vec[4],
        whole(up_s),
        small_s[8 * part : 8 * part + FF // shards],
        whole(down_s),
        vec[5],
        vec[6],
        vec[7],
    )


def solution(mesh):
    tokens = P(("rep", "shard"), None, None)
    matrix, vector = P("shard", None), P("shard")
    params = (
        matrix,
        vector,
        vector,
        matrix,
        vector,
        vector,
        vector,
        matrix,
        vector,
        matrix,
        vector,
        vector,
        vector,
    )
    return jax.shard_map(
        partial(local, shards=mesh.shape["shard"], reps=mesh.shape["rep"]),
        mesh=mesh,
        in_specs=(tokens, P(("rep", "shard")), tokens) + params + (tokens,),
        out_specs=(tokens, tokens) + params,
        check_vma=False,
    )
```

time: 549 us -> 501 us (0.913)
  Pallas kernels: 498 us -> 468 us
  matrix products: 11.7 us -> 0 us
  local copies, waits for them, and re-layouts: 22.6 us -> 16.3 us
    pallas_call x2 -> x1, Pallas kernels: 92.8 us -> 25.5 us  [gather_now(): pl.pallas_call(partial(gather_body, shards, reps, count), in_specs=[pl.Bl...]
    pallas_call x1 -> x2, Pallas kernels: 59.2 us -> 92.5 us  [the longest x1 79.5 us: attention_forward(): pl.pallas_call(partial(attention_forward_body, shards, reps), grid_spec=p...]
    dot_general x1 -> x0, matrix products: 11.7 us -> none  [dot_nt(): lax.dot_general(left, right, (((1,), (1,)), ((), ())), preferred_element_...]
    unnamed x50 -> x47, local copies, waits for them, and re-layouts: 12.2 us -> 3.72 us
where the time goes in v3:
time: 501 us; the launch traced here: 495 us
  Pallas kernels  468 us (93%)
  local copies, waits for them, and re-layouts  16.3 us (3%)
  other arithmetic  8.6 us (2%)
    pallas_call x2, Pallas kernels, reduce_now(): pl.pallas_call(partial(reduce_body, shards, reps, count), in_specs=[pl.Bl...  158 us
    pallas_call x1, Pallas kernels, attention_backward(): pl.pallas_call(attention_backward_body, grid_spec=pltpu.PrefetchScalarGri...  94.6 us
    pallas_call x1, Pallas kernels, attention_forward(): pl.pallas_call(partial(attention_forward_body, shards, reps), grid_spec=p...  79.5 us
    pallas_call x1, Pallas kernels, middle(): pl.pallas_call(partial(middle_body, T=T, chunk=chunk, sub_rows=sub_rows),...  62.1 us
    pallas_call x3, Pallas kernels, weight_grad(): pl.pallas_call(weight_grad_body, grid=grid, in_specs=[pl.BlockSpec(lb, li...  35.6 us
    pallas_call x1, Pallas kernels, gather_now(): pl.pallas_call(partial(gather_body, shards, reps, count), in_specs=[pl.Bl...  25.5 us
    pallas_call x1, Pallas kernels, input_grad(): pl.pallas_call(input_grad_body, grid=(back_sum.shape[0] // rows,), in_spe...  13 us

profile of v3, /device:TPU:9, one launch (start us, length us, event | category | flops | bytes accessed | tf_op | source)
XLA Modules:
  0.0 494.8 jit_solution(13752268562155415824)
XLA Ops:
  0.7 6.1 %concatenate.43 = bf16[1152]{0:T(1024)(128)(2,1)S(1)} concatenate(bf16[96]{0:T(256)(128)(2,1)} %param.21, bf16[96]{0:T(256)(128)(2,1)} %param.22, bf16[96]{0:T(256)(128)(2,1)} %param.24, bf16[96]{0:T(256)(128)(2,1)} %param.25, bf16[96]{0:T(256)(128)(2,1)} %param.26, bf16[96]{0:T(256)(128)(2,1)} %param.30, bf16[96]{0:T(256)(128)(2,1)} %param.31, bf16[96]{0:T(256)(128)(2,1)} %param.32, ...), dimensions={0} | concatenate | bytes 4608 | tf_op jit(solution)/shard_map/concatenate | solution.py:694
  6.8 0.9 copy.51.row_ref
  7.7 0.0 copy-start.5
  7.7 0.0 copy-start.3
  7.8 0.0 copy-start.4
  7.8 0.0 copy-start.6
  7.8 0.0 copy-start.7
  7.8 4.9 bitcast_convert_fusion.x_ref
  12.7 0.0 copy-done.5
  12.7 25.5 %gather_weights.1 = (bf16[8,96,2304]{2,1,0:T(8,128)(2,1)S(1)}, bf16[8,16,256]{2,1,0:T(8,128)(2,1)S(1)}) custom-call(bf16[96,2304]{1,0:T(8,128)(2,1)S(1)} %copy-done.5, bf16[16,256]{1,0:T(8,128)(2,1)S(1)} %reshape.109.refs_1_), custom_call_target="tpu_custom_call" | custom-call | tf_op jit(solution)/shard_map/gather_weights/pallas_call | solution.py:163
  38.2 0.0 copy-start
  38.2 1.8 copy-done
  40.0 0.1 copy.56
  40.2 0.6 copy.57
  40.8 0.1 reshape.111
  40.9 0.1 slice.162
  41.0 0.1 slice.160
  41.0 0.6 pad_maximum_fusion.3.vec_ref
  41.7 0.1 squeeze.92
  41.7 0.1 squeeze.93
  41.8 0.0 copy-done.3
  41.8 0.0 copy-done.4
  41.9 0.0 copy-done.6
  41.9 0.0 copy-done.7
  41.9 79.5 %attention_forward.1 = (bf16[2048,768]{1,0:T(8,128)(2,1)}, bf16[2048,2304]{1,0:T(8,128)(2,1)}, bf16[8,96,3072]{2,1,0:T(8,128)(2,1)}, bf16[8,384,768]{2,1,0:T(8,128)(2,1)}, bf16[8,96,768]{2,1,0:T(8,128)(2,1)S(1)}) custom-call(s32[2]{0:T(128)S(1)} %copy-done.7, bf16[2048,768]{1,0:T(8,128)(2,1)} %bitcast_convert_fusion.x_ref, bf16[768,2304]{1,0:T(8,128)(2,1)} %bitcast.91, ...), custom_call_target="tpu_custom_call" | custom-call | tf_op jit(solution)/shard_map/attention_forward/pallas_call | solution.py:405
  121.4 0.0 copy-start.1
  121.4 1.0 copy-done.1
  122.4 62.1 %middle.1 = (f32[2048,768]{1,0:T(8,128)}, f32[2048,768]{1,0:T(8,128)}, bf16[2048,768]{1,0:T(8,128)(2,1)}, bf16[2048,3072]{1,0:T(8,128)(2,1)}, bf16[2048,3072]{1,...) custom-call(s32[2]{0:T(128)} %len_ref.5, ...), custom_call_target="tpu_custom_call" | custom-call | tf_op jit(solution)/shard_map/middle/pallas_call | solution.py:654
  184.6 0.0 copy-start.9
  184.6 0.0 copy-start.10
  184.6 0.0 copy-start.8
  184.6 6.1 %out_weight_grad.1 = bf16[768,768]{1,0:T(8,128)(2,1)} custom-call(bf16[2048,768]{1,0:T(8,128)(2,1)} %get-tuple-element.46.a_ref.l_ref, bf16[2048,768]{1,0:T(8,128)(2,1)} %get-tuple-element.69.r_ref), custom_call_target="tpu_custom_call" | custom-call | flops 2415919104 | bytes 7471104 | tf_op jit(solution)/shard_map/out_weight_grad/pallas_call | solution.py:673
  190.7 0.0 copy-done.9
  190.7 0.0 copy-done.10
  190.8 0.1 concatenate.49
  190.8 0.0 copy-done.8
  190.9 94.6 %attention_backward.1 = (bf16[2048,768]{1,0:T(8,128)(2,1)S(1)}, bf16[2048,768]{1,0:T(8,128)(2,1)}, bf16[2048,768]{1,0:T(8,128)(2,1)}, bf16[3,768,768]{2,1,0:T(8,128)(2,1)}, f32[2,6,4,128]{3,2,1,0:T(4,128)S(1)}) custom-call(s32[2]{0:T(128)S(1)} %copy-done.8, bf16[2048,768]{1,0:T(8,128)(2,1)} %bitcast_convert_fusion.x_ref, ...), custom_call_target="tpu_custom_call" | custom-call | flops 70000001024 | bytes 30000000 | tf_op jit(solution)/shard_map/attention_backward/pallas_call | solution.py:540
  285.5 13.0 %input_grad.1 = f32[2048,768]{1,0:T(8,128)} custom-call(f32[2048,768]{1,0:T(8,128)} %get-tuple-element.51.bs_ref, bf16[2048,768]{1,0:T(8,128)(2,1)S(1)} %get-tuple-element.54.dq_ref, bf16[2048,768]{1,0:T(8,128)(2,1)} %get-tuple-element.55.dk_ref, bf16[2048,768]{1,0:T(8,128)(2,1)} %get-tuple-element.56.dv_ref, bf16[768,2304]{1,0:T(8,128)(2,1)} %bitcast.94), custom_call_target="tpu_custom_call" | custom-call | tf_op jit(solution)/shard_map/input_grad/pallas_call | solution.py:684
  298.5 0.1 slice.212
  298.6 0.1 concatenate.46
  298.7 0.1 fusion.6
  298.8 0.1 pad_maximum_fusion.5
  298.8 0.1 concatenate.48
  298.9 0.1 reshape.120
  299.1 3.2 fusion.3
  302.3 48.3 %reduce_grads.2 = (f32[2,96,384]{2,1,0:T(8,128)S(1)}, f32[2,96,384]{2,1,0:T(8,128)S(1)}, f32[2,96,384]{2,1,0:T(8,128)S(1)}, f32[2,16,128]{2,1,0:T(8,128)S(1)}) custom-call(bf16[8,96,768]{2,1,0:T(8,128)(2,1)S(1)} %bitcast.96, bf16[8,96,768]{2,1,0:T(8,128)(2,1)S(1)} %bitcast.95, bf16[8,96,768]{2,1,0:T(8,128)(2,1)} %bitcast.105, bf16[8,16,256]{2,1,0:T(8,128)(2,1)S(1)} %bitcast.99), custom_call_target="tpu_custom_call" | custom-call | tf_op jit(solution)/shard_map/reduce_grads/pallas_call | solution.py:300
  350.7 0.6 slice.221
  351.2 0.6 fusion.5
  352.1 0.0 copy-start.11
  352.1 14.9 %down_weight_grad.1 = bf16[3072,768]{1,0:T(8,128)(2,1)} custom-call(bf16[2048,3072]{1,0:T(8,128)(2,1)} %get-tuple-element.65.l_ref, bf16[2048,768]{1,0:T(8,128)(2,1)} %get-tuple-element.66.r_ref), custom_call_target="tpu_custom_call" | custom-call | flops 9663676416 | bytes 20447232 | tf_op jit(solution)/shard_map/down_weight_grad/pallas_call | solution.py:673
  367.0 0.0 copy-done.11
  367.0 0.0 copy-start.2
  367.0 14.7 %up_weight_grad.1 = bf16[768,3072]{1,0:T(8,128)(2,1)} custom-call(bf16[2048,768]{1,0:T(8,128)(2,1)} %get-tuple-element.67.l_ref, bf16[2048,3072]{1,0:T(8,128)(2,1)} %get-tuple-element.68.r_ref), custom_call_target="tpu_custom_call" | custom-call | flops 9663676416 | bytes 20447232 | tf_op jit(solution)/shard_map/up_weight_grad/pallas_call | solution.py:673
  381.7 0.0 copy-done.2
  381.7 109.5 %reduce_grads.3 = (f32[2,384,384]{2,1,0:T(8,128)S(1)}, f32[2,96,1536]{2,1,0:T(8,128)S(1)}, f32[2,96,384]{2,1,0:T(8,128)S(1)}) custom-call(bf16[8,384,768]{2,1,0:T(8,128)(2,1)} %bitcast.106, bf16[8,96,3072]{2,1,0:T(8,128)(2,1)} %bitcast.107, bf16[8,96,768]{2,1,0:T(8,128)(2,1)S(1)} %bitcast.98), custom_call_target="tpu_custom_call" | custom-call | tf_op jit(solution)/shard_map/reduce_grads/pallas_call | solution.py:300
  491.2 0.7 pad_maximum_fusion.2
  492.0 0.1 slice_bitcast_fusion.3
  492.0 1.1 pad_maximum_fusion
  493.1 0.1 slice_bitcast_fusion.1
  493.2 1.1 pad_maximum_fusion.1
  (43 shorter events, 0.4 us)
Async XLA Ops:
  7.7 4.9 copy-start.5
  7.7 34.1 %copy-start.3 = (bf16[96,3072]{1,0:T(8,128)(2,1)S(1)}, bf16[96,3072]{1,0:T(8,128)(2,1)}, u32[]{:S(2)}) copy-start(bf16[96,3072]{1,0:T(8,128)(2,1)} %rest_0_.1) | copy-start | bytes 1769476
  7.8 34.1 %copy-start.4 = (bf16[384,768]{1,0:T(8,128)(2,1)S(1)}, bf16[384,768]{1,0:T(8,128)(2,1)}, u32[]{:S(2)}) copy-start(bf16[384,768]{1,0:T(8,128)(2,1)} %rest_1_.1) | copy-start | bytes 1769476
  7.8 34.1 %copy-start.6 = (bf16[96,768]{1,0:T(8,128)(2,1)S(1)}, bf16[96,768]{1,0:T(8,128)(2,1)}, u32[]{:S(2)}) copy-start(bf16[96,768]{1,0:T(8,128)(2,1)} %rest_2_.1) | copy-start | bytes 442372
  7.8 34.1 %copy-start.7 = (s32[2]{0:T(128)S(1)}, s32[2]{0:T(128)}, u32[]{:S(2)}) copy-start(s32[2]{0:T(128)} %len_ref.5) | copy-start | bytes 28
  38.2 1.8 copy-start
  121.4 1.0 copy-start.1
  184.6 6.1 %copy-start.9 = (f32[1,3072]{1,0:T(1,128)S(1)}, f32[1,3072]{1,0:T(1,128)}, u32[]{:S(2)}) copy-start(f32[1,3072]{1,0:T(1,128)} %get-tuple-element.60) | copy-start | bytes 36868
  184.6 6.2 %copy-start.10 = (f32[8,768]{1,0:T(8,128)S(1)}, f32[8,768]{1,0:T(8,128)}, u32[]{:S(2)}) copy-start(f32[8,768]{1,0:T(8,128)} %get-tuple-element.59) | copy-start | bytes 73732
  184.6 6.3 %copy-start.8 = (s32[2]{0:T(128)S(1)}, s32[2]{0:T(128)}, u32[]{:S(2)}) copy-start(s32[2]{0:T(128)} %len_ref.5) | copy-start | bytes 28
  352.1 14.9 %copy-start.11 = (f32[96,2304]{1,0:T(8,128)}, f32[96,2304]{1,0:T(8,128)S(1)}, u32[]{:S(2)}) copy-start(f32[96,2304]{1,0:T(8,128)S(1)} %bitcast_dynamic-update-slice_fusion) | copy-start | bytes 2654212
  367.0 14.7 %copy-start.2 = (bf16[768,768]{1,0:T(8,128)(2,1)S(1)}, bf16[768,768]{1,0:T(8,128)(2,1)}, u32[]{:S(2)}) copy-start(bf16[768,768]{1,0:T(8,128)(2,1)} %out_weight_grad.1) | copy-start | bytes 3538948

commit v4 on v3

--- a/solution.py
+++ b/solution.py
@@ -149,14 +149,12 @@
         for make in self.sent:
             cond,desc=make()
             when(cond,desc.wait_send)
-    def steps(self):
-        return [self.begin,lambda: self.wave(1),lambda: self.across(0),lambda: self.wave(2),lambda: self.across(1),lambda: self.wave(3),lambda: self.across(2),lambda: self.across(3),self.finish]
-
 def gather_body(shards,reps,count,*refs):
     ins,outs,sems=refs[:count],refs[count:2*count],refs[2*count:]
     place=Place(shards,reps)
     meet(place,False)
-    for step in Gather(place,ins,outs,sems).steps(): step()
+    G=Gather(place,ins,outs,sems)
+    G.begin(); G.wave(1); G.across(0); G.wave(2); G.across(1); G.wave(3); G.across(2); G.across(3); G.finish()
 
 def gather_now(arrays,shards,reps,collective_id):
     count=len(arrays)
@@ -169,20 +167,20 @@
         name="gather_weights")(*arrays)
 
 ORDER=(3,0,2,1)
-def reduce_scratch(shapes,shards,reps,store=True):
+def reduce_scratch(shapes,shards,reps):
     S=shards; Y=S//ROWS; X=reps//2; A=len(shapes)
     out=[]
     for r,c in shapes:
         n=c//2
         out+=[pltpu.VMEM((S,r,n),bf),pltpu.VMEM((S,r,n),bf),pltpu.VMEM((max(Y-1,1),ROWS,r,n),bf),
-              pltpu.VMEM((2,ROWS,r,n),bf),pltpu.VMEM((X,r,n),bf)]
+              pltpu.VMEM((ROWS+1,r,n),bf),pltpu.VMEM((X,r,n),bf),pltpu.VMEM((2,r,n),f32)]
     dma=pltpu.SemaphoreType.DMA
-    return out+[dma((A,S)),dma((A,S)),dma((A,S)),dma((A,Y,ROWS)),dma((A,Y,ROWS)),dma((A,2,ROWS)),dma((A,2,ROWS)),dma((A,X)),dma((A,X)),dma((A,)),dma((A,))]
+    return out+[dma((A,S)),dma((A,S)),dma((A,S)),dma((A,Y,ROWS)),dma((A,Y,ROWS)),dma((A,ROWS+1)),dma((A,ROWS+1)),dma((A,X)),dma((A,X)),dma((A,)),dma((A,)),dma((A,))]
 class Reduce:
     def __init__(self,place,ins,outs,scratch):
         self.p=place; self.ins=ins; self.outs=outs; A=len(ins); self.A=range(A)
-        self.bufs=[scratch[5*a:5*a+5] for a in range(A)]
-        (self.own,self.core_s,self.core_r,self.y_s,self.y_r,self.line_s,self.line_r,self.x_s,self.x_r,self.end_s,self.end_r)=scratch[5*A:]
+        self.bufs=[scratch[6*a:6*a+6] for a in range(A)]
+        (self.own,self.core_s,self.core_r,self.y_s,self.y_r,self.line_s,self.line_r,self.x_s,self.x_r,self.end_s,self.end_r,self.out_s)=scratch[6*A:]
         self.sent=[]
     def copy(self,src,dst,ss,rs,dev):
         return pltpu.make_async_remote_copy(src_ref=src,dst_ref=dst,send_sem=ss,recv_sem=rs,device_id=dev,device_id_type=MESH)
@@ -193,22 +191,27 @@
         n=self.ins[a].shape[-1]//2
         return self.ins[a].at[shard,:,pl.ds(pl.multiple_of(core*n,128),n)]
     def add(self,dst,others):
-        rows=dst.shape[0]; step=48 if rows%48==0 else 16
-        def body(i,_):
-            at=pl.ds(pl.multiple_of(i*step,16),step)
+        rows,n=dst.shape; step=next(s for s in (96,48,16) if rows%s==0 and (s==16 or s*n<=96*512))
+        def block(at):
             value=dst[at,:].astype(f32)
             for o in others: value=value+o[at,:].astype(f32)
             dst[at,:]=value.astype(bf)
+        if rows==step: block(slice(0,rows)); return
+        def body(i,_):
+            block(pl.ds(pl.multiple_of(i*step,16),step))
             return 0
         lax.fori_loop(0,rows//step,body,0)
     def begin(self):
         p=self.p
         for k in list(range(1,p.Y))+[0]:
             for d in ORDER:
-                shard=d*p.Y+lax.rem(p.y+k,p.Y)
                 for a in self.A:
                     H,Rc=self.bufs[a][0:2]
-                    self.send(lambda a=a,Rc=Rc,shard=shard: (None,self.copy(self.half(a,shard,1-p.core),Rc.at[shard],self.core_s.at[a,shard],self.core_r.at[a,shard],p.other_core())))
+                    def make(a=a,d=d,k=k,Rc=Rc):
+                        shard=d*p.Y+lax.rem(p.y+k,p.Y)
+                        return None,self.copy(self.half(a,shard,1-p.core),Rc.at[shard],self.core_s.at[a,shard],self.core_r.at[a,shard],p.other_core())
+                    self.send(make)
+                    shard=d*p.Y+lax.rem(p.y+k,p.Y)
                     pltpu.make_async_copy(self.half(a,shard,p.core),H.at[shard],self.own.at[a,shard]).start()
     def join_core(self,shard):
         p=self.p
@@ -220,41 +223,53 @@
     def to_y(self,d):
         p=self.p
         for k in range(1,p.Y):
-            shard=d*p.Y+lax.rem(p.y+k,p.Y)
-            self.join_core(shard)
+            self.join_core(d*p.Y+lax.rem(p.y+k,p.Y))
             for a in self.A:
                 H,_,Ry=self.bufs[a][0:3]
-                self.send(lambda a=a,H=H,Ry=Ry,k=k,shard=shard: (None,self.copy(H.at[shard],Ry.at[k-1,d],self.y_s.at[a,k,d],self.y_r.at[a,k,d],p.other_y(k))))
+                def make(a=a,H=H,Ry=Ry,k=k):
+                    shard=d*p.Y+lax.rem(p.y+k,p.Y)
+                    return None,self.copy(H.at[shard],Ry.at[k-1,d],self.y_s.at[a,k,d],self.y_r.at[a,k,d],p.other_y(k))
+                self.send(make)
     def own_y(self,d):
         self.join_core(d*self.p.Y+self.p.y)
+    def along(self,d,up,j):
+        p=self.p
+        if (j>=d) if up else (ROWS-1-j<=d): return
+        here=p.z==(j if up else ROWS-1-j)
+        shard=d*p.Y+p.y
+        if j>0:
+            def add_in():
+                for a in self.A:
+                    H,Rl=self.bufs[a][0],self.bufs[a][3]
+                    self.copy(Rl.at[d],Rl.at[d],self.line_s.at[a,d],self.line_r.at[a,d],p.near_z(0)).wait_recv()
+                    self.add(H.at[shard],[Rl.at[d]])
+            pl.when(here)(add_in)
+        last=(j==d-1) if up else (ROWS-1-j==d+1)
+        slot=ROWS if last and not up else d
+        for a in self.A:
+            def make(a=a):
+                H,Rl=self.bufs[a][0],self.bufs[a][3]
+                return p.z==(j if up else ROWS-1-j),self.copy(H.at[d*p.Y+p.y],Rl.at[slot],self.line_s.at[a,slot],self.line_r.at[a,slot],p.near_z(1 if up else -1))
+            self.send(make)
     def line(self,d):
         p=self.p; shard=d*p.Y+p.y
         for a in self.A:
-            H,_,Ry,Rl=self.bufs[a][0:4]
+            H,_,Ry=self.bufs[a][0:3]
             for k in range(1,p.Y):
                 self.copy(Ry.at[k-1,d],Ry.at[k-1,d],self.y_s.at[a,k,d],self.y_r.at[a,k,d],p.other_y(k)).wait_recv()
             self.add(H.at[shard],[Ry.at[k-1,d] for k in range(1,p.Y)])
-        for up in (0,1):
-            passes=(p.z<d) if up==0 else (p.z>d)
-            inner=(p.z>0) if up==0 else (p.z<ROWS-1)
-            def add_in(up=up):
+        self.along(d,True,0); self.along(d,False,0)
+    def relay(self,d,j):
+        self.along(d,True,j); self.along(d,False,j)
+    def to_x(self):
+        p=self.p
+        for slot,cond in ((p.z,p.z>0),(ROWS,p.z<ROWS-1)):
+            def add_in(slot=slot):
                 for a in self.A:
                     H,Rl=self.bufs[a][0],self.bufs[a][3]
-                    self.copy(Rl.at[up,d],Rl.at[up,d],self.line_s.at[a,up,d],self.line_r.at[a,up,d],p.near_z(0)).wait_recv()
-                    self.add(H.at[shard],[Rl.at[up,d]])
-            pl.when(jnp.logical_and(passes,inner))(add_in)
-            for a in self.A:
-                H,Rl=self.bufs[a][0],self.bufs[a][3]
-                self.send(lambda a=a,H=H,Rl=Rl,up=up,passes=passes: (passes,self.copy(H.at[shard],Rl.at[up,d],self.line_s.at[a,up,d],self.line_r.at[a,up,d],p.near_z(1 if up==0 else -1))))
-    def to_x(self):
-        p=self.p
-        for up in (0,1):
-            def add_in(up=up):
-                for a in self.A:
-                    H,Rl=self.bufs[a][0],self.bufs[a][3]
-                    self.copy(Rl.at[up,p.z],Rl.at[up,p.z],self.line_s.at[a,up,p.z],self.line_r.at[a,up,p.z],p.near_z(0)).wait_recv()
-                    self.add(H.at[p.s],[Rl.at[up,p.z]])
-            pl.when((p.z>0) if up==0 else (p.z<ROWS-1))(add_in)
+                    self.copy(Rl.at[slot],Rl.at[slot],self.line_s.at[a,slot],self.line_r.at[a,slot],p.near_z(0)).wait_recv()
+                    self.add(H.at[p.s],[Rl.at[slot]])
+            pl.when(cond)(add_in)
         for a in self.A:
             H,Rx=self.bufs[a][0],self.bufs[a][4]
             for k in range(1,p.X):
@@ -262,7 +277,7 @@
     def to_core(self):
         p=self.p
         for a in self.A:
-            H,Rx=self.bufs[a][0],self.bufs[a][4]; out=self.outs[a]
+            H,Rx,F=self.bufs[a][0],self.bufs[a][4],self.bufs[a][5]
             for k in range(1,p.X):
                 src=lax.rem(p.x-k+p.X,p.X)
                 self.copy(Rx.at[src],Rx.at[src],self.x_s.at[a,k],self.x_r.at[a,src],p.other_x(k)).wait_recv()
@@ -273,50 +288,91 @@
                 value=jnp.zeros_like(own)
                 for q in range(p.X):
                     value=value+jnp.where(p.x==q,own,Rx[q,at,:].astype(f32))
-                out[p.core,at,:]=value
+                F[p.core,at,:]=value
                 return 0
             lax.fori_loop(0,rows//step,body,0)
         for a in self.A:
-            out=self.outs[a]
-            self.send(lambda a=a,out=out: (None,self.copy(out.at[p.core],out.at[p.core],self.end_s.at[a],self.end_r.at[a],p.other_core())))
+            F=self.bufs[a][5]
+            self.send(lambda a=a,F=F: (None,self.copy(F.at[p.core],F.at[p.core],self.end_s.at[a],self.end_r.at[a],p.other_core())))
     def finish(self):
         p=self.p
         for a in self.A:
-            ref=self.outs[a].at[1-p.core]
+            F=self.bufs[a][5]; ref=F.at[1-p.core]
             self.copy(ref,ref,self.end_s.at[a],self.end_r.at[a],p.other_core()).wait_recv()
+            pltpu.make_async_copy(F,self.outs[a],self.out_s.at[a]).start()
         for make in self.sent:
             cond,desc=make()
             when(cond,desc.wait_send)
-    def steps(self):
-        part=lambda f,d: (lambda: f(d))
-        return [self.begin]+[part(self.to_y,d) for d in ORDER]+[part(self.own_y,d) for d in ORDER]+[part(self.line,d) for d in ORDER]+[self.to_x,self.to_core,self.finish]
-def reduce_body(shards,reps,count,*refs):
-    ins,outs,scratch=refs[:count],refs[count:2*count],refs[2*count:]
-    place=Place(shards,reps)
-    meet(place,True)
-    for step in Reduce(place,ins,outs,scratch).steps(): step()
-def reduce_now(arrays,shards,reps,collective_id):
-    count=len(arrays)
-    return pl.pallas_call(partial(reduce_body,shards,reps,count),
-        in_specs=[pl.BlockSpec(memory_space=pl.ANY)]*count,
-        out_specs=[pl.BlockSpec(memory_space=pltpu.VMEM)]*count,
-        out_shape=[jax.ShapeDtypeStruct((2,a.shape[1],a.shape[2]//2),f32) for a in arrays],
-        scratch_shapes=reduce_scratch([a.shape[1:] for a in arrays],shards,reps),
-        compiler_params=pltpu.CompilerParams(collective_id=collective_id,has_side_effects=True,vmem_limit_bytes=50<<20),
-        name="reduce_grads")(*arrays)
+        for a in self.A: pltpu.make_async_copy(self.bufs[a][5],self.outs[a],self.out_s.at[a]).wait()
+    def run(self,what,*args): getattr(self,what)(*args)
+def result_shapes(shapes):
+    return [jax.ShapeDtypeStruct((2,r,c//2),f32) for r,c in shapes]
 
 GATHER_PLAN = {
-    0: (("u", 0), ("d", 0)),
-    2: (("u", 1),),
-    3: (("d", 1), ("u", 2)),
-    4: (("d", 2),),
-    5: (("u", 3), ("u", 4)),
-    6: (("d", 3), ("d", 4)),
-    8: (("u", 5), ("u", 6)),
-    9: (("d", 5), ("d", 6)),
-    11: (("u", 7),),
-    100: (("d", 7), ("u", 8), ("d", 8)),
+    0: (("u", "begin"), ("d", "begin")),
+    2: (("u", "wave", 1),),
+    3: (("d", "wave", 1),),
+    4: (("u", "across", 0), ("d", "across", 0)),
+    5: (("u", "wave", 2),),
+    6: (("d", "wave", 2), ("u", "across", 1)),
+    8: (("u", "wave", 3),),
+    9: (("d", "wave", 3), ("d", "across", 1)),
+    11: (("u", "across", 2),),
+    100: (("d", "across", 2), ("u", "across", 3), ("d", "across", 3), ("u", "finish"), ("d", "finish")),
 }
+
+
+def each(name, what, *more):
+    return tuple((name, what, d) + more for d in ORDER)
+
+
+REDUCE_PLAN = {
+    0: (("d", "begin"), ("u", "begin")),
+    1: each("d", "to_y") + each("d", "own_y"),
+    2: each("u", "to_y") + (("d", "line", 3),) + each("u", "own_y"),
+    3: (("d", "line", 0), ("d", "relay", 3, 1)),
+    4: (("g", "begin"), ("d", "line", 2), ("d", "relay", 0, 1), ("d", "relay", 3, 2)),
+    5: each("g", "to_y")
+    + each("g", "own_y")
+    + (("d", "line", 1), ("d", "relay", 2, 1), ("d", "relay", 0, 2)),
+    6: (("d", "relay", 1, 1), ("u", "line", 3)),
+    7: (("d", "to_x"), ("u", "line", 0), ("u", "relay", 3, 1)),
+    8: (("d", "to_core"), ("u", "line", 2), ("u", "relay", 0, 1), ("u", "relay", 3, 2)),
+    9: (("u", "line", 1), ("u", "relay", 2, 1), ("u", "relay", 0, 2)) + each("g", "line"),
+    10: (("u", "relay", 1, 1),) + each("g", "relay", 1),
+    11: each("g", "relay", 2) + (("u", "to_x"),),
+    100: (
+        ("g", "to_x"),
+        ("u", "to_core"),
+        ("g", "to_core"),
+        ("d", "finish"),
+        ("u", "finish"),
+        ("g", "finish"),
+    ),
+}
+LAST_PLAN = {
+    0: (("r", "begin"),),
+    1: each("r", "to_y") + each("r", "own_y"),
+    2: each("r", "line"),
+    3: each("r", "relay", 1),
+    100: each("r", "relay", 2) + (("r", "to_x"), ("r", "to_core"), ("r", "finish")),
+}
+
+
+def follow(plan, jobs, step, last, ready):
+    def run(at):
+        for name, what, *more in plan.get(at, ()):
+            getattr(jobs[name], what)(*more)
+
+    def first():
+        ready()
+        run(0)
+
+    pl.when(step == 0)(first)
+    for at in sorted(plan):
+        if 0 < at < 100:
+            pl.when(step == at)(partial(run, at))
+    return lambda: pl.when(step == last)(partial(run, 100))
 
 
 def low_lanes():
@@ -346,25 +402,13 @@
     sems = rest[14:]
     step = pl.program_id(0) * PAIRS + pl.program_id(1)
     place = Place(shards, reps)
-    up, down = [
-        Gather(place, [ins[a] for a in which], [outs[a] for a in which], sems[7 * k : 7 * k + 7])
-        for k, which in enumerate(((0,), (1, 2)))
-    ]
-    u, d = up.steps(), down.steps()
-    plan = GATHER_PLAN
-
-    def run(at):
-        for name, k in plan.get(at, ()):
-            (u if name == "u" else d)[k]()
-
-    def first():
-        meet(place, False)
-        run(0)
-
-    pl.when(step == 0)(first)
-    for at in sorted(plan):
-        if 0 < at < 100:
-            pl.when(step == at)(partial(run, at))
+    jobs = {
+        "u": Gather(place, ins[:1], outs[:1], sems[:7]),
+        "d": Gather(place, ins[1:], outs[1:], sems[7:]),
+    }
+    end = follow(
+        GATHER_PLAN, jobs, step, pl.num_programs(0) * PAIRS - 1, lambda: meet(place, False)
+    )
 
     count = len_ref[pl.program_id(0)]
     weight = jnp.concatenate([wq_ref[...], wk_ref[...], wv_ref[...]], axis=1)
@@ -394,7 +438,7 @@
             mixed[e][sl, :] = dot_nn(probs, values[sl]).astype(bf)
     placed = [dot_nn(tables[e][...], mixed[e][...]) for e in range(2)]
     att_ref[...] = jnp.where(low, placed[0], placed[1]).astype(bf)
-    pl.when(step == pl.num_programs(0) * PAIRS - 1)(partial(run, 100))
+    end()
 
 
 def attention_forward(lengths, rounded, weight, bias, rows, arrays, shards, reps, collective_id):
@@ -435,29 +479,29 @@
     )(lengths, rounded, weight, weight, weight, bias, bias, bias, rows, *arrays)
 
 
-def attention_backward_body(
-    len_ref,
-    x_ref,
-    proj_ref,
-    datt_ref,
-    row_ref,
-    dq_ref,
-    dk_ref,
-    dv_ref,
-    dw_ref,
-    db_ref,
-    t0,
-    t1,
-    s0,
-    s1,
-    d0,
-    d1,
-    p0,
-    p1,
-    e0,
-    e1,
-    total,
-):
+def attention_backward_body(shards, reps, shapes, *refs):
+    len_ref, x_ref, proj_ref, datt_ref, row_ref = refs[:5]
+    grads, refs = refs[5:8], refs[8:]
+    (dq_ref, dk_ref, dv_ref, dw_ref, db_ref), sums, refs = refs[:5], refs[5:9], refs[9:]
+    t0, t1, s0, s1, d0, d1, p0, p1, e0, e1, total, group = refs[:12]
+    refs = refs[12:]
+    turn = pl.program_id(0)
+    step = turn * pl.num_programs(1) + pl.program_id(1)
+    place = Place(shards, reps)
+    sizes = [len(reduce_scratch(shapes[k], shards, reps)) for k in "dug"]
+    parts = [refs[sum(sizes[:k]) : sum(sizes[: k + 1])] for k in range(3)]
+    jobs = {
+        "d": Reduce(place, grads[:1], sums[:1], parts[0]),
+        "u": Reduce(place, grads[1:], sums[1:3], parts[1]),
+        "g": Reduce(place, [group], sums[3:], parts[2]),
+    }
+    end = follow(
+        REDUCE_PLAN,
+        jobs,
+        step,
+        pl.num_programs(0) * pl.num_programs(1) - 1,
+        lambda: meet(place, True),
+    )
     seq = pl.program_id(1)
     count = len_ref[seq]
     low = low_lanes()
@@ -528,17 +572,37 @@
 
     dw_ref[0] = total[...].astype(bf)
 
+    @pl.when(turn < 2)
+    def _():
+        rows = D // shards
+        columns = pl.ds(pl.multiple_of(turn * 384, 128), 384)
+        for k in range(shards):
+            group[k, :, columns] = total[k * rows : (k + 1) * rows, :].astype(bf)
+
+    end()
+
 
 def pair_at(i):
     return (i % 2) * (PAIRS // 2) + i // 2
 
 
-def attention_backward(lengths, rounded, proj, datt, rows):
+def pair_at(i):
+    return (i % 2) * (PAIRS // 2) + i // 2
+
+
+def attention_backward(lengths, rounded, proj, datt, rows, grads, shards, reps, collective_id):
     seqs = rows.shape[0]
     tokens = seqs * LEN
     own = lambda width: pl.BlockSpec((LEN, width), lambda i, s, n: (s, pair_at(i)))
+    part = (D // shards, D)
+    shapes = {
+        "d": [grads[0].shape[1:]],
+        "u": [g.shape[1:] for g in grads[1:]],
+        "g": [part],
+    }
+    every = shapes["d"] + shapes["u"] + shapes["g"]
     return pl.pallas_call(
-        attention_backward_body,
+        partial(attention_backward_body, shards, reps, shapes),
         grid_spec=pltpu.PrefetchScalarGridSpec(
             num_scalar_prefetch=1,
             grid=(PAIRS, seqs),
@@ -547,28 +611,31 @@
                 own(384),
                 own(128),
                 pl.BlockSpec((1, 1, 2, LEN), lambda i, s, n: (s, pair_at(i), 0, 0)),
-            ],
+            ]
+            + [pl.BlockSpec(memory_space=pl.ANY)] * 3,
             out_specs=[own(128)] * 3
             + [
                 pl.BlockSpec((1, D, 384), lambda i, s, n: (i // 2, 0, i % 2)),
                 pl.BlockSpec((1, 1, 4, 128), lambda i, s, n: (s, pair_at(i), 0, 0)),
-            ],
+            ]
+            + [pl.BlockSpec(memory_space=pl.ANY)] * 4,
             scratch_shapes=[pltpu.VMEM((LEN, LEN), bf)] * 2
             + [pltpu.VMEM((LEN, 128), f32)] * 4
             + [pltpu.VMEM((LEN, 128), bf)] * 4
-            + [pltpu.VMEM((D, 384), f32)],
+            + [pltpu.VMEM((D, 384), f32), pltpu.VMEM((shards,) + part, bf)]
+            + sum([reduce_scratch(shapes[k], shards, reps) for k in "dug"], []),
         ),
         out_shape=[jax.ShapeDtypeStruct((tokens, D), bf)] * 3
         + [
             jax.ShapeDtypeStruct((PAIRS // 2, D, D), bf),
             jax.ShapeDtypeStruct((seqs, PAIRS, 4, 128), f32),
-        ],
-        compiler_params=pltpu.CompilerParams(vmem_limit_bytes=50 << 20),
-        cost_estimate=pl.CostEstimate(
-            flops=70_000_000_000, bytes_accessed=30_000_000, transcendentals=0
+        ]
+        + result_shapes(every),
+        compiler_params=pltpu.CompilerParams(
+            vmem_limit_bytes=62 << 20, collective_id=collective_id, has_side_effects=True
         ),
         name="attention_backward",
-    )(lengths, rounded, proj, datt, rows)
+    )(lengths, rounded, proj, datt, rows, *grads)
 
 
 def norm_stats(x):
@@ -677,14 +744,24 @@
         compiler_params=pltpu.CompilerParams(vmem_limit_bytes=60<<20),name=name)(left,right)
 
 
-def input_grad_body(bs_ref,dq_ref,dk_ref,dv_ref,w_ref,out_ref):
+def input_grad_body(shards,reps,shapes,bs_ref,dq_ref,dk_ref,dv_ref,w_ref,*refs):
+    n=len(shapes)
+    grads,out_ref,sums,scratch=refs[:n],refs[n],refs[n+1:2*n+1],refs[2*n+1:]
+    place=Place(shards,reps); step=pl.program_id(0)
+    end=follow(LAST_PLAN,{"r":Reduce(place,grads,sums,scratch)},step,pl.num_programs(0)-1,lambda: meet(place,True))
     out_ref[...]=bs_ref[...]+dot_nt(dq_ref[...],w_ref[:,0:D])+dot_nt(dk_ref[...],w_ref[:,D:2*D])+dot_nt(dv_ref[...],w_ref[:,2*D:3*D])
-def input_grad(back_sum,dq,dk,dv,weight,rows=512):
+    end()
+def input_grad(back_sum,dq,dk,dv,weight,grads,shards,reps,collective_id):
+    rows=back_sum.shape[0]//4
     tile=pl.BlockSpec((rows,D),lambda i:(i,0))
-    return pl.pallas_call(input_grad_body,grid=(back_sum.shape[0]//rows,),
-        in_specs=[tile]*4+[pl.BlockSpec((D,3*D),lambda i:(0,0),pipeline_mode=pl.Buffered(1))],out_specs=tile,
-        out_shape=jax.ShapeDtypeStruct(back_sum.shape,f32),
-        compiler_params=pltpu.CompilerParams(vmem_limit_bytes=50<<20),name="input_grad")(back_sum,dq,dk,dv,weight)
+    anywhere=[pl.BlockSpec(memory_space=pl.ANY)]*len(grads)
+    shapes=[g.shape[1:] for g in grads]
+    return pl.pallas_call(partial(input_grad_body,shards,reps,shapes),grid=(4,),
+        in_specs=[tile]*4+[pl.BlockSpec((D,3*D),lambda i:(0,0),pipeline_mode=pl.Buffered(1))]+anywhere,
+        out_specs=[tile]+anywhere,
+        out_shape=[jax.ShapeDtypeStruct(back_sum.shape,f32)]+result_shapes(shapes),
+        scratch_shapes=reduce_scratch(shapes,shards,reps),
+        compiler_params=pltpu.CompilerParams(vmem_limit_bytes=50<<20,collective_id=collective_id,has_side_effects=True),name="input_grad")(back_sum,dq,dk,dv,weight,*grads)
 
 
 WIDE = 4096
@@ -781,9 +858,16 @@
     down_g = weight_grad(activated, second_low, D, "down_weight_grad")
     up_g = weight_grad(first_low, pre_low, D, "up_weight_grad", True)
     out_g = weight_grad(attended, sum_low, D // 2, "out_weight_grad")
-    dq, dk, dv, in_g, bias_sums = attention_backward(lengths, rounded, proj, back_attended, rows)
-    down_s, up_s, out_s = reduce_now(
-        [g.reshape(shards, -1, g.shape[-1]) for g in (down_g, up_g, out_g)], shards, reps, 3
+    dq, dk, dv, in_g, bias_sums, down_s, up_s, out_s, in_first = attention_backward(
+        lengths,
+        rounded,
+        proj,
+        back_attended,
+        rows,
+        [g.reshape(shards, -1, g.shape[-1]) for g in (down_g, up_g, out_g)],
+        shards,
+        reps,
+        3,
     )
     bias_sums = jnp.sum(bias_sums, axis=0)
     query_sum = bias_sums[:, 0:2, DH:].reshape(D)
@@ -797,10 +881,19 @@
         axis=1,
     ).astype(bf)
     small = jnp.pad(small, ((0, 0), (0, WIDE - small.shape[1]))).reshape(shards, 16, 256)
-    *in_s, small_s = reduce_now(
-        [in_g[g].reshape(shards, part, D) for g in range(PAIRS // 2)] + [small], shards, reps, 4
-    )
-    back_input = input_grad(back_sum, dq, dk, dv, in_w).reshape(seqs, LEN, D)
+    back_input, *in_s, small_s = input_grad(
+        back_sum,
+        dq,
+        dk,
+        dv,
+        in_w,
+        [in_g[g].reshape(shards, part, D) for g in range(1, PAIRS // 2)] + [small],
+        shards,
+        reps,
+        4,
+    )
+    back_input = back_input.reshape(seqs, LEN, D)
+    in_s = [in_first] + in_s
     in_s = jnp.concatenate(
         [
             in_s[g][c, :, 128 * t : 128 * t + 128]

time: 501 us -> 398 us (0.79)
  Pallas kernels: 468 us -> 359 us
  local copies, waits for them, and re-layouts: 16.3 us -> 22.9 us
    pallas_call x4 -> x2, Pallas kernels: 265 us -> 157 us  [the longest x1 117 us: attention_backward(): pl.pallas_call(partial(attention_backward_body, shards, reps, shapes), gr...]
    pallas_call x1, Pallas kernels: 79.5 us -> 68.1 us  [attention_forward(): pl.pallas_call(partial(attention_forward_body, shards, reps), grid_spec=p...]
    pallas_call x1, Pallas kernels: 62.1 us -> 73.3 us  [middle(): pl.pallas_call(partial(middle_body, T=T, chunk=chunk, sub_rows=sub_rows),...]
    unnamed x47 -> x52, local copies, waits for them, and re-layouts: 3.72 us -> 11 us
where the time goes in v4:
time: 398 us; the launch traced here: 393 us
  Pallas kernels  359 us (90%)
  local copies, waits for them, and re-layouts  22.9 us (6%)
  other arithmetic  9.35 us (2%)
    pallas_call x1, Pallas kernels, attention_backward(): pl.pallas_call(partial(attention_backward_body, shards, reps, shapes), gr...  117 us
    pallas_call x1, Pallas kernels, middle(): pl.pallas_call(partial(middle_body, T=T, chunk=chunk, sub_rows=sub_rows),...  73.3 us
    pallas_call x1, Pallas kernels, attention_forward(): pl.pallas_call(partial(attention_forward_body, shards, reps), grid_spec=p...  68.1 us
    pallas_call x1, Pallas kernels, input_grad(): pl.pallas_call(partial(input_grad_body, shards, reps, shapes), grid=(4,),...  40.1 us
    pallas_call x3, Pallas kernels, weight_grad(): pl.pallas_call(weight_grad_body, grid=grid, in_specs=[pl.BlockSpec(lb, li...  35.3 us
    pallas_call x1, Pallas kernels, gather_now(): pl.pallas_call(partial(gather_body, shards, reps, count), in_specs=[pl.Bl...  25.5 us
    unnamed x52, local copies, waits for them, and re-layouts  11 us

profile of v4, /device:TPU:9, one launch (start us, length us, event | category | flops | bytes accessed | tf_op | source)
XLA Modules:
  0.0 393.0 jit_solution(996749517457785960)
XLA Ops:
  0.6 6.1 %concatenate.43 = bf16[1152]{0:T(1024)(128)(2,1)S(1)} concatenate(bf16[96]{0:T(256)(128)(2,1)} %param.21, bf16[96]{0:T(256)(128)(2,1)} %param.22, bf16[96]{0:T(256)(128)(2,1)} %param.24, bf16[96]{0:T(256)(128)(2,1)} %param.25, bf16[96]{0:T(256)(128)(2,1)} %param.26, bf16[96]{0:T(256)(128)(2,1)} %param.30, bf16[96]{0:T(256)(128)(2,1)} %param.31, bf16[96]{0:T(256)(128)(2,1)} %param.32, ...), dimensions={0} | concatenate | bytes 4608 | tf_op jit(solution)/shard_map/concatenate | solution.py:771
  6.8 0.9 copy.51.row_ref.refs_4_
  7.7 0.0 copy-start.2
  7.7 0.0 copy-start.5
  7.7 0.0 copy-start.3
  7.8 0.0 copy-start.4
  7.8 0.0 copy-start.6
  7.8 0.0 copy-start.7
  7.8 4.9 %bitcast_convert_fusion.x_ref.refs_1_ = bf16[2048,768]{1,0:T(8,128)(2,1)} fusion(f32[2,1024,768]{2,1,0:T(8,128)} %param.17), kind=kLoop, calls=%fused_computation.46 | loop fusion | flops 1572864 | bytes 9437184 | tf_op jit(solution)/shard_map/convert_element_type | solution.py:822
  12.7 0.0 copy-done.5
  12.7 25.5 %gather_weights.1 = (bf16[8,96,2304]{2,1,0:T(8,128)(2,1)S(1)}, bf16[8,16,256]{2,1,0:T(8,128)(2,1)S(1)}) custom-call(bf16[96,2304]{1,0:T(8,128)(2,1)S(1)} %copy-done.5, bf16[16,256]{1,0:T(8,128)(2,1)S(1)} %reshape.109.refs_1_), custom_call_target="tpu_custom_call" | custom-call | tf_op jit(solution)/shard_map/gather_weights/pallas_call | solution.py:161
  38.2 0.0 copy-start
  38.2 1.9 copy-done
  40.1 0.1 copy.56
  40.2 0.6 copy.57
  40.8 0.1 reshape.111
  40.9 0.1 slice.159
  41.0 0.1 slice.157
  41.1 0.6 pad_maximum_fusion.3.vec_ref
  41.7 0.1 squeeze.92
  41.8 0.1 squeeze.93
  41.9 0.0 copy-done.2
  41.9 0.0 copy-done.3
  41.9 0.0 copy-done.4
  41.9 0.0 copy-done.6
  41.9 0.0 copy-done.7
  42.0 68.1 %attention_forward.1 = (bf16[2048,768]{1,0:T(8,128)(2,1)}, bf16[2048,2304]{1,0:T(8,128)(2,1)}, bf16[8,96,3072]{2,1,0:T(8,128)(2,1)}, bf16[8,384,768]{2,1,0:T(8,128)(2,1)}, bf16[8,96,768]{2,1,0:T(8,128)(2,1)S(1)}) custom-call(s32[2]{0:T(128)S(1)} %copy-done.7, bf16[2048,768]{1,0:T(8,128)(2,1)} %bitcast_convert_fusion.x_ref.refs_1_, ...), custom_call_target="tpu_custom_call" | custom-call | tf_op jit(solution)/shard_map/attention_forward/pallas_call | solution.py:449
  110.0 0.0 copy-start.1
  110.0 1.0 copy-done.1
  111.0 73.3 %middle.1 = (f32[2048,768]{1,0:T(8,128)}, f32[2048,768]{1,0:T(8,128)}, bf16[2048,768]{1,0:T(8,128)(2,1)}, bf16[2048,3072]{1,0:T(8,128)(2,1)}, bf16[2048,3072]{1,...) custom-call(s32[2]{0:T(128)} %refs_0_.3, ...), custom_call_target="tpu_custom_call" | custom-call | tf_op jit(solution)/shard_map/middle/pallas_call | solution.py:721
  184.4 0.0 copy-start.11
  184.4 0.0 copy-start.12
  184.4 6.1 %out_weight_grad.1 = bf16[768,768]{1,0:T(8,128)(2,1)} custom-call(bf16[2048,768]{1,0:T(8,128)(2,1)} %get-tuple-element.47.a_ref.l_ref, bf16[2048,768]{1,0:T(8,128)(2,1)} %get-tuple-element.59.r_ref), custom_call_target="tpu_custom_call" | custom-call | flops 2415919104 | bytes 7471104 | tf_op jit(solution)/shard_map/out_weight_grad/pallas_call | solution.py:740
  190.5 0.0 copy-done.11
  190.5 0.0 copy-done.12
  190.6 0.1 concatenate.49
  190.6 14.7 %down_weight_grad.1 = bf16[3072,768]{1,0:T(8,128)(2,1)} custom-call(bf16[2048,3072]{1,0:T(8,128)(2,1)} %get-tuple-element.55.l_ref, bf16[2048,768]{1,0:T(8,128)(2,1)} %get-tuple-element.56.r_ref), custom_call_target="tpu_custom_call" | custom-call | flops 9663676416 | bytes 20447232 | tf_op jit(solution)/shard_map/down_weight_grad/pallas_call | solution.py:740
  205.3 14.6 %up_weight_grad.1 = bf16[768,3072]{1,0:T(8,128)(2,1)} custom-call(bf16[2048,768]{1,0:T(8,128)(2,1)} %get-tuple-element.57.l_ref, bf16[2048,3072]{1,0:T(8,128)(2,1)} %get-tuple-element.58.r_ref), custom_call_target="tpu_custom_call" | custom-call | flops 9663676416 | bytes 20447232 | tf_op jit(solution)/shard_map/up_weight_grad/pallas_call | solution.py:740
  219.9 117.0 %attention_backward.1 = (bf16[2048,768]{1,0:T(8,128)(2,1)}, bf16[2048,768]{1,0:T(8,128)(2,1)}, bf16[2048,768]{1,0:T(8,128)(2,1)}, bf16[3,768,768]{2,1,0:T(8,128)...) custom-call(s32[2]{0:T(128)} %refs_0_.3, ...), custom_call_target="tpu_custom_call" | custom-call | tf_op jit(solution)/shard_map/attention_backward/pallas_call | solution.py:604
  336.9 0.8 reduce_sum.9
  337.6 0.1 slice.208
  337.7 0.1 concatenate.46
  337.8 0.1 fusion.6
  337.9 0.1 pad_maximum_fusion.5
  338.0 0.1 concatenate.48
  338.1 0.1 reshape.122
  338.2 1.1 slice_bitcast_fusion.5
  339.3 0.7 pad_maximum_fusion.2
  340.0 0.8 bitcast_dynamic-update-slice_fusion.17
  340.8 1.3 slice_bitcast_fusion.3
  342.2 0.0 copy-start.8
  342.2 1.1 pad_maximum_fusion
  343.3 0.0 copy-done.9
  343.3 0.1 slice_bitcast_fusion.1
  343.4 1.1 pad_maximum_fusion.1
  344.5 0.6 copy-done.8
  345.0 0.2 fusion.3
  345.2 0.0 copy-start.10
  345.2 40.1 %input_grad.1 = (f32[2048,768]{1,0:T(8,128)}, f32[2,96,384]{2,1,0:T(8,128)S(1)}, f32[2,96,384]{2,1,0:T(8,128)S(1)}, f32[2,16,128]{2,1,0:T(8,128)S(1)}) custom-call(f32[2048,768]{1,0:T(8,128)} %get-tuple-element.52.bs_ref, bf16[2048,768]{1,0:T(8,128)(2,1)} %get-tuple-element.60.dq_ref, bf16[2048,768]{1,0:T(8,128)(2,1)} %get-tuple-element.61.dk_ref, ...), custom_call_target="tpu_custom_call" | custom-call | tf_op jit(solution)/shard_map/input_grad/pallas_call | solution.py:759
  385.3 0.0 copy-done.10
  385.5 0.0 copy-start.13
  385.6 0.6 slice.217
  386.2 0.6 fusion.5
  386.8 5.9 %copy.84 = f32[2,1024,768]{2,1,0:T(8,128)} copy(f32[2,1024,768]{2,1,0:T(8,128)} %bitcast.99) | data formatting | bytes 12582912
  (42 shorter events, 0.3 us)
Async XLA Ops:
  7.7 34.2 %copy-start.2 = (s32[2,6,2,1024]{3,2,1,0:T(2,128)}, s32[2,6,2,1024]{3,2,1,0:T(2,128)S(1)}, u32[]{:S(2)}) copy-start(s32[2,6,2,1024]{3,2,1,0:T(2,128)S(1)} %copy.51.row_ref.refs_4_) | copy-start | bytes 294916
  7.7 4.9 %copy-start.5 = (bf16[96,2304]{1,0:T(8,128)(2,1)S(1)}, bf16[96,2304]{1,0:T(8,128)(2,1)}, u32[]{:S(2)}) copy-start(bf16[96,2304]{1,0:T(8,128)(2,1)} %refs_0_.2) | copy-start | bytes 1327108
  7.7 34.2 %copy-start.3 = (bf16[96,3072]{1,0:T(8,128)(2,1)S(1)}, bf16[96,3072]{1,0:T(8,128)(2,1)}, u32[]{:S(2)}) copy-start(bf16[96,3072]{1,0:T(8,128)(2,1)} %rest_0_.1) | copy-start | bytes 1769476
  7.8 34.2 %copy-start.4 = (bf16[384,768]{1,0:T(8,128)(2,1)S(1)}, bf16[384,768]{1,0:T(8,128)(2,1)}, u32[]{:S(2)}) copy-start(bf16[384,768]{1,0:T(8,128)(2,1)} %rest_1_.1) | copy-start | bytes 1769476
  7.8 34.2 %copy-start.6 = (bf16[96,768]{1,0:T(8,128)(2,1)S(1)}, bf16[96,768]{1,0:T(8,128)(2,1)}, u32[]{:S(2)}) copy-start(bf16[96,768]{1,0:T(8,128)(2,1)} %rest_2_.1) | copy-start | bytes 442372
  7.8 34.2 %copy-start.7 = (s32[2]{0:T(128)S(1)}, s32[2]{0:T(128)}, u32[]{:S(2)}) copy-start(s32[2]{0:T(128)} %refs_0_.3) | copy-start | bytes 28
  38.2 1.9 copy-start
  110.0 1.0 copy-start.1
  184.4 6.1 %copy-start.11 = (f32[1,3072]{1,0:T(1,128)S(1)}, f32[1,3072]{1,0:T(1,128)}, u32[]{:S(2)}) copy-start(f32[1,3072]{1,0:T(1,128)} %get-tuple-element.66) | copy-start | bytes 36868
  184.4 6.2 %copy-start.12 = (f32[8,768]{1,0:T(8,128)S(1)}, f32[8,768]{1,0:T(8,128)}, u32[]{:S(2)}) copy-start(f32[8,768]{1,0:T(8,128)} %get-tuple-element.65) | copy-start | bytes 73732
  338.1 5.2 %copy-start.9 = (f32[2,384,384]{2,1,0:T(8,128)S(1)}, f32[2,384,384]{2,1,0:T(8,128)}, u32[]{:S(2)}) copy-start(f32[2,384,384]{2,1,0:T(8,128)} %get-tuple-element.74) | copy-start | bytes 3538948
  342.2 2.9 copy-start.8
  345.2 40.1 %copy-start.10 = (f32[2,96,384]{2,1,0:T(8,128)S(1)}, f32[2,96,384]{2,1,0:T(8,128)}, u32[]{:S(2)}) copy-start(f32[2,96,384]{2,1,0:T(8,128)} %get-tuple-element.68) | copy-start | bytes 884740
  385.5 7.2 %copy-start.13 = (f32[96,2304]{1,0:T(8,128)}, f32[96,2304]{1,0:T(8,128)S(1)}, u32[]{:S(2)}) copy-start(f32[96,2304]{1,0:T(8,128)S(1)} %bitcast_dynamic-update-slice_fusion) | copy-start | bytes 2654212

commit v5 on v4

--- a/solution.py
+++ b/solution.py
@@ -65,24 +65,22 @@
     pl.when(jnp.logical_not(inner))(lambda: pl.semaphore_wait(sem,others+1))
 
 def gather_semaphores(count,shards):
-    Y=shards//ROWS
-    return [pltpu.SemaphoreType.DMA((count,2,ROWS)),pltpu.SemaphoreType.DMA((count,2,ROWS)),
-            pltpu.SemaphoreType.DMA((count,ROWS,Y)),pltpu.SemaphoreType.DMA((count,ROWS,Y)),
-            pltpu.SemaphoreType.DMA((count,shards)),pltpu.SemaphoreType.DMA((count,shards)),
-            pltpu.SemaphoreType.DMA((count,))]
+    Y=shards//ROWS; dma=pltpu.SemaphoreType.DMA
+    return [dma((count,2,ROWS)),dma((count,2,ROWS)),dma((count,ROWS,Y)),dma((count,ROWS,Y)),
+            dma((count,2,shards)),dma((count,2,shards)),dma((count,shards)),dma((count,shards)),dma((count,))]
 
 class Gather:
-    def __init__(self,place,ins,outs,sems):
-        self.p=place; self.ins=ins; self.outs=outs
-        self.line_s,self.line_r,self.y_s,self.y_r,self.core_s,self.core_r,self.own=sems
+    def __init__(self,place,ins,outs,sems,share=False):
+        self.p=place; self.ins=ins; self.outs=outs; self.share=share and place.X==2
+        self.line_s,self.line_r,self.y_s,self.y_r,self.core_s,self.core_r,self.x_s,self.x_r,self.own=sems
         self.sent=[]
-    def half(self,ref,shard=None):
-        n=ref.shape[-1]//2
-        cols=pl.ds(pl.multiple_of(self.p.core*n,128),n)
-        return ref.at[:,cols] if shard is None else ref.at[shard,:,cols]
-    def other_half(self,ref,shard):
-        n=ref.shape[-1]//2
-        return ref.at[shard,:,pl.ds(pl.multiple_of((1-self.p.core)*n,128),n)]
+    def piece(self,ref,shard=None,core=None,x=None):
+        p=self.p; n=ref.shape[-1]//2; r=ref.shape[-2]
+        cols=pl.ds(pl.multiple_of((p.core if core is None else core)*n,128),n)
+        rows=slice(None)
+        if self.share:
+            rows=pl.ds(pl.multiple_of((p.x if x is None else x)*(r//2),16),r//2)
+        return ref.at[rows,cols] if shard is None else ref.at[shard,rows,cols]
     def send(self,make):
         cond,desc=make()
         when(cond,desc.start); self.sent.append(make)
@@ -92,27 +90,38 @@
         zz=self.p.z+places
         if places==0: return None,zz
         return jnp.logical_and(zz>=0,zz<ROWS),jnp.clip(zz,0,ROWS-1)
+    def shard_at(self,zz,k):
+        p=self.p
+        return zz*p.Y+(lax.rem(p.y-k+p.Y,p.Y) if k else p.y)
     def to_line(self,a,places,d):
         p=self.p; i,o=self.ins[a],self.outs[a]
         def make():
             cond,zz=self.at(places); shard=zz*p.Y+p.y
             edge=(p.z<ROWS-1) if d==0 else (p.z>0)
-            src=self.half(i) if places==0 else self.half(o,shard)
-            return (edge if cond is None else jnp.logical_and(cond,edge)),self.copy(src,self.half(o,shard),self.line_s.at[a,d,zz],self.line_r.at[a,d,zz],p.near_z(1 if d==0 else -1))
+            src=self.piece(i) if places==0 else self.piece(o,shard)
+            return (edge if cond is None else jnp.logical_and(cond,edge)),self.copy(src,self.piece(o,shard),self.line_s.at[a,d,zz],self.line_r.at[a,d,zz],p.near_z(1 if d==0 else -1))
         self.send(make)
     def to_y(self,a,places,k):
         p=self.p; i,o=self.ins[a],self.outs[a]
         def make():
             cond,zz=self.at(places); shard=zz*p.Y+p.y
-            src=self.half(i) if places==0 else self.half(o,shard)
-            return cond,self.copy(src,self.half(o,shard),self.y_s.at[a,zz,k],self.y_r.at[a,zz,k],p.other_y(k))
+            src=self.piece(i) if places==0 else self.piece(o,shard)
+            return cond,self.copy(src,self.piece(o,shard),self.y_s.at[a,zz,k],self.y_r.at[a,zz,k],p.other_y(k))
         self.send(make)
-    def to_core(self,a,places,k):
+    def to_core(self,a,places,k,other=False):
+        p=self.p; o=self.outs[a]; slot=1 if other else 0
+        def make():
+            cond,zz=self.at(places); shard=self.shard_at(zz,k)
+            ref=self.piece(o,shard,x=1-p.x if other else p.x)
+            return cond,self.copy(ref,ref,self.core_s.at[a,slot,shard],self.core_r.at[a,slot,shard],p.other_core())
+        self.send(make)
+    def to_x(self,a,places,k):
         p=self.p; o=self.outs[a]
+        if not self.share: return
         def make():
-            cond,zz=self.at(places); shard=zz*p.Y+lax.rem(p.y-k+p.Y,p.Y)
-            ref=self.half(o,shard)
-            return cond,self.copy(ref,ref,self.core_s.at[a,shard],self.core_r.at[a,shard],p.other_core())
+            cond,zz=self.at(places); shard=self.shard_at(zz,k)
+            ref=self.piece(o,shard)
+            return cond,self.copy(ref,ref,self.x_s.at[a,shard],self.x_r.at[a,shard],p.other_x(1))
         self.send(make)
     def begin(self):
         for a,(i,o) in enumerate(zip(self.ins,self.outs)):
@@ -124,27 +133,36 @@
         for d in (0,1):
             places=-w if d==0 else w
             for a,o in enumerate(self.outs):
-                cond,zz=self.at(places); ref=self.half(o,zz*p.Y+p.y)
+                cond,zz=self.at(places); ref=self.piece(o,zz*p.Y+p.y)
                 when(cond,self.copy(ref,ref,self.line_s.at[a,d,zz],self.line_r.at[a,d,zz],p.near_z(0)).wait_recv)
                 self.to_line(a,places,d)
                 for k in range(1,p.Y): self.to_y(a,places,k)
-                self.to_core(a,places,0)
+                self.to_x(a,places,0); self.to_core(a,places,0)
     def across(self,w):
         p=self.p
         for places in ((0,) if w==0 else (-w,w)):
             for k in range(1,p.Y):
                 for a,o in enumerate(self.outs):
-                    cond,zz=self.at(places); shard=zz*p.Y+lax.rem(p.y-k+p.Y,p.Y)
-                    ref=self.half(o,shard)
+                    cond,zz=self.at(places); ref=self.piece(o,self.shard_at(zz,k))
                     when(cond,self.copy(ref,ref,self.y_s.at[a,zz,k],self.y_r.at[a,zz,k],p.other_y(k)).wait_recv)
-                    self.to_core(a,places,k)
+                    self.to_x(a,places,k); self.to_core(a,places,k)
+    def over(self,w):
+        p=self.p
+        if not self.share: return
+        for places in ((0,) if w==0 else (-w,w)):
+            for k in range(1 if w==0 else 0,p.Y):
+                for a,o in enumerate(self.outs):
+                    cond,zz=self.at(places); shard=self.shard_at(zz,k); ref=self.piece(o,shard,x=1-p.x)
+                    when(cond,self.copy(ref,ref,self.x_s.at[a,shard],self.x_r.at[a,shard],p.other_x(1)).wait_recv)
+                    self.to_core(a,places,k,True)
     def finish(self):
         p=self.p
         for a,(i,o) in enumerate(zip(self.ins,self.outs)):
             for k in range(1,p.S):
                 shard=lax.rem(p.s+k,p.S)
-                ref=self.other_half(o,shard)
-                self.copy(ref,ref,self.core_s.at[a,shard],self.core_r.at[a,shard],p.other_core()).wait_recv()
+                for slot in range(2 if self.share else 1):
+                    ref=self.piece(o,shard,core=1-p.core,x=1-p.x if slot else p.x)
+                    self.copy(ref,ref,self.core_s.at[a,slot,shard],self.core_r.at[a,slot,shard],p.other_core()).wait_recv()
             pltpu.make_async_copy(i,o.at[p.s],self.own.at[a]).wait()
         for make in self.sent:
             cond,desc=make()
@@ -167,21 +185,22 @@
         name="gather_weights")(*arrays)
 
 ORDER=(3,0,2,1)
-def reduce_scratch(shapes,shards,reps):
+def reduce_scratch(shapes,shards,reps,x_first=False):
+    x_first=x_first and reps==4
     S=shards; Y=S//ROWS; X=reps//2; A=len(shapes)
     out=[]
     for r,c in shapes:
-        n=c//2
-        out+=[pltpu.VMEM((S,r,n),bf),pltpu.VMEM((S,r,n),bf),pltpu.VMEM((max(Y-1,1),ROWS,r,n),bf),
-              pltpu.VMEM((ROWS+1,r,n),bf),pltpu.VMEM((X,r,n),bf),pltpu.VMEM((2,r,n),f32)]
+        n=c//2; m=r//2 if x_first else r
+        out+=[pltpu.VMEM((S,r,n),bf),pltpu.VMEM((S,r,n),bf),pltpu.VMEM((max(Y-1,1),ROWS,m,n),bf),
+              pltpu.VMEM((ROWS+1,m,n),bf),pltpu.VMEM((S+1,m,n) if x_first else (X,r,n),bf),pltpu.VMEM((2,r,n),f32)]
     dma=pltpu.SemaphoreType.DMA
-    return out+[dma((A,S)),dma((A,S)),dma((A,S)),dma((A,Y,ROWS)),dma((A,Y,ROWS)),dma((A,ROWS+1)),dma((A,ROWS+1)),dma((A,X)),dma((A,X)),dma((A,)),dma((A,)),dma((A,))]
+    return out+[dma((A,S)),dma((A,S)),dma((A,S)),dma((A,Y,ROWS)),dma((A,Y,ROWS)),dma((A,ROWS+1)),dma((A,ROWS+1)),dma((A,S+X)),dma((A,S+X)),dma((A,)),dma((A,)),dma((A,))]
 class Reduce:
-    def __init__(self,place,ins,outs,scratch):
+    def __init__(self,place,ins,outs,scratch,x_first=False):
         self.p=place; self.ins=ins; self.outs=outs; A=len(ins); self.A=range(A)
         self.bufs=[scratch[6*a:6*a+6] for a in range(A)]
         (self.own,self.core_s,self.core_r,self.y_s,self.y_r,self.line_s,self.line_r,self.x_s,self.x_r,self.end_s,self.end_r,self.out_s)=scratch[6*A:]
-        self.sent=[]
+        self.sent=[]; self.x_first=x_first and place.X==2
     def copy(self,src,dst,ss,rs,dev):
         return pltpu.make_async_remote_copy(src_ref=src,dst_ref=dst,send_sem=ss,recv_sem=rs,device_id=dev,device_id_type=MESH)
     def send(self,make):
@@ -190,12 +209,17 @@
     def half(self,a,shard,core):
         n=self.ins[a].shape[-1]//2
         return self.ins[a].at[shard,:,pl.ds(pl.multiple_of(core*n,128),n)]
+    def mine(self,a,shard,x=None):
+        H=self.bufs[a][0]
+        if not self.x_first: return H.at[shard]
+        m=H.shape[1]//2
+        return H.at[shard,pl.ds(pl.multiple_of((self.p.x if x is None else x)*m,16),m)]
     def add(self,dst,others):
-        rows,n=dst.shape; step=next(s for s in (96,48,16) if rows%s==0 and (s==16 or s*n<=96*512))
+        rows,n=dst.shape; step=next(s for s in (192,96,48,16) if rows%s==0 and (s==16 or s*n<=96*768))
         def block(at):
-            value=dst[at,:].astype(f32)
-            for o in others: value=value+o[at,:].astype(f32)
-            dst[at,:]=value.astype(bf)
+            value=dst[at,:]
+            for o in others: value=value+o[at,:]
+            dst[at,:]=value
         if rows==step: block(slice(0,rows)); return
         def body(i,_):
             block(pl.ds(pl.multiple_of(i*step,16),step))
@@ -220,18 +244,34 @@
             pltpu.make_async_copy(self.half(a,shard,p.core),H.at[shard],self.own.at[a,shard]).wait()
             self.copy(Rc.at[shard],Rc.at[shard],self.core_s.at[a,shard],self.core_r.at[a,shard],p.other_core()).wait_recv()
             self.add(H.at[shard],[Rc.at[shard]])
+    def to_pair(self,k,d):
+        p=self.p; shard=d*p.Y+lax.rem(p.y+k,p.Y)
+        if not self.x_first: return
+        self.join_core(shard)
+        for a in self.A:
+            def make(a=a):
+                shard=d*p.Y+lax.rem(p.y+k,p.Y)
+                return None,self.copy(self.mine(a,shard,1-p.x),self.bufs[a][4].at[shard],self.x_s.at[a,shard],self.x_r.at[a,shard],p.other_x(1))
+            self.send(make)
+    def ready(self,shard):
+        p=self.p
+        if not self.x_first: self.join_core(shard); return
+        for a in self.A:
+            got=self.bufs[a][4].at[shard]
+            self.copy(got,got,self.x_s.at[a,shard],self.x_r.at[a,shard],p.other_x(1)).wait_recv()
+            self.add(self.mine(a,shard),[got])
     def to_y(self,d):
         p=self.p
         for k in range(1,p.Y):
-            self.join_core(d*p.Y+lax.rem(p.y+k,p.Y))
+            self.ready(d*p.Y+lax.rem(p.y+k,p.Y))
             for a in self.A:
                 H,_,Ry=self.bufs[a][0:3]
                 def make(a=a,H=H,Ry=Ry,k=k):
                     shard=d*p.Y+lax.rem(p.y+k,p.Y)
-                    return None,self.copy(H.at[shard],Ry.at[k-1,d],self.y_s.at[a,k,d],self.y_r.at[a,k,d],p.other_y(k))
+                    return None,self.copy(self.mine(a,shard),Ry.at[k-1,d],self.y_s.at[a,k,d],self.y_r.at[a,k,d],p.other_y(k))
                 self.send(make)
     def own_y(self,d):
-        self.join_core(d*self.p.Y+self.p.y)
+        self.ready(d*self.p.Y+self.p.y)
     def along(self,d,up,j):
         p=self.p
         if (j>=d) if up else (ROWS-1-j<=d): return
@@ -242,14 +282,14 @@
                 for a in self.A:
                     H,Rl=self.bufs[a][0],self.bufs[a][3]
                     self.copy(Rl.at[d],Rl.at[d],self.line_s.at[a,d],self.line_r.at[a,d],p.near_z(0)).wait_recv()
-                    self.add(H.at[shard],[Rl.at[d]])
+                    self.add(self.mine(a,shard),[Rl.at[d]])
             pl.when(here)(add_in)
         last=(j==d-1) if up else (ROWS-1-j==d+1)
         slot=ROWS if last and not up else d
         for a in self.A:
             def make(a=a):
                 H,Rl=self.bufs[a][0],self.bufs[a][3]
-                return p.z==(j if up else ROWS-1-j),self.copy(H.at[d*p.Y+p.y],Rl.at[slot],self.line_s.at[a,slot],self.line_r.at[a,slot],p.near_z(1 if up else -1))
+                return p.z==(j if up else ROWS-1-j),self.copy(self.mine(a,d*p.Y+p.y),Rl.at[slot],self.line_s.at[a,slot],self.line_r.at[a,slot],p.near_z(1 if up else -1))
             self.send(make)
     def line(self,d):
         p=self.p; shard=d*p.Y+p.y
@@ -257,7 +297,7 @@
             H,_,Ry=self.bufs[a][0:3]
             for k in range(1,p.Y):
                 self.copy(Ry.at[k-1,d],Ry.at[k-1,d],self.y_s.at[a,k,d],self.y_r.at[a,k,d],p.other_y(k)).wait_recv()
-            self.add(H.at[shard],[Ry.at[k-1,d] for k in range(1,p.Y)])
+            self.add(self.mine(a,shard),[Ry.at[k-1,d] for k in range(1,p.Y)])
         self.along(d,True,0); self.along(d,False,0)
     def relay(self,d,j):
         self.along(d,True,j); self.along(d,False,j)
@@ -268,16 +308,26 @@
                 for a in self.A:
                     H,Rl=self.bufs[a][0],self.bufs[a][3]
                     self.copy(Rl.at[slot],Rl.at[slot],self.line_s.at[a,slot],self.line_r.at[a,slot],p.near_z(0)).wait_recv()
-                    self.add(H.at[p.s],[Rl.at[slot]])
+                    self.add(self.mine(a,p.s),[Rl.at[slot]])
             pl.when(cond)(add_in)
         for a in self.A:
             H,Rx=self.bufs[a][0],self.bufs[a][4]
+            if self.x_first:
+                self.send(lambda a=a,Rx=Rx: (None,self.copy(self.mine(a,p.s),Rx.at[p.S],self.x_s.at[a,p.S],self.x_r.at[a,p.S],p.other_x(1))))
+                continue
             for k in range(1,p.X):
                 self.send(lambda a=a,H=H,Rx=Rx,k=k: (None,self.copy(H.at[p.s],Rx.at[p.x],self.x_s.at[a,k],self.x_r.at[a,p.x],p.other_x(k))))
     def to_core(self):
         p=self.p
         for a in self.A:
             H,Rx,F=self.bufs[a][0],self.bufs[a][4],self.bufs[a][5]
+            if self.x_first:
+                got=Rx.at[p.S]; m=H.shape[1]//2
+                self.copy(got,got,self.x_s.at[a,p.S],self.x_r.at[a,p.S],p.other_x(1)).wait_recv()
+                for x in range(2):
+                    own=H[p.s,x*m:(x+1)*m,:]
+                    F[p.core,x*m:(x+1)*m,:]=jnp.where(p.x==x,own,Rx[p.S]).astype(f32)
+                continue
             for k in range(1,p.X):
                 src=lax.rem(p.x-k+p.X,p.X)
                 self.copy(Rx.at[src],Rx.at[src],self.x_s.at[a,k],self.x_r.at[a,src],p.other_x(k)).wait_recv()
@@ -311,14 +361,15 @@
 GATHER_PLAN = {
     0: (("u", "begin"), ("d", "begin")),
     2: (("u", "wave", 1),),
-    3: (("d", "wave", 1),),
-    4: (("u", "across", 0), ("d", "across", 0)),
-    5: (("u", "wave", 2),),
-    6: (("d", "wave", 2), ("u", "across", 1)),
-    8: (("u", "wave", 3),),
-    9: (("d", "wave", 3), ("d", "across", 1)),
-    11: (("u", "across", 2),),
-    100: (("d", "across", 2), ("u", "across", 3), ("d", "across", 3), ("u", "finish"), ("d", "finish")),
+    3: (("d", "wave", 1), ("u", "across", 0), ("d", "across", 0)),
+    4: (("u", "wave", 2),),
+    5: (("d", "wave", 2),),
+    6: (("u", "across", 1), ("d", "over", 0)),
+    7: (("u", "wave", 3),),
+    8: (("d", "wave", 3), ("d", "across", 1)),
+    9: (("u", "across", 2), ("u", "across", 3)),
+    10: (("d", "across", 2), ("d", "across", 3), ("d", "over", 1)),
+    100: (("d", "over", 2), ("d", "over", 3), ("u", "finish"), ("d", "finish")),
 }
 
 
@@ -328,20 +379,22 @@
 
 REDUCE_PLAN = {
     0: (("d", "begin"), ("u", "begin")),
-    1: each("d", "to_y") + each("d", "own_y"),
-    2: each("u", "to_y") + (("d", "line", 3),) + each("u", "own_y"),
-    3: (("d", "line", 0), ("d", "relay", 3, 1)),
-    4: (("g", "begin"), ("d", "line", 2), ("d", "relay", 0, 1), ("d", "relay", 3, 2)),
-    5: each("g", "to_y")
-    + each("g", "own_y")
-    + (("d", "line", 1), ("d", "relay", 2, 1), ("d", "relay", 0, 2)),
-    6: (("d", "relay", 1, 1), ("u", "line", 3)),
-    7: (("d", "to_x"), ("u", "line", 0), ("u", "relay", 3, 1)),
-    8: (("d", "to_core"), ("u", "line", 2), ("u", "relay", 0, 1), ("u", "relay", 3, 2)),
-    9: (("u", "line", 1), ("u", "relay", 2, 1), ("u", "relay", 0, 2)) + each("g", "line"),
-    10: (("u", "relay", 1, 1),) + each("g", "relay", 1),
-    11: each("g", "relay", 2) + (("u", "to_x"),),
-    100: (
+    1: each("d", "to_y"),
+    2: tuple(("u", "to_pair", 1, d) for d in ORDER) + each("d", "own_y"),
+    3: tuple(("u", "to_pair", 0, d) for d in ORDER) + (("d", "line", 3),),
+    4: (("g", "begin"), ("d", "line", 0)),
+    5: each("u", "to_y") + (("d", "line", 2), ("d", "relay", 3, 1)),
+    6: each("g", "to_y") + each("g", "own_y") + (("d", "line", 1), ("d", "relay", 0, 1)),
+    7: (("d", "relay", 3, 2), ("d", "relay", 2, 1), ("u", "own_y", 3), ("u", "own_y", 0)),
+    8: (("d", "relay", 0, 2), ("d", "relay", 1, 1), ("u", "own_y", 2), ("u", "own_y", 1))
+    + (("u", "line", 3), ("u", "line", 0)),
+    9: (("d", "to_x"), ("u", "line", 2), ("u", "line", 1), ("u", "relay", 3, 1), ("u", "relay", 0, 1)),
+    10: (("d", "to_core"), ("u", "relay", 2, 1), ("u", "relay", 3, 2), ("u", "relay", 0, 2))
+    + each("g", "line"),
+    11: (("u", "relay", 1, 1),) + each("g", "relay", 1),
+    100: each("g", "relay", 2)
+    + (
+        ("u", "to_x"),
         ("g", "to_x"),
         ("u", "to_core"),
         ("g", "to_core"),
@@ -351,11 +404,18 @@
     ),
 }
 LAST_PLAN = {
-    0: (("r", "begin"),),
-    1: each("r", "to_y") + each("r", "own_y"),
-    2: each("r", "line"),
-    3: each("r", "relay", 1),
-    100: each("r", "relay", 2) + (("r", "to_x"), ("r", "to_core"), ("r", "finish")),
+    0: (("a", "begin"), ("b", "begin")),
+    1: each("a", "to_y"),
+    2: tuple(("b", "to_pair", k, d) for k in (1, 0) for d in ORDER) + each("a", "own_y"),
+    4: (("a", "line", 3), ("a", "line", 0)),
+    5: (("a", "line", 2), ("a", "line", 1)) + each("b", "to_y"),
+    6: each("b", "own_y") + each("a", "relay", 1),
+    7: (("a", "relay", 3, 2), ("a", "relay", 0, 2)) + each("b", "line"),
+    100: (("a", "to_x"),)
+    + each("b", "relay", 1)
+    + (("a", "to_core"),)
+    + each("b", "relay", 2)
+    + (("b", "to_x"), ("b", "to_core"), ("a", "finish"), ("b", "finish")),
 }
 
 
@@ -380,12 +440,25 @@
 
 
 def table_of(order_row):
-    positions = lax.broadcasted_iota(jnp.int32, (LEN, LEN), 0)
-    return jnp.where(jnp.broadcast_to(order_row, (LEN, LEN)) == positions, 1.0, 0.0).astype(bf)
+    held = jnp.broadcast_to(order_row.astype(jnp.int16), (LEN, LEN))
+    positions = lax.broadcasted_iota(jnp.int16, (LEN, LEN), 0)
+    return jnp.where(held == positions, jnp.ones((), bf), jnp.zeros((), bf))
+
+
+def turned_table_of(order_row):
+    held = jnp.transpose(jnp.broadcast_to(order_row, (128, LEN))).astype(jnp.int16)
+    lanes = lax.broadcasted_iota(jnp.int16, (LEN, 128), 1)
+    return jnp.concatenate(
+        [
+            jnp.where(held == lanes + jnp.int16(128 * b), jnp.ones((), bf), jnp.zeros((), bf))
+            for b in range(LEN // 128)
+        ],
+        axis=1,
+    )
 
 
 def half_roll(source):
-    return pltpu.roll(source.astype(f32), DH, 1).astype(bf)
+    return pltpu.roll(source, DH, 1)
 
 
 def softmax_rows(scores):
@@ -395,20 +468,24 @@
 
 
 def attention_forward_body(
-    shards, reps, len_ref, x_ref, wq_ref, wk_ref, wv_ref, bq_ref, bk_ref, bv_ref, row_ref, *rest
+    shards, reps, len_ref, h_ref, wq_ref, wk_ref, wv_ref, bq_ref, bk_ref, bv_ref, row_ref, *rest
 ):
-    ins, (att_ref, proj_ref), outs = rest[:3], rest[3:5], rest[5:8]
-    tables, scores, mixed = rest[8:10], rest[10:12], rest[12:14]
-    sems = rest[14:]
+    ins, (att_ref, proj_ref, x_ref), outs = rest[:3], rest[3:6], rest[6:9]
+    tables, scores, mixed = rest[9:11], rest[11:13], rest[13:15]
+    sems = rest[15:]
     step = pl.program_id(0) * PAIRS + pl.program_id(1)
     place = Place(shards, reps)
     jobs = {
-        "u": Gather(place, ins[:1], outs[:1], sems[:7]),
-        "d": Gather(place, ins[1:], outs[1:], sems[7:]),
+        "u": Gather(place, ins[:1], outs[:1], sems[:9]),
+        "d": Gather(place, ins[1:], outs[1:], sems[9:], True),
     }
     end = follow(
-        GATHER_PLAN, jobs, step, pl.num_programs(0) * PAIRS - 1, lambda: meet(place, False)
-    )
+        GATHER_PLAN, jobs, step, pl.num_programs(0) * PAIRS - 1, lambda: meet(place, True)
+    )
+
+    @pl.when(pl.program_id(1) == 0)
+    def _():
+        x_ref[...] = h_ref[...].astype(bf)
 
     count = len_ref[pl.program_id(0)]
     weight = jnp.concatenate([wq_ref[...], wk_ref[...], wv_ref[...]], axis=1)
@@ -418,11 +495,11 @@
     query, key, value = proj[:, 0:128], proj[:, 128:256], proj[:, 256:384]
     pairs = [jnp.where(low, query, half_roll(key)), jnp.where(low, half_roll(query), key)]
     proj_ref[...] = jnp.concatenate([pairs[0], value, pairs[1]], axis=1)
-    rows = [row_ref[0, 0, e : e + 1, :] for e in range(2)]
+    rows = [row_ref[0, pl.ds(2 * pl.program_id(1) + e, 1), :] for e in range(2)]
     for e in range(2):
         tables[e][...] = table_of(rows[e])
     picked = [
-        dot_tn(tables[e][...], jnp.concatenate([pairs[e], value], axis=1)).astype(bf)
+        dot_nn(turned_table_of(rows[e]), jnp.concatenate([pairs[e], value], axis=1)).astype(bf)
         for e in range(2)
     ]
     for e in range(2):
@@ -441,7 +518,7 @@
     end()
 
 
-def attention_forward(lengths, rounded, weight, bias, rows, arrays, shards, reps, collective_id):
+def attention_forward(lengths, hidden, weight, bias, rows, arrays, shards, reps, collective_id):
     seqs = rows.shape[0]
     tokens = seqs * LEN
     column = lambda part: pl.BlockSpec((D, 128), lambda s, h, n: (0, part * PAIRS + h))
@@ -454,11 +531,12 @@
             in_specs=[pl.BlockSpec((LEN, D), lambda s, h, n: (s, 0))]
             + [column(part) for part in range(3)]
             + [column_b(part) for part in range(3)]
-            + [pl.BlockSpec((1, 1, 2, LEN), lambda s, h, n: (s, h, 0, 0))]
+            + [pl.BlockSpec((1, H, LEN), lambda s, h, n: (s, 0, 0))]
             + [pl.BlockSpec(memory_space=pltpu.VMEM)] * 3,
             out_specs=[
                 pl.BlockSpec((LEN, 128), lambda s, h, n: (s, h)),
                 pl.BlockSpec((LEN, 384), lambda s, h, n: (s, h)),
+                pl.BlockSpec((LEN, D), lambda s, h, n: (s, 0)),
             ]
             + [pl.BlockSpec(memory_space=pl.ANY)] * 3,
             scratch_shapes=[pltpu.VMEM((LEN, LEN), bf)] * 2
@@ -470,13 +548,14 @@
         out_shape=[
             jax.ShapeDtypeStruct((tokens, D), bf),
             jax.ShapeDtypeStruct((tokens, 3 * D), bf),
+            jax.ShapeDtypeStruct((tokens, D), bf),
         ]
         + [jax.ShapeDtypeStruct((shards,) + a.shape, bf) for a in arrays],
         compiler_params=pltpu.CompilerParams(
             vmem_limit_bytes=50 << 20, collective_id=collective_id, has_side_effects=True
         ),
         name="attention_forward",
-    )(lengths, rounded, weight, weight, weight, bias, bias, bias, rows, *arrays)
+    )(lengths, hidden, weight, weight, weight, bias, bias, bias, rows, *arrays)
 
 
 def attention_backward_body(shards, reps, shapes, *refs):
@@ -488,11 +567,11 @@
     turn = pl.program_id(0)
     step = turn * pl.num_programs(1) + pl.program_id(1)
     place = Place(shards, reps)
-    sizes = [len(reduce_scratch(shapes[k], shards, reps)) for k in "dug"]
+    sizes = [len(reduce_scratch(shapes[k], shards, reps, k == "u")) for k in "dug"]
     parts = [refs[sum(sizes[:k]) : sum(sizes[: k + 1])] for k in range(3)]
     jobs = {
         "d": Reduce(place, grads[:1], sums[:1], parts[0]),
-        "u": Reduce(place, grads[1:], sums[1:3], parts[1]),
+        "u": Reduce(place, grads[1:], sums[1:3], parts[1], True),
         "g": Reduce(place, [group], sums[3:], parts[2]),
     }
     end = follow(
@@ -507,7 +586,7 @@
     low = low_lanes()
     zero = jnp.zeros((), bf)
     tables, scores, back_probs, probs_low, backs = (t0, t1), (s0, s1), (d0, d1), (p0, p1), (e0, e1)
-    rows = [row_ref[0, 0, e : e + 1, :] for e in range(2)]
+    rows = [row_ref[0, pl.ds(2 * pair_at(turn) + e, 1), :] for e in range(2)]
     for e in range(2):
         tables[e][...] = table_of(rows[e])
     datt = datt_ref[...]
@@ -517,7 +596,7 @@
         jnp.concatenate([proj_ref[:, 256 * e : 256 * e + 128], middle[e]], axis=1)
         for e in range(2)
     ]
-    picked = [dot_tn(tables[e][...], sources[e]).astype(bf) for e in range(2)]
+    picked = [dot_nn(turned_table_of(rows[e]), sources[e]).astype(bf) for e in range(2)]
     for e in range(2):
         qk, dv = picked[e][:, 0:128], picked[e][:, 128:256]
         key_low = jnp.where(low, half_roll(qk), zero)
@@ -534,7 +613,7 @@
             probs_low[e][sl, :] = probs.astype(bf)
             inner = jnp.sum(back * probs, axis=-1, keepdims=True)
             backs[e][sl, :] = (0.125 * (probs * (back - inner))).astype(bf)
-    placed = []
+    moved = []
     for e in range(2):
         qk, dv = picked[e][:, 0:128], picked[e][:, 128:256]
         queries, keys, values = [], [], []
@@ -547,10 +626,8 @@
         value = jnp.concatenate(values, 0)
         db_ref[0, 0, e : e + 1, :] = jnp.sum(key_query, axis=0, keepdims=True)
         db_ref[0, 0, 2 + e : 3 + e, :] = jnp.sum(value, axis=0, keepdims=True)
-        parts = [key_query.astype(bf), value.astype(bf)]
-        placed.append(
-            dot_nn(tables[e][...], jnp.concatenate(parts, axis=1))
-        )
+        moved.append(jnp.concatenate([key_query.astype(bf), value.astype(bf)], axis=1))
+    placed = [dot_nn(tables[e][...], moved[e]) for e in range(2)]
     key_queries = [placed[e][:, 0:128] for e in range(2)]
     turned = [pltpu.roll(t, DH, 1) for t in key_queries]
     query = jnp.where(low, turned[0], key_queries[1]).astype(bf)
@@ -610,7 +687,7 @@
                 pl.BlockSpec((LEN, D), lambda i, s, n: (s, 0)),
                 own(384),
                 own(128),
-                pl.BlockSpec((1, 1, 2, LEN), lambda i, s, n: (s, pair_at(i), 0, 0)),
+                pl.BlockSpec((1, H, LEN), lambda i, s, n: (s, 0, 0)),
             ]
             + [pl.BlockSpec(memory_space=pl.ANY)] * 3,
             out_specs=[own(128)] * 3
@@ -623,7 +700,7 @@
             + [pltpu.VMEM((LEN, 128), f32)] * 4
             + [pltpu.VMEM((LEN, 128), bf)] * 4
             + [pltpu.VMEM((D, 384), f32), pltpu.VMEM((shards,) + part, bf)]
-            + sum([reduce_scratch(shapes[k], shards, reps) for k in "dug"], []),
+            + sum([reduce_scratch(shapes[k], shards, reps, k == "u") for k in "dug"], []),
         ),
         out_shape=[jax.ShapeDtypeStruct((tokens, D), bf)] * 3
         + [
@@ -748,28 +825,33 @@
     n=len(shapes)
     grads,out_ref,sums,scratch=refs[:n],refs[n],refs[n+1:2*n+1],refs[2*n+1:]
     place=Place(shards,reps); step=pl.program_id(0)
-    end=follow(LAST_PLAN,{"r":Reduce(place,grads,sums,scratch)},step,pl.num_programs(0)-1,lambda: meet(place,True))
+    size=len(reduce_scratch(shapes[1:],shards,reps))
+    jobs={"a":Reduce(place,grads[1:],sums[1:],scratch[:size]),"b":Reduce(place,grads[:1],sums[:1],scratch[size:],True)}
+    end=follow(LAST_PLAN,jobs,step,pl.num_programs(0)-1,lambda: meet(place,True))
     out_ref[...]=bs_ref[...]+dot_nt(dq_ref[...],w_ref[:,0:D])+dot_nt(dk_ref[...],w_ref[:,D:2*D])+dot_nt(dv_ref[...],w_ref[:,2*D:3*D])
     end()
 def input_grad(back_sum,dq,dk,dv,weight,grads,shards,reps,collective_id):
-    rows=back_sum.shape[0]//4
+    rows=back_sum.shape[0]//8
     tile=pl.BlockSpec((rows,D),lambda i:(i,0))
     anywhere=[pl.BlockSpec(memory_space=pl.ANY)]*len(grads)
     shapes=[g.shape[1:] for g in grads]
-    return pl.pallas_call(partial(input_grad_body,shards,reps,shapes),grid=(4,),
+    return pl.pallas_call(partial(input_grad_body,shards,reps,shapes),grid=(8,),
         in_specs=[tile]*4+[pl.BlockSpec((D,3*D),lambda i:(0,0),pipeline_mode=pl.Buffered(1))]+anywhere,
         out_specs=[tile]+anywhere,
         out_shape=[jax.ShapeDtypeStruct(back_sum.shape,f32)]+result_shapes(shapes),
-        scratch_shapes=reduce_scratch(shapes,shards,reps),
+        scratch_shapes=reduce_scratch(shapes[1:],shards,reps)+reduce_scratch(shapes[:1],shards,reps,True),
         compiler_params=pltpu.CompilerParams(vmem_limit_bytes=50<<20,collective_id=collective_id,has_side_effects=True),name="input_grad")(back_sum,dq,dk,dv,weight,*grads)
 
 
-WIDE = 4096
-
-
-def shard_vectors(vectors):
-    row = jnp.concatenate(vectors)
-    return jnp.pad(row, (0, WIDE - row.shape[0])).reshape(16, 256)
+def as_rows(row):
+    filled = -(-row.shape[-1] // 128)
+    row = jnp.pad(row, ((0, 0), (0, filled * 128 - row.shape[-1])))
+    return jnp.pad(row.reshape(-1, filled, 128), ((0, 0), (0, 0), (0, 128)))
+
+
+def pack_vectors(vectors):
+    rows = jnp.concatenate([as_rows(v) for v in vectors], axis=1)
+    return jnp.pad(rows, ((0, 0), (0, 16 - rows.shape[1]), (0, 0)))
 
 
 def local(
@@ -797,8 +879,10 @@
     seqs = hidden.shape[0]
     tokens = seqs * LEN
     part = D // shards
-    vectors = shard_vectors(
-        (
+    vectors = pack_vectors(
+        [
+            v[None]
+            for v in (
             query_bias,
             value_bias,
             out_bias,
@@ -808,25 +892,24 @@
             norm2_gain,
             norm2_bias,
             up_bias,
-        )
-    )
+            )
+        ]
+    )[0]
     in_w, vectors = gather_now((input_weight, vectors), shards, reps, 1)
     in_w = in_w.reshape(D, 3 * D)
-    vectors = vectors.reshape(shards, WIDE).astype(f32)
-    table = vectors[:, : 8 * part].reshape(shards, 8, part).transpose(1, 0, 2).reshape(8, D)
+    vectors = vectors.astype(f32)
+    table = vectors[:, :8, :part].transpose(1, 0, 2).reshape(8, D)
     bias_all = jnp.concatenate([table[0], jnp.zeros((D,), f32), table[1]])[None]
     norm_rows = jnp.concatenate([table[2:], table[:2]])
-    up_b = vectors[:, 8 * part : 8 * part + FF // shards].reshape(1, FF)
+    up_b = vectors[:, 8:, :128].reshape(shards, -1)[:, : FF // shards].reshape(1, FF)
 
     flat = hidden.reshape(tokens, D)
-    rounded = flat.astype(bf)
-    rows = clusters.reshape(seqs, PAIRS, 2, LEN)
-    attended, proj, up_w, down_w, out_w = attention_forward(
+    attended, proj, rounded, up_w, down_w, out_w = attention_forward(
         lengths,
-        rounded,
+        flat,
         in_w,
         bias_all,
-        rows,
+        clusters,
         (up_weight, down_weight, out_weight),
         shards,
         reps,
@@ -863,7 +946,7 @@
         rounded,
         proj,
         back_attended,
-        rows,
+        clusters,
         [g.reshape(shards, -1, g.shape[-1]) for g in (down_g, up_g, out_g)],
         shards,
         reps,
@@ -873,27 +956,23 @@
     query_sum = bias_sums[:, 0:2, DH:].reshape(D)
     value_sum = jnp.concatenate([bias_sums[:, 2, :DH], bias_sums[:, 3, DH:]], axis=1).reshape(D)
     table = jnp.concatenate([query_sum[None], value_sum[None], norm_sums[:6]])
-    small = jnp.concatenate(
-        [
-            table.reshape(8, shards, part).transpose(1, 0, 2).reshape(shards, 8 * part),
-            up_b_sum.reshape(shards, FF // shards),
-        ],
-        axis=1,
-    ).astype(bf)
-    small = jnp.pad(small, ((0, 0), (0, WIDE - small.shape[1]))).reshape(shards, 16, 256)
+    table = table.reshape(8, shards, part)
+    small = pack_vectors(
+        [table[i].astype(bf) for i in range(8)] + [up_b_sum.reshape(shards, -1).astype(bf)]
+    )
     back_input, *in_s, small_s = input_grad(
         back_sum,
         dq,
         dk,
         dv,
         in_w,
-        [in_g[g].reshape(shards, part, D) for g in range(1, PAIRS // 2)] + [small],
+        [in_g[2].reshape(shards, part, D), in_g[1].reshape(shards, part, D), small],
         shards,
         reps,
         4,
     )
     back_input = back_input.reshape(seqs, LEN, D)
-    in_s = [in_first] + in_s
+    in_s = [in_first, in_s[1], in_s[0]]
     in_s = jnp.concatenate(
         [
             in_s[g][c, :, 128 * t : 128 * t + 128]
@@ -907,8 +986,8 @@
     def whole(halves):
         return jnp.concatenate([halves[0], halves[1]], axis=1)
 
-    small_s = whole(small_s).reshape(WIDE)
-    vec = [small_s[i * part : (i + 1) * part] for i in range(8)]
+    small_s = small_s[0]
+    vec = [small_s[i, :part] for i in range(8)]
     return (
         result.reshape(seqs, LEN, D),
         back_input,
@@ -920,7 +999,7 @@
         vec[3],
         vec[4],
         whole(up_s),
-        small_s[8 * part : 8 * part + FF // shards],
+        small_s[8:].reshape(-1)[: FF // shards],
         whole(down_s),
         vec[5],
         vec[6],

time: 398 us -> 364 us (0.915)
  Pallas kernels: 359 us -> 326 us
  local copies, waits for them, and re-layouts: 22.9 us -> 28.1 us
  other arithmetic: 9.35 us -> 4.45 us
    pallas_call x1, Pallas kernels: 117 us -> 92.1 us  [attention_backward(): pl.pallas_call(partial(attention_backward_body, shards, reps, shapes), gr...]
    pallas_call x1, Pallas kernels: 40.1 us -> 32 us  [input_grad(): pl.pallas_call(partial(input_grad_body, shards, reps, shapes), grid=(8,),...]
    concatenate x4 -> x2, local copies, waits for them, and re-layouts: 6.37 us -> 0.17 us  [pack_vectors(): rows = jnp.concatenate([as_rows(v) for v in vectors], axis=1)]
    unnamed x52, local copies, waits for them, and re-layouts: 11 us -> 16.5 us
    convert_element_type x1 -> x2, other arithmetic: 4.89 us -> 0.05 us  [the longest x1 0.04 us: local(): up_b_sum.reshape(shards, -1).astype(bf)]
    reshape x6 -> x24, local copies, waits for them, and re-layouts: 1.15 us -> 5.42 us  [as_rows(): return jnp.pad(row.reshape(-1, filled, 128), ((0, 0), (0, 0), (0, 128)))]
where the time goes in v5:
time: 364 us; the launch traced here: 360 us
  Pallas kernels  326 us (90%)
  local copies, waits for them, and re-layouts  28.1 us (8%)
  other arithmetic  4.45 us (1%)
    pallas_call x1, Pallas kernels, attention_backward(): pl.pallas_call(partial(attention_backward_body, shards, reps, shapes), gr...  92.1 us
    pallas_call x1, Pallas kernels, middle(): pl.pallas_call(partial(middle_body, T=T, chunk=chunk, sub_rows=sub_rows),...  74.5 us
    pallas_call x1, Pallas kernels, attention_forward(): pl.pallas_call(partial(attention_forward_body, shards, reps), grid_spec=p...  66.2 us
    pallas_call x3, Pallas kernels, weight_grad(): pl.pallas_call(weight_grad_body, grid=grid, in_specs=[pl.BlockSpec(lb, li...  35.2 us
    pallas_call x1, Pallas kernels, input_grad(): pl.pallas_call(partial(input_grad_body, shards, reps, shapes), grid=(8,),...  32 us
    pallas_call x1, Pallas kernels, gather_now(): pl.pallas_call(partial(gather_body, shards, reps, count), in_specs=[pl.Bl...  26.1 us
    unnamed x52, local copies, waits for them, and re-layouts  16.5 us

profile of v5, /device:TPU:9, one launch (start us, length us, event | category | flops | bytes accessed | tf_op | source)
XLA Modules:
  0.0 360.0 jit_solution(17511750321173993946)
XLA Ops:
  0.6 0.7 pad_bitcast_fusion.16
  1.3 0.7 pad_bitcast_fusion.15
  2.0 0.7 pad_bitcast_fusion.14
  2.7 0.7 pad_bitcast_fusion.13
  3.3 0.7 pad_bitcast_fusion.12
  4.0 0.7 pad_bitcast_fusion.11
  4.7 0.7 pad_bitcast_fusion.10
  5.3 0.7 pad_bitcast_fusion.9
  6.0 0.7 pad.132
  6.7 0.9 copy.75.row_ref.refs_4_
  7.7 0.0 copy-start.5
  7.7 1.0 copy-done.5
  8.7 26.1 %gather_weights.1 = (bf16[8,96,2304]{2,1,0:T(8,128)(2,1)S(1)}, bf16[8,16,256]{2,1,0:T(8,128)(2,1)S(1)}) custom-call(bf16[96,2304]{1,0:T(8,128)(2,1)S(1)} %copy-done.5, bf16[16,256]{1,0:T(8,128)(2,1)S(1)} %pad_bitcast_fusion.refs_1_), custom_call_target="tpu_custom_call" | custom-call | tf_op jit(solution)/shard_map/gather_weights/pallas_call | solution.py:179
  34.8 0.0 copy-start
  34.8 1.9 copy-done
  36.8 0.6 copy.90
  37.4 0.1 slice.209
  37.5 0.1 slice.207
  37.6 0.6 pad_maximum_fusion.3.vec_ref
  38.2 0.1 squeeze.125
  38.3 0.1 squeeze.126
  38.4 0.0 copy-start.3
  38.4 1.1 copy-done.3
  39.5 1.1 copy-done.4
  40.5 0.9 copy-done.6
  41.4 0.7 copy-done.7
  42.1 66.2 %attention_forward.1 = (bf16[2048,768]{1,0:T(8,128)(2,1)}, bf16[2048,2304]{1,0:T(8,128)(2,1)}, bf16[2048,768]{1,0:T(8,128)(2,1)}, bf16[8,96,3072]{2,1,0:T(8,128)...) custom-call(s32[2]{0:T(128)S(1)} %copy-done.7, f32[2048,768]{1,0:T(8,128)} %bitcast.146, ...), custom_call_target="tpu_custom_call" | custom-call | tf_op jit(solution)/shard_map/attention_forward/pallas_call | solution.py:526
  108.3 0.0 copy-done.1
  108.3 0.0 copy-start.2
  108.3 1.0 copy-done.2
  109.3 74.5 %middle.1 = (f32[2048,768]{1,0:T(8,128)}, f32[2048,768]{1,0:T(8,128)}, bf16[2048,768]{1,0:T(8,128)(2,1)}, bf16[2048,3072]{1,0:T(8,128)(2,1)}, bf16[2048,3072]{1,...) custom-call(s32[2]{0:T(128)} %refs_0_.3, ...), custom_call_target="tpu_custom_call" | custom-call | tf_op jit(solution)/shard_map/middle/pallas_call | solution.py:798
  183.9 0.0 copy-start.11
  183.9 6.1 %out_weight_grad.1 = bf16[768,768]{1,0:T(8,128)(2,1)} custom-call(bf16[2048,768]{1,0:T(8,128)(2,1)} %get-tuple-element.48.a_ref.l_ref, bf16[2048,768]{1,0:T(8,128)(2,1)} %get-tuple-element.61.r_ref), custom_call_target="tpu_custom_call" | custom-call | flops 2415919104 | bytes 7471104 | tf_op jit(solution)/shard_map/out_weight_grad/pallas_call | solution.py:817
  190.1 0.1 slice_reduce_fusion.2
  190.1 0.1 convert_element_type.94
  190.2 0.1 convert_element_type.93
  190.3 0.1 convert_element_type.92
  190.4 0.1 convert_element_type.91
  190.5 0.1 convert_element_type.90
  190.6 0.1 convert_element_type.89
  190.8 14.5 %down_weight_grad.1 = bf16[3072,768]{1,0:T(8,128)(2,1)} custom-call(bf16[2048,3072]{1,0:T(8,128)(2,1)} %get-tuple-element.57.l_ref, bf16[2048,768]{1,0:T(8,128)(2,1)} %get-tuple-element.58.r_ref), custom_call_target="tpu_custom_call" | custom-call | flops 9663676416 | bytes 20447232 | tf_op jit(solution)/shard_map/down_weight_grad/pallas_call | solution.py:817
  205.4 14.6 %up_weight_grad.1 = bf16[768,3072]{1,0:T(8,128)(2,1)} custom-call(bf16[2048,768]{1,0:T(8,128)(2,1)} %get-tuple-element.59.l_ref, bf16[2048,3072]{1,0:T(8,128)(2,1)} %get-tuple-element.60.r_ref), custom_call_target="tpu_custom_call" | custom-call | flops 9663676416 | bytes 20447232 | tf_op jit(solution)/shard_map/up_weight_grad/pallas_call | solution.py:817
  220.0 92.1 %attention_backward.1 = (bf16[2048,768]{1,0:T(8,128)(2,1)}, bf16[2048,768]{1,0:T(8,128)(2,1)}, bf16[2048,768]{1,0:T(8,128)(2,1)}, bf16[3,768,768]{2,1,0:T(8,128)...) custom-call(s32[2]{0:T(128)} %refs_0_.3, ...), custom_call_target="tpu_custom_call" | custom-call | tf_op jit(solution)/shard_map/attention_backward/pallas_call | solution.py:681
  312.1 0.8 reduce_sum.9
  312.8 0.1 slice.265
  312.9 0.1 convert_element_type.87
  313.0 0.1 fusion.1
  313.1 0.1 pad_maximum_fusion.5
  313.2 0.1 convert_element_type.88
  313.3 0.1 concatenate.33
  313.5 1.1 slice_bitcast_fusion.5
  314.6 0.7 pad_maximum_fusion.2
  315.3 0.8 bitcast_dynamic-update-slice_fusion.17
  316.1 1.3 slice_bitcast_fusion.3
  317.4 1.1 pad_maximum_fusion
  318.5 0.1 slice_bitcast_fusion.1
  318.6 1.1 pad_maximum_fusion.1
  319.7 0.6 copy-done.8
  320.3 0.2 fusion
  320.5 32.0 %input_grad.1 = (f32[2048,768]{1,0:T(8,128)}, f32[2,96,384]{2,1,0:T(8,128)S(1)}, f32[2,96,384]{2,1,0:T(8,128)S(1)}, f32[2,16,128]{2,1,0:T(8,128)S(1)}) custom-call(f32[2048,768]{1,0:T(8,128)} %get-tuple-element.53.bs_ref, bf16[2048,768]{1,0:T(8,128)(2,1)} %get-tuple-element.62.dq_ref, bf16[2048,768]{1,0:T(8,128)(2,1)} %get-tuple-element.63.dk_ref, ...), custom_call_target="tpu_custom_call" | custom-call | tf_op jit(solution)/shard_map/input_grad/pallas_call | solution.py:838
  352.7 0.0 copy-start.13
  352.7 0.6 slice_bitcast_fusion.10
  353.3 0.5 slice_bitcast_fusion.11
  353.9 5.9 %copy.113 = f32[2,1024,768]{2,1,0:T(8,128)} copy(f32[2,1024,768]{2,1,0:T(8,128)} %bitcast.148) | data formatting | bytes 12582912
  (84 shorter events, 0.6 us)
Async XLA Ops:
  7.7 1.0 copy-start.5
  8.7 99.6 %copy-start.1 = (s32[2,12,1024]{2,1,0:T(8,128)}, s32[2,12,1024]{2,1,0:T(8,128)S(1)}, u32[]{:S(2)}) copy-start(s32[2,12,1024]{2,1,0:T(8,128)S(1)} %copy.75.row_ref.refs_4_) | copy-start | bytes 294916
  34.8 1.9 copy-start
  38.4 1.1 copy-start.3
  39.5 1.1 copy-start.4
  40.5 0.9 copy-start.6
  41.4 0.7 copy-start.7
  108.3 1.0 copy-start.2
  183.9 6.1 %copy-start.12 = (f32[1,3072]{1,0:T(1,128)S(1)}, f32[1,3072]{1,0:T(1,128)}, u32[]{:S(2)}) copy-start(f32[1,3072]{1,0:T(1,128)} %get-tuple-element.68) | copy-start | bytes 36868
  183.9 6.2 %copy-start.11 = (f32[8,768]{1,0:T(8,128)S(1)}, f32[8,768]{1,0:T(8,128)}, u32[]{:S(2)}) copy-start(f32[8,768]{1,0:T(8,128)} %get-tuple-element.67) | copy-start | bytes 73732
  313.3 5.2 %copy-start.9 = (f32[2,384,384]{2,1,0:T(8,128)S(1)}, f32[2,384,384]{2,1,0:T(8,128)}, u32[]{:S(2)}) copy-start(f32[2,384,384]{2,1,0:T(8,128)} %get-tuple-element.76) | copy-start | bytes 3538948
  317.4 2.9 copy-start.8
  320.4 32.0 %copy-start.10 = (f32[2,96,384]{2,1,0:T(8,128)S(1)}, f32[2,96,384]{2,1,0:T(8,128)}, u32[]{:S(2)}) copy-start(f32[2,96,384]{2,1,0:T(8,128)} %get-tuple-element.70) | copy-start | bytes 884740
  352.7 7.1 %copy-start.13 = (f32[96,2304]{1,0:T(8,128)}, f32[96,2304]{1,0:T(8,128)S(1)}, u32[]{:S(2)}) copy-start(f32[96,2304]{1,0:T(8,128)S(1)} %bitcast_dynamic-update-slice_fusion) | copy-start | bytes 2654212

commit v6 on v5

--- a/solution.py
+++ b/solution.py
@@ -532,7 +532,7 @@
             + [column(part) for part in range(3)]
             + [column_b(part) for part in range(3)]
             + [pl.BlockSpec((1, H, LEN), lambda s, h, n: (s, 0, 0))]
-            + [pl.BlockSpec(memory_space=pltpu.VMEM)] * 3,
+            + [pl.BlockSpec(memory_space=pl.ANY)] * 3,
             out_specs=[
                 pl.BlockSpec((LEN, 128), lambda s, h, n: (s, h)),
                 pl.BlockSpec((LEN, 384), lambda s, h, n: (s, h)),
@@ -806,19 +806,38 @@
         name="middle")(lengths,hidden,att,ct,ow,uw,dw,vec,ub)
 
 
-def weight_grad_body(l_ref,r_ref,out_ref):
-    out_ref[...]=dot_tn(l_ref[...],r_ref[...]).astype(bf)
-def weight_grad(left,right,block,name,columns=False):
-    K,M=left.shape; N=right.shape[1]
-    if columns:
-        grid,lb,rb,ob,li,ri,oi=(N//block,),(K,M),(K,block),(M,block),(lambda i:(0,0)),(lambda i:(0,i)),(lambda i:(0,i))
-    else:
-        grid,lb,rb,ob,li,ri,oi=(M//block,),(K,block),(K,N),(block,N),(lambda i:(0,i)),(lambda i:(0,0)),(lambda i:(i,0))
-    return pl.pallas_call(weight_grad_body,grid=grid,
-        in_specs=[pl.BlockSpec(lb,li),pl.BlockSpec(rb,ri)],out_specs=pl.BlockSpec(ob,oi),
-        out_shape=jax.ShapeDtypeStruct((M,N),bf),
-        cost_estimate=pl.CostEstimate(flops=2*K*M*N,bytes_accessed=2*(K*M+K*N+M*N),transcendentals=0),
-        compiler_params=pltpu.CompilerParams(vmem_limit_bytes=60<<20),name=name)(left,right)
+def weight_grads_body(act,d2,low,pre,att,sl,down_ref,up_ref,out_ref,left,right,left_sem,right_sem):
+    i=pl.program_id(0)
+    def block(ref,j):
+        return ref if ref.shape[1]==D else ref.at[:,j*D:(j+1)*D]
+    def fetch(ref,j,slot,to_left):
+        return pltpu.make_async_copy(block(ref,j),(left if to_left else right).at[slot],(left_sem if to_left else right_sem).at[slot])
+    loads={0:((act,0,0,True),(d2,0,0,False),(act,1,1,True)),1:((act,2,0,True),(pre,0,1,False)),2:((act,3,1,True),),
+           3:((low,0,0,True),),4:((pre,1,0,False),(att,0,1,True)),5:((pre,2,1,False),),6:((pre,3,0,False),),7:((sl,0,1,False),)}
+    needs={0:((act,0,0,True),(d2,0,0,False)),1:((act,1,1,True),),2:((act,2,0,True),),3:((act,3,1,True),),4:((low,0,0,True),(pre,0,1,False)),
+           5:((pre,1,0,False),),6:((pre,2,1,False),),7:((pre,3,0,False),),8:((att,0,1,True),(sl,0,1,False))}
+    for k in range(9):
+        def move(k=k):
+            for one in loads.get(k,()): fetch(*one).start()
+            for one in needs[k]: fetch(*one).wait()
+        pl.when(i==k)(move)
+    l=jnp.where(i<4,lax.rem(i,2),jnp.where(i<8,0,1))
+    r=jnp.where(i<4,0,jnp.where(i<8,lax.rem(i+1,2),1))
+    grad=dot_tn(left[l],right[r]).astype(bf)
+    @pl.when(i<4)
+    def _(): down_ref[...]=grad
+    @pl.when(jnp.logical_and(i>=4,i<8))
+    def _(): up_ref[...]=grad
+    @pl.when(i==8)
+    def _(): out_ref[...]=grad
+def weight_grads(act,d2,low,pre,att,sl):
+    tokens=act.shape[0]
+    return pl.pallas_call(weight_grads_body,grid=(9,),
+        in_specs=[pl.BlockSpec(memory_space=pl.ANY)]*6,
+        out_specs=[pl.BlockSpec((D,D),lambda i:(jnp.minimum(i,3),0)),pl.BlockSpec((D,D),lambda i:(0,jnp.clip(i-4,0,3))),pl.BlockSpec((D,D),lambda i:(0,0))],
+        out_shape=[jax.ShapeDtypeStruct((FF,D),bf),jax.ShapeDtypeStruct((D,FF),bf),jax.ShapeDtypeStruct((D,D),bf)],
+        scratch_shapes=[pltpu.VMEM((2,tokens,D),bf),pltpu.VMEM((2,tokens,D),bf),pltpu.SemaphoreType.DMA((2,)),pltpu.SemaphoreType.DMA((2,))],
+        compiler_params=pltpu.CompilerParams(vmem_limit_bytes=60<<20),name="weight_grads")(act,d2,low,pre,att,sl)
 
 
 def input_grad_body(shards,reps,shapes,bs_ref,dq_ref,dk_ref,dv_ref,w_ref,*refs):
@@ -847,6 +866,24 @@
     filled = -(-row.shape[-1] // 128)
     row = jnp.pad(row, ((0, 0), (0, filled * 128 - row.shape[-1])))
     return jnp.pad(row.reshape(-1, filled, 128), ((0, 0), (0, 0), (0, 128)))
+
+
+def pack_body(*refs):
+    *ins, out = refs
+    rows = []
+    for ref in ins:
+        value = ref[...].astype(f32)
+        for at in range(0, value.shape[0], 128):
+            part = value[at : at + 128].reshape(1, -1)
+            rows.append(jnp.pad(part, ((0, 0), (0, 256 - part.shape[1]))))
+    rows.append(jnp.zeros((16 - len(rows), 256), f32))
+    out[...] = jnp.concatenate(rows, axis=0).astype(bf)
+
+
+def pack_shards(vectors):
+    return pl.pallas_call(
+        pack_body, out_shape=jax.ShapeDtypeStruct((16, 256), bf), name="pack_vectors"
+    )(*vectors)
 
 
 def pack_vectors(vectors):
@@ -879,10 +916,8 @@
     seqs = hidden.shape[0]
     tokens = seqs * LEN
     part = D // shards
-    vectors = pack_vectors(
-        [
-            v[None]
-            for v in (
+    vectors = pack_shards(
+        (
             query_bias,
             value_bias,
             out_bias,
@@ -892,9 +927,8 @@
             norm2_gain,
             norm2_bias,
             up_bias,
-            )
-        ]
-    )[0]
+        )
+    )
     in_w, vectors = gather_now((input_weight, vectors), shards, reps, 1)
     in_w = in_w.reshape(D, 3 * D)
     vectors = vectors.astype(f32)
@@ -938,9 +972,9 @@
         norm_rows,
         up_b,
     )
-    down_g = weight_grad(activated, second_low, D, "down_weight_grad")
-    up_g = weight_grad(first_low, pre_low, D, "up_weight_grad", True)
-    out_g = weight_grad(attended, sum_low, D // 2, "out_weight_grad")
+    down_g, up_g, out_g = weight_grads(
+        activated, second_low, first_low, pre_low, attended, sum_low
+    )
     dq, dk, dv, in_g, bias_sums, down_s, up_s, out_s, in_first = attention_backward(
         lengths,
         rounded,

time: 364 us -> 345 us (0.948)
  Pallas kernels: 326 us -> 310 us
  local copies, waits for them, and re-layouts: 28.1 us -> 22.7 us
    pallas_call x1, Pallas kernels: 74.5 us -> 62 us  [middle(): pl.pallas_call(partial(middle_body, T=T, chunk=chunk, sub_rows=sub_rows),...]
    reshape x24 -> x16, local copies, waits for them, and re-layouts: 5.42 us -> 0.13 us  [as_rows(): return jnp.pad(row.reshape(-1, filled, 128), ((0, 0), (0, 0), (0, 128)))]
    pallas_call x3 -> x2, Pallas kernels: 35.2 us -> 31.6 us  [the longest x1 30.1 us: weight_grads(): pl.pallas_call(weight_grads_body, grid=(9,), in_specs=[pl.BlockSpec(memor...]
    unnamed x52 -> x50, local copies, waits for them, and re-layouts: 16.5 us -> 17.2 us
where the time goes in v6:
time: 345 us; the launch traced here: 340 us
  Pallas kernels  310 us (90%)
  local copies, waits for them, and re-layouts  22.7 us (7%)
  other arithmetic  5.89 us (2%)
    pallas_call x1, Pallas kernels, attention_backward(): pl.pallas_call(partial(attention_backward_body, shards, reps, shapes), gr...  91.9 us
    pallas_call x1, Pallas kernels, attention_forward(): pl.pallas_call(partial(attention_forward_body, shards, reps), grid_spec=p...  66.2 us
    pallas_call x1, Pallas kernels, middle(): pl.pallas_call(partial(middle_body, T=T, chunk=chunk, sub_rows=sub_rows),...  62 us
    pallas_call x1, Pallas kernels, input_grad(): pl.pallas_call(partial(input_grad_body, shards, reps, shapes), grid=(8,),...  32.5 us
    pallas_call x1, Pallas kernels, weight_grads(): pl.pallas_call(weight_grads_body, grid=(9,), in_specs=[pl.BlockSpec(memor...  30.1 us
    pallas_call x1, Pallas kernels, gather_now(): pl.pallas_call(partial(gather_body, shards, reps, count), in_specs=[pl.Bl...  26.1 us
    unnamed x50, local copies, waits for them, and re-layouts  17.2 us

profile of v6, /device:TPU:9, one launch (start us, length us, event | category | flops | bytes accessed | tf_op | source)
XLA Modules:
  0.0 339.9 jit_solution(10582912965906630284)
XLA Ops:
  0.6 1.4 pack_vectors.1.refs_1_
  2.1 0.9 copy.75.row_ref.refs_4_
  3.0 0.0 copy-start.5
  3.0 1.0 copy-done.5
  4.0 0.0 copy-start.7
  4.0 0.7 copy-done.7
  4.7 0.0 copy-start.1
  4.7 26.1 %gather_weights.1 = (bf16[8,96,2304]{2,1,0:T(8,128)(2,1)S(1)}, bf16[8,16,256]{2,1,0:T(8,128)(2,1)S(1)}) custom-call(bf16[96,2304]{1,0:T(8,128)(2,1)S(1)} %copy-done.5, bf16[16,256]{1,0:T(8,128)(2,1)S(1)} %copy-done.7), custom_call_target="tpu_custom_call" | custom-call | tf_op jit(solution)/shard_map/gather_weights/pallas_call | solution.py:179
  30.8 0.0 copy-start
  30.8 1.9 copy-done
  32.8 0.6 copy.90
  33.4 0.1 slice.209
  33.5 0.1 slice.207
  33.6 0.6 pad_maximum_fusion.3.vec_ref
  34.2 0.1 squeeze.121
  34.3 0.1 squeeze.122
  34.4 0.0 copy-start.3
  34.4 1.1 copy-done.3
  35.5 1.1 copy-done.4
  36.5 0.9 copy-done.6
  37.5 0.7 copy-done.8
  38.1 66.2 %attention_forward.1 = (bf16[2048,768]{1,0:T(8,128)(2,1)}, bf16[2048,2304]{1,0:T(8,128)(2,1)}, bf16[2048,768]{1,0:T(8,128)(2,1)}, bf16[8,96,3072]{2,1,0:T(8,128)...) custom-call(s32[2]{0:T(128)S(1)} %copy-done.8, f32[2048,768]{1,0:T(8,128)} %bitcast.119, ...), custom_call_target="tpu_custom_call" | custom-call | tf_op jit(solution)/shard_map/attention_forward/pallas_call | solution.py:526
  104.3 0.0 copy-done.1
  104.3 0.0 copy-start.2
  104.3 1.0 copy-done.2
  105.3 62.0 %middle.1 = (f32[2048,768]{1,0:T(8,128)}, f32[2048,768]{1,0:T(8,128)}, bf16[2048,768]{1,0:T(8,128)(2,1)}, bf16[2048,3072]{1,0:T(8,128)(2,1)}, bf16[2048,3072]{1,...) custom-call(s32[2]{0:T(128)} %refs_0_.5, ...), custom_call_target="tpu_custom_call" | custom-call | tf_op jit(solution)/shard_map/middle/pallas_call | solution.py:798
  167.3 0.7 convert_reduce_fusion
  168.1 0.7 convert.18
  168.9 0.1 slice_reduce_fusion.2
  168.9 0.1 convert_element_type.72
  169.0 0.1 convert_element_type.71
  169.1 0.1 convert_element_type.70
  169.2 0.1 convert_element_type.69
  169.4 0.1 convert_element_type.68
  169.5 0.1 convert_element_type.67
  169.7 30.1 %weight_grads.1 = (bf16[3072,768]{1,0:T(8,128)(2,1)}, bf16[768,3072]{1,0:T(8,128)(2,1)}, bf16[768,768]{1,0:T(8,128)(2,1)}) custom-call(bf16[2048,3072]{1,0:T(8,128)(2,1)} %get-tuple-element.60.act, bf16[2048,768]{1,0:T(8,128)(2,1)} %get-tuple-element.61.d2, bf16[2048,768]{1,0:T(8,128)(2,1)} %get-tuple-element.62.low, ...), custom_call_target="tpu_custom_call" | custom-call | tf_op jit(solution)/shard_map/weight_grads/pallas_call | solution.py:835
  199.8 91.9 %attention_backward.1 = (bf16[2048,768]{1,0:T(8,128)(2,1)}, bf16[2048,768]{1,0:T(8,128)(2,1)}, bf16[2048,768]{1,0:T(8,128)(2,1)}, bf16[3,768,768]{2,1,0:T(8,128)...) custom-call(s32[2]{0:T(128)} %refs_0_.5, ...), custom_call_target="tpu_custom_call" | custom-call | tf_op jit(solution)/shard_map/attention_backward/pallas_call | solution.py:681
  291.7 0.8 reduce_sum.9
  292.5 0.1 slice.265
  292.6 0.1 convert_element_type.65
  292.7 0.1 fusion.1
  292.7 0.1 pad_maximum_fusion.5
  292.8 0.1 convert_element_type.66
  293.0 0.0 copy-start.10
  293.0 0.1 concatenate.29
  293.1 1.1 slice_bitcast_fusion.5
  294.2 0.7 pad_maximum_fusion.2
  295.0 0.8 bitcast_dynamic-update-slice_fusion.17
  295.8 1.3 slice_bitcast_fusion.3
  297.1 0.0 copy-start.9
  297.1 1.1 pad_maximum_fusion
  298.2 0.0 copy-done.10
  298.2 0.1 slice_bitcast_fusion.1
  298.3 1.1 pad_maximum_fusion.1
  299.4 0.6 copy-done.9
  299.9 0.2 fusion
  300.1 0.0 copy-start.11
  300.1 32.5 %input_grad.1 = (f32[2048,768]{1,0:T(8,128)}, f32[2,96,384]{2,1,0:T(8,128)S(1)}, f32[2,96,384]{2,1,0:T(8,128)S(1)}, f32[2,16,128]{2,1,0:T(8,128)S(1)}) custom-call(f32[2048,768]{1,0:T(8,128)} %get-tuple-element.56.bs_ref, bf16[2048,768]{1,0:T(8,128)(2,1)} %get-tuple-element.68.dq_ref, bf16[2048,768]{1,0:T(8,128)(2,1)} %get-tuple-element.69.dk_ref, ...), custom_call_target="tpu_custom_call" | custom-call | tf_op jit(solution)/shard_map/input_grad/pallas_call | solution.py:857
  332.6 0.0 copy-done.11
  332.9 0.0 copy-start.12
  332.9 0.6 slice_bitcast_fusion.10
  333.5 0.5 slice_bitcast_fusion.11
  334.0 5.9 %copy.113 = f32[2,1024,768]{2,1,0:T(8,128)} copy(f32[2,1024,768]{2,1,0:T(8,128)} %bitcast.121) | data formatting | bytes 12582912
  339.9 0.0 copy-done.12
  (62 shorter events, 0.5 us)
Async XLA Ops:
  3.0 1.0 copy-start.5
  4.0 0.7 copy-start.7
  4.7 99.6 %copy-start.1 = (s32[2,12,1024]{2,1,0:T(8,128)}, s32[2,12,1024]{2,1,0:T(8,128)S(1)}, u32[]{:S(2)}) copy-start(s32[2,12,1024]{2,1,0:T(8,128)S(1)} %copy.75.row_ref.refs_4_) | copy-start | bytes 294916
  30.8 1.9 copy-start
  34.4 1.1 copy-start.3
  35.5 1.1 copy-start.4
  36.5 0.9 copy-start.6
  37.5 0.7 copy-start.8
  104.3 1.0 copy-start.2
  293.0 5.2 %copy-start.10 = (f32[2,384,384]{2,1,0:T(8,128)S(1)}, f32[2,384,384]{2,1,0:T(8,128)}, u32[]{:S(2)}) copy-start(f32[2,384,384]{2,1,0:T(8,128)} %get-tuple-element.82) | copy-start | bytes 3538948
  297.1 2.9 copy-start.9
  300.1 32.6 %copy-start.11 = (f32[2,96,384]{2,1,0:T(8,128)S(1)}, f32[2,96,384]{2,1,0:T(8,128)}, u32[]{:S(2)}) copy-start(f32[2,96,384]{2,1,0:T(8,128)} %get-tuple-element.76) | copy-start | bytes 884740
  332.9 7.1 %copy-start.12 = (f32[96,2304]{1,0:T(8,128)}, f32[96,2304]{1,0:T(8,128)S(1)}, u32[]{:S(2)}) copy-start(f32[96,2304]{1,0:T(8,128)S(1)} %bitcast_dynamic-update-slice_fusion) | copy-start | bytes 2654212

commit v7 on v6

--- a/solution.py
+++ b/solution.py
@@ -194,7 +194,7 @@
         out+=[pltpu.VMEM((S,r,n),bf),pltpu.VMEM((S,r,n),bf),pltpu.VMEM((max(Y-1,1),ROWS,m,n),bf),
               pltpu.VMEM((ROWS+1,m,n),bf),pltpu.VMEM((S+1,m,n) if x_first else (X,r,n),bf),pltpu.VMEM((2,r,n),f32)]
     dma=pltpu.SemaphoreType.DMA
-    return out+[dma((A,S)),dma((A,S)),dma((A,S)),dma((A,Y,ROWS)),dma((A,Y,ROWS)),dma((A,ROWS+1)),dma((A,ROWS+1)),dma((A,S+X)),dma((A,S+X)),dma((A,)),dma((A,)),dma((A,))]
+    return out+[dma((A,S)),dma((A,S)),dma((A,S)),dma((A,Y,ROWS)),dma((A,Y,ROWS)),dma((A,ROWS+1)),dma((A,ROWS+1)),dma((A,S+X)),dma((A,S+X)),dma((A,)),dma((A,)),dma((A,2))]
 class Reduce:
     def __init__(self,place,ins,outs,scratch,x_first=False):
         self.p=place; self.ins=ins; self.outs=outs; A=len(ins); self.A=range(A)
@@ -225,9 +225,9 @@
             block(pl.ds(pl.multiple_of(i*step,16),step))
             return 0
         lax.fori_loop(0,rows//step,body,0)
-    def begin(self):
-        p=self.p
-        for k in list(range(1,p.Y))+[0]:
+    def begin(self,ks=None):
+        p=self.p
+        for k in (list(range(1,p.Y)) if ks is None else ks):
             for d in ORDER:
                 for a in self.A:
                     H,Rc=self.bufs[a][0:2]
@@ -344,31 +344,33 @@
         for a in self.A:
             F=self.bufs[a][5]
             self.send(lambda a=a,F=F: (None,self.copy(F.at[p.core],F.at[p.core],self.end_s.at[a],self.end_r.at[a],p.other_core())))
+    def result(self,a,core):
+        F=self.bufs[a][5]; n=F.shape[2]
+        return pltpu.make_async_copy(F.at[core],self.outs[a].at[:,core*n:(core+1)*n],self.out_s.at[a,core])
     def finish(self):
         p=self.p
         for a in self.A:
-            F=self.bufs[a][5]; ref=F.at[1-p.core]
+            ref=self.bufs[a][5].at[1-p.core]
             self.copy(ref,ref,self.end_s.at[a],self.end_r.at[a],p.other_core()).wait_recv()
-            pltpu.make_async_copy(F,self.outs[a],self.out_s.at[a]).start()
+            for core in range(2): self.result(a,core).start()
         for make in self.sent:
             cond,desc=make()
             when(cond,desc.wait_send)
-        for a in self.A: pltpu.make_async_copy(self.bufs[a][5],self.outs[a],self.out_s.at[a]).wait()
-    def run(self,what,*args): getattr(self,what)(*args)
+        for a in self.A:
+            for core in range(2): self.result(a,core).wait()
 def result_shapes(shapes):
-    return [jax.ShapeDtypeStruct((2,r,c//2),f32) for r,c in shapes]
+    return [jax.ShapeDtypeStruct((r,c),f32) for r,c in shapes]
 
 GATHER_PLAN = {
     0: (("u", "begin"), ("d", "begin")),
     2: (("u", "wave", 1),),
-    3: (("d", "wave", 1), ("u", "across", 0), ("d", "across", 0)),
-    4: (("u", "wave", 2),),
-    5: (("d", "wave", 2),),
-    6: (("u", "across", 1), ("d", "over", 0)),
-    7: (("u", "wave", 3),),
-    8: (("d", "wave", 3), ("d", "across", 1)),
-    9: (("u", "across", 2), ("u", "across", 3)),
-    10: (("d", "across", 2), ("d", "across", 3), ("d", "over", 1)),
+    3: (("d", "wave", 1), ("u", "across", 0)),
+    4: (("u", "wave", 2), ("d", "across", 0)),
+    6: (("d", "wave", 2),),
+    7: (("u", "wave", 3), ("u", "across", 1)),
+    8: (("d", "wave", 3), ("d", "across", 1), ("d", "over", 0)),
+    10: (("u", "across", 2), ("u", "across", 3), ("d", "across", 2), ("d", "across", 3)),
+    11: (("d", "over", 1),),
     100: (("d", "over", 2), ("d", "over", 3), ("u", "finish"), ("d", "finish")),
 }
 
@@ -378,33 +380,27 @@
 
 
 REDUCE_PLAN = {
-    0: (("d", "begin"), ("u", "begin")),
-    1: each("d", "to_y"),
-    2: tuple(("u", "to_pair", 1, d) for d in ORDER) + each("d", "own_y"),
-    3: tuple(("u", "to_pair", 0, d) for d in ORDER) + (("d", "line", 3),),
-    4: (("g", "begin"), ("d", "line", 0)),
-    5: each("u", "to_y") + (("d", "line", 2), ("d", "relay", 3, 1)),
-    6: each("g", "to_y") + each("g", "own_y") + (("d", "line", 1), ("d", "relay", 0, 1)),
-    7: (("d", "relay", 3, 2), ("d", "relay", 2, 1), ("u", "own_y", 3), ("u", "own_y", 0)),
-    8: (("d", "relay", 0, 2), ("d", "relay", 1, 1), ("u", "own_y", 2), ("u", "own_y", 1))
-    + (("u", "line", 3), ("u", "line", 0)),
-    9: (("d", "to_x"), ("u", "line", 2), ("u", "line", 1), ("u", "relay", 3, 1), ("u", "relay", 0, 1)),
-    10: (("d", "to_core"), ("u", "relay", 2, 1), ("u", "relay", 3, 2), ("u", "relay", 0, 2))
-    + each("g", "line"),
-    11: (("u", "relay", 1, 1),) + each("g", "relay", 1),
-    100: each("g", "relay", 2)
-    + (
-        ("u", "to_x"),
-        ("g", "to_x"),
-        ("u", "to_core"),
-        ("g", "to_core"),
-        ("d", "finish"),
-        ("u", "finish"),
-        ("g", "finish"),
-    ),
+    0: (("d", "begin"), ("u", "begin"), ("d", "begin", (0,)), ("u", "begin", (0,))),
+    1: each("d", "to_y") + tuple(("u", "to_pair", 1, d) for d in ORDER),
+    2: tuple(("u", "to_pair", 0, d) for d in ORDER) + each("d", "own_y") + (("d", "line", 3),),
+    3: (("d", "line", 0), ("d", "relay", 3, 1)),
+    4: (("g", "begin"), ("g", "begin", (0,)))
+    + (("d", "line", 2), ("d", "relay", 0, 1), ("d", "relay", 3, 2))
+    + each("u", "to_y"),
+    5: (("d", "line", 1), ("d", "relay", 2, 1), ("d", "relay", 0, 2))
+    + each("g", "to_y")
+    + each("g", "own_y")
+    + (("u", "own_y", 3), ("u", "own_y", 0)),
+    6: (("d", "relay", 1, 1), ("u", "line", 3), ("u", "line", 0), ("u", "own_y", 2), ("u", "own_y", 1)),
+    7: (("d", "to_x"), ("u", "relay", 3, 1), ("u", "relay", 0, 1), ("u", "line", 2), ("u", "line", 1)),
+    8: (("d", "to_core"), ("u", "relay", 3, 2), ("u", "relay", 0, 2)) + each("g", "line"),
+    9: (("u", "relay", 2, 1), ("u", "relay", 1, 1)) + each("g", "relay", 1),
+    10: (("u", "to_x"),) + each("g", "relay", 2),
+    11: (("g", "to_x"), ("u", "to_core")),
+    100: (("g", "to_core"), ("d", "finish"), ("u", "finish"), ("g", "finish")),
 }
 LAST_PLAN = {
-    0: (("a", "begin"), ("b", "begin")),
+    0: (("a", "begin"), ("b", "begin"), ("a", "begin", (0,)), ("b", "begin", (0,))),
     1: each("a", "to_y"),
     2: tuple(("b", "to_pair", k, d) for k in (1, 0) for d in ORDER) + each("a", "own_y"),
     4: (("a", "line", 3), ("a", "line", 0)),
@@ -552,7 +548,7 @@
         ]
         + [jax.ShapeDtypeStruct((shards,) + a.shape, bf) for a in arrays],
         compiler_params=pltpu.CompilerParams(
-            vmem_limit_bytes=50 << 20, collective_id=collective_id, has_side_effects=True
+            vmem_limit_bytes=63 << 20, collective_id=collective_id, has_side_effects=True
         ),
         name="attention_forward",
     )(lengths, hidden, weight, weight, weight, bias, bias, bias, rows, *arrays)
@@ -1009,7 +1005,7 @@
     in_s = [in_first, in_s[1], in_s[0]]
     in_s = jnp.concatenate(
         [
-            in_s[g][c, :, 128 * t : 128 * t + 128]
+            in_s[g][:, 384 * c + 128 * t : 384 * c + 128 * t + 128]
             for t in range(3)
             for c in range(2)
             for g in range(PAIRS // 2)
@@ -1017,10 +1013,7 @@
         axis=1,
     )
 
-    def whole(halves):
-        return jnp.concatenate([halves[0], halves[1]], axis=1)
-
-    small_s = small_s[0]
+    small_s = small_s[:, :128]
     vec = [small_s[i, :part] for i in range(8)]
     return (
         result.reshape(seqs, LEN, D),
@@ -1028,13 +1021,13 @@
         in_s,
         vec[0],
         vec[1],
-        whole(out_s),
+        out_s,
         vec[2],
         vec[3],
         vec[4],
-        whole(up_s),
+        up_s,
         small_s[8:].reshape(-1)[: FF // shards],
-        whole(down_s),
+        down_s,
         vec[5],
         vec[6],
         vec[7],

time: 345 us -> 339 us (0.983)
    unnamed x50 -> x43, local copies, waits for them, and re-layouts: 17.2 us -> 15.5 us
where the time goes in v7:
time: 339 us; the launch traced here: 334 us
  Pallas kernels  309 us (91%)
  local copies, waits for them, and re-layouts  20.6 us (6%)
    pallas_call x1, Pallas kernels, attention_backward(): pl.pallas_call(partial(attention_backward_body, shards, reps, shapes), gr...  90.2 us
    pallas_call x1, Pallas kernels, attention_forward(): pl.pallas_call(partial(attention_forward_body, shards, reps), grid_spec=p...  65.5 us
    pallas_call x1, Pallas kernels, middle(): pl.pallas_call(partial(middle_body, T=T, chunk=chunk, sub_rows=sub_rows),...  62.1 us
    pallas_call x1, Pallas kernels, input_grad(): pl.pallas_call(partial(input_grad_body, shards, reps, shapes), grid=(8,),...  33.5 us
    pallas_call x1, Pallas kernels, weight_grads(): pl.pallas_call(weight_grads_body, grid=(9,), in_specs=[pl.BlockSpec(memor...  30.1 us
    pallas_call x1, Pallas kernels, gather_now(): pl.pallas_call(partial(gather_body, shards, reps, count), in_specs=[pl.Bl...  26.1 us
    unnamed x43, local copies, waits for them, and re-layouts  15.5 us

profile of v7, /device:TPU:9, one launch (start us, length us, event | category | flops | bytes accessed | tf_op | source)
XLA Modules:
  0.0 333.6 jit_solution(307548581275697785)
XLA Ops:
  0.6 1.4 pack_vectors.1.refs_1_
  2.1 1.6 copy.75.row_ref.refs_4_
  3.7 0.0 copy-start.1
  3.7 1.0 copy-done.1
  4.7 0.0 copy-start.2
  4.7 0.7 copy-done.2
  5.4 26.1 %gather_weights.1 = (bf16[8,96,2304]{2,1,0:T(8,128)(2,1)S(1)}, bf16[8,16,256]{2,1,0:T(8,128)(2,1)S(1)}) custom-call(bf16[96,2304]{1,0:T(8,128)(2,1)S(1)} %copy-done.1, bf16[16,256]{1,0:T(8,128)(2,1)S(1)} %copy-done.2), custom_call_target="tpu_custom_call" | custom-call | tf_op jit(solution)/shard_map/gather_weights/pallas_call | solution.py:179
  31.5 0.0 copy-start
  31.5 1.9 copy-done
  33.4 0.6 copy.90
  34.1 0.1 slice.196
  34.2 0.1 slice.194
  34.3 0.6 pad_maximum_fusion.vec_ref
  34.9 0.1 squeeze.46
  35.0 0.1 squeeze.47
  35.1 0.6 broadcast_in_dim.7.bq_ref.bk_ref.bv_ref
  35.7 65.5 %attention_forward.1 = (bf16[2048,768]{1,0:T(8,128)(2,1)}, bf16[2048,2304]{1,0:T(8,128)(2,1)}, bf16[2048,768]{1,0:T(8,128)(2,1)}, bf16[8,96,3072]{2,1,0:T(8,128)...) custom-call(s32[2]{0:T(128)} %refs_0_.5, f32[2048,768]{1,0:T(8,128)} %bitcast.68, ...), custom_call_target="tpu_custom_call" | custom-call | tf_op jit(solution)/shard_map/attention_forward/pallas_call | solution.py:522
  101.2 62.1 %middle.1 = (f32[2048,768]{1,0:T(8,128)}, f32[2048,768]{1,0:T(8,128)}, bf16[2048,768]{1,0:T(8,128)(2,1)}, bf16[2048,3072]{1,0:T(8,128)(2,1)}, bf16[2048,3072]{1,...) custom-call(s32[2]{0:T(128)} %refs_0_.5, ...), custom_call_target="tpu_custom_call" | custom-call | tf_op jit(solution)/shard_map/middle/pallas_call | solution.py:794
  163.3 0.7 convert_reduce_fusion
  164.0 0.7 convert.18
  164.8 0.1 slice_reduce_fusion.2
  164.9 0.1 convert_element_type.72
  165.0 0.1 convert_element_type.71
  165.1 0.1 convert_element_type.70
  165.2 0.1 convert_element_type.69
  165.3 0.1 convert_element_type.68
  165.4 0.1 convert_element_type.67
  165.6 30.1 %weight_grads.1 = (bf16[3072,768]{1,0:T(8,128)(2,1)}, bf16[768,3072]{1,0:T(8,128)(2,1)}, bf16[768,768]{1,0:T(8,128)(2,1)}) custom-call(bf16[2048,3072]{1,0:T(8,128)(2,1)} %get-tuple-element.60.act, bf16[2048,768]{1,0:T(8,128)(2,1)} %get-tuple-element.61.d2, bf16[2048,768]{1,0:T(8,128)(2,1)} %get-tuple-element.62.low, ...), custom_call_target="tpu_custom_call" | custom-call | tf_op jit(solution)/shard_map/weight_grads/pallas_call | solution.py:831
  195.7 90.2 %attention_backward.1 = (bf16[2048,768]{1,0:T(8,128)(2,1)}, bf16[2048,768]{1,0:T(8,128)(2,1)}, bf16[2048,768]{1,0:T(8,128)(2,1)}, bf16[3,768,768]{2,1,0:T(8,128)...) custom-call(s32[2]{0:T(128)} %refs_0_.5, ...), custom_call_target="tpu_custom_call" | custom-call | tf_op jit(solution)/shard_map/attention_backward/pallas_call | solution.py:677
  285.9 0.8 reduce_sum.9
  286.7 0.1 slice.245
  286.7 0.1 convert_element_type.65
  286.8 0.1 fusion.1
  286.9 0.1 pad_maximum_fusion.2
  287.0 0.1 convert_element_type.66
  287.2 0.1 concatenate.20
  287.3 0.8 slice_dynamic-update-slice_fusion.17
  288.1 1.8 fusion
  289.9 0.0 copy-start.5
  289.9 33.5 %input_grad.1 = (f32[2048,768]{1,0:T(8,128)}, f32[96,768]{1,0:T(8,128)S(1)}, f32[96,768]{1,0:T(8,128)S(1)}, f32[16,256]{1,0:T(8,128)S(1)}) custom-call(f32[2048,768]{1,0:T(8,128)} %get-tuple-element.56.bs_ref, bf16[2048,768]{1,0:T(8,128)(2,1)} %get-tuple-element.68.dq_ref, bf16[2048,768]{1,0:T(8,128)(2,1)} %get-tuple-element.69.dk_ref, ...), custom_call_target="tpu_custom_call" | custom-call | tf_op jit(solution)/shard_map/input_grad/pallas_call | solution.py:853
  323.5 0.0 copy-done.5
  323.7 0.0 copy-start.7
  323.7 0.6 slice_bitcast_fusion.3
  324.3 0.5 slice_bitcast_fusion.4
  324.9 0.0 copy-start.6
  324.9 0.0 copy-start.4
  324.9 6.0 %copy.116 = f32[2,1024,768]{2,1,0:T(8,128)} copy(f32[2,1024,768]{2,1,0:T(8,128)} %bitcast.70) | data formatting | bytes 12582912
  330.9 0.0 copy-done.7
  330.9 0.0 copy-done.6
  330.9 0.0 copy-start.3
  330.9 0.7 copy.117
  331.6 0.0 copy-done.4
  331.6 1.0 copy.118
  332.6 0.0 copy-done.3
  332.6 1.0 copy.119
  (57 shorter events, 0.4 us)
Async XLA Ops:
  3.7 1.0 copy-start.1
  4.7 0.7 copy-start.2
  31.5 1.9 copy-start
  289.9 33.6 %copy-start.5 = (f32[96,768]{1,0:T(8,128)S(1)}, f32[96,768]{1,0:T(8,128)}, u32[]{:S(2)}) copy-start(f32[96,768]{1,0:T(8,128)} %get-tuple-element.76) | copy-start | bytes 884740
  323.7 7.2 %copy-start.7 = (f32[96,2304]{1,0:T(8,128)}, f32[96,2304]{1,0:T(8,128)S(1)}, u32[]{:S(2)}) copy-start(f32[96,2304]{1,0:T(8,128)S(1)} %slice_dynamic-update-slice_fusion) | copy-start | bytes 2654212
  324.9 6.0 %copy-start.6 = (f32[96,768]{1,0:T(8,128)S(1)}, f32[96,768]{1,0:T(8,128)}, u32[]{:S(2)}) copy-start(f32[96,768]{1,0:T(8,128)} %get-tuple-element.125) | copy-start | bytes 884740
  324.9 6.7 %copy-start.4 = (f32[96,3072]{1,0:T(8,128)S(1)}, f32[96,3072]{1,0:T(8,128)}, u32[]{:S(2)}) copy-start(f32[96,3072]{1,0:T(8,128)} %get-tuple-element.129) | copy-start | bytes 3538948
  330.9 1.7 copy-start.3

commit v8 on v7

--- a/solution.py
+++ b/solution.py
@@ -839,11 +839,17 @@
 def input_grad_body(shards,reps,shapes,bs_ref,dq_ref,dk_ref,dv_ref,w_ref,*refs):
     n=len(shapes)
     grads,out_ref,sums,scratch=refs[:n],refs[n],refs[n+1:2*n+1],refs[2*n+1:]
+    weight,loaded=scratch[-2:]
+    load=lambda: pltpu.make_async_copy(w_ref,weight,loaded.at[0])
+    def ready():
+        load().start()
+        meet(place,True)
     place=Place(shards,reps); step=pl.program_id(0)
     size=len(reduce_scratch(shapes[1:],shards,reps))
-    jobs={"a":Reduce(place,grads[1:],sums[1:],scratch[:size]),"b":Reduce(place,grads[:1],sums[:1],scratch[size:],True)}
-    end=follow(LAST_PLAN,jobs,step,pl.num_programs(0)-1,lambda: meet(place,True))
-    out_ref[...]=bs_ref[...]+dot_nt(dq_ref[...],w_ref[:,0:D])+dot_nt(dk_ref[...],w_ref[:,D:2*D])+dot_nt(dv_ref[...],w_ref[:,2*D:3*D])
+    jobs={"a":Reduce(place,grads[1:],sums[1:],scratch[:size]),"b":Reduce(place,grads[:1],sums[:1],scratch[size:-2],True)}
+    end=follow(LAST_PLAN,jobs,step,pl.num_programs(0)-1,ready)
+    pl.when(step==0)(lambda: load().wait())
+    out_ref[...]=bs_ref[...]+dot_nt(dq_ref[...],weight[:,0:D])+dot_nt(dk_ref[...],weight[:,D:2*D])+dot_nt(dv_ref[...],weight[:,2*D:3*D])
     end()
 def input_grad(back_sum,dq,dk,dv,weight,grads,shards,reps,collective_id):
     rows=back_sum.shape[0]//8
@@ -851,10 +857,10 @@
     anywhere=[pl.BlockSpec(memory_space=pl.ANY)]*len(grads)
     shapes=[g.shape[1:] for g in grads]
     return pl.pallas_call(partial(input_grad_body,shards,reps,shapes),grid=(8,),
-        in_specs=[tile]*4+[pl.BlockSpec((D,3*D),lambda i:(0,0),pipeline_mode=pl.Buffered(1))]+anywhere,
+        in_specs=[tile]*4+[pl.BlockSpec(memory_space=pl.ANY)]+anywhere,
         out_specs=[tile]+anywhere,
         out_shape=[jax.ShapeDtypeStruct(back_sum.shape,f32)]+result_shapes(shapes),
-        scratch_shapes=reduce_scratch(shapes[1:],shards,reps)+reduce_scratch(shapes[:1],shards,reps,True),
+        scratch_shapes=reduce_scratch(shapes[1:],shards,reps)+reduce_scratch(shapes[:1],shards,reps,True)+[pltpu.VMEM((D,3*D),bf),pltpu.SemaphoreType.DMA((1,))],
         compiler_params=pltpu.CompilerParams(vmem_limit_bytes=50<<20,collective_id=collective_id,has_side_effects=True),name="input_grad")(back_sum,dq,dk,dv,weight,*grads)
 
 

time: 339 us -> 337 us (level)
  no operation moved by 1% of the time
where the time goes in v8:
time: 337 us; the launch traced here: 332 us
  Pallas kernels  307 us (91%)
  local copies, waits for them, and re-layouts  20.6 us (6%)
    pallas_call x1, Pallas kernels, attention_backward(): pl.pallas_call(partial(attention_backward_body, shards, reps, shapes), gr...  90.2 us
    pallas_call x1, Pallas kernels, attention_forward(): pl.pallas_call(partial(attention_forward_body, shards, reps), grid_spec=p...  65.5 us
    pallas_call x1, Pallas kernels, middle(): pl.pallas_call(partial(middle_body, T=T, chunk=chunk, sub_rows=sub_rows),...  62.1 us
    pallas_call x1, Pallas kernels, input_grad(): pl.pallas_call(partial(input_grad_body, shards, reps, shapes), grid=(8,),...  32 us
    pallas_call x1, Pallas kernels, weight_grads(): pl.pallas_call(weight_grads_body, grid=(9,), in_specs=[pl.BlockSpec(memor...  30.1 us
    pallas_call x1, Pallas kernels, gather_now(): pl.pallas_call(partial(gather_body, shards, reps, count), in_specs=[pl.Bl...  26.1 us
    unnamed x43, local copies, waits for them, and re-layouts  15.5 us

profile of v8, /device:TPU:9, one launch (start us, length us, event | category | flops | bytes accessed | tf_op | source)
XLA Modules:
  0.0 332.1 jit_solution(3970632805530569844)
XLA Ops:
  0.6 1.4 pack_vectors.1.refs_1_
  2.1 1.6 copy.75.row_ref.refs_4_
  3.7 0.0 copy-start.1
  3.7 1.0 copy-done.1
  4.7 0.0 copy-start.2
  4.7 0.7 copy-done.2
  5.4 26.1 %gather_weights.1 = (bf16[8,96,2304]{2,1,0:T(8,128)(2,1)S(1)}, bf16[8,16,256]{2,1,0:T(8,128)(2,1)S(1)}) custom-call(bf16[96,2304]{1,0:T(8,128)(2,1)S(1)} %copy-done.1, bf16[16,256]{1,0:T(8,128)(2,1)S(1)} %copy-done.2), custom_call_target="tpu_custom_call" | custom-call | tf_op jit(solution)/shard_map/gather_weights/pallas_call | solution.py:179
  31.5 0.0 copy-start
  31.5 1.9 copy-done
  33.4 0.6 copy.90
  34.1 0.1 slice.196
  34.2 0.1 slice.194
  34.3 0.6 pad_maximum_fusion.vec_ref
  34.9 0.1 squeeze.46
  35.0 0.1 squeeze.47
  35.1 0.6 broadcast_in_dim.7.bq_ref.bk_ref.bv_ref
  35.7 65.5 %attention_forward.1 = (bf16[2048,768]{1,0:T(8,128)(2,1)}, bf16[2048,2304]{1,0:T(8,128)(2,1)}, bf16[2048,768]{1,0:T(8,128)(2,1)}, bf16[8,96,3072]{2,1,0:T(8,128)...) custom-call(s32[2]{0:T(128)} %refs_0_.5, f32[2048,768]{1,0:T(8,128)} %bitcast.68, ...), custom_call_target="tpu_custom_call" | custom-call | tf_op jit(solution)/shard_map/attention_forward/pallas_call | solution.py:522
  101.2 62.1 %middle.1 = (f32[2048,768]{1,0:T(8,128)}, f32[2048,768]{1,0:T(8,128)}, bf16[2048,768]{1,0:T(8,128)(2,1)}, bf16[2048,3072]{1,0:T(8,128)(2,1)}, bf16[2048,3072]{1,...) custom-call(s32[2]{0:T(128)} %refs_0_.5, ...), custom_call_target="tpu_custom_call" | custom-call | tf_op jit(solution)/shard_map/middle/pallas_call | solution.py:794
  163.3 0.7 convert_reduce_fusion
  164.0 0.7 convert.18
  164.8 0.1 slice_reduce_fusion.2
  164.9 0.1 convert_element_type.72
  165.0 0.1 convert_element_type.71
  165.1 0.1 convert_element_type.70
  165.2 0.1 convert_element_type.69
  165.3 0.1 convert_element_type.68
  165.4 0.1 convert_element_type.67
  165.6 30.1 %weight_grads.1 = (bf16[3072,768]{1,0:T(8,128)(2,1)}, bf16[768,3072]{1,0:T(8,128)(2,1)}, bf16[768,768]{1,0:T(8,128)(2,1)}) custom-call(bf16[2048,3072]{1,0:T(8,128)(2,1)} %get-tuple-element.60.act, bf16[2048,768]{1,0:T(8,128)(2,1)} %get-tuple-element.61.d2, bf16[2048,768]{1,0:T(8,128)(2,1)} %get-tuple-element.62.low, ...), custom_call_target="tpu_custom_call" | custom-call | tf_op jit(solution)/shard_map/weight_grads/pallas_call | solution.py:831
  195.7 90.2 %attention_backward.1 = (bf16[2048,768]{1,0:T(8,128)(2,1)}, bf16[2048,768]{1,0:T(8,128)(2,1)}, bf16[2048,768]{1,0:T(8,128)(2,1)}, bf16[3,768,768]{2,1,0:T(8,128)...) custom-call(s32[2]{0:T(128)} %refs_0_.5, ...), custom_call_target="tpu_custom_call" | custom-call | tf_op jit(solution)/shard_map/attention_backward/pallas_call | solution.py:677
  285.9 0.8 reduce_sum.9
  286.7 0.1 slice.245
  286.7 0.1 convert_element_type.65
  286.8 0.1 fusion.1
  286.9 0.1 pad_maximum_fusion.2
  287.0 0.1 convert_element_type.66
  287.2 0.1 concatenate.20
  287.3 0.8 slice_dynamic-update-slice_fusion.17
  288.1 1.8 fusion
  289.9 0.0 copy-start.5
  289.9 32.0 %input_grad.1 = (f32[2048,768]{1,0:T(8,128)}, f32[96,768]{1,0:T(8,128)S(1)}, f32[96,768]{1,0:T(8,128)S(1)}, f32[16,256]{1,0:T(8,128)S(1)}) custom-call(f32[2048,768]{1,0:T(8,128)} %get-tuple-element.56.bs_ref, bf16[2048,768]{1,0:T(8,128)(2,1)} %get-tuple-element.68.dq_ref, bf16[2048,768]{1,0:T(8,128)(2,1)} %get-tuple-element.69.dk_ref, ...), custom_call_target="tpu_custom_call" | custom-call | tf_op jit(solution)/shard_map/input_grad/pallas_call | solution.py:859
  321.9 0.0 copy-done.5
  322.1 0.0 copy-start.7
  322.1 0.6 slice_bitcast_fusion.3
  322.8 0.5 slice_bitcast_fusion.4
  323.3 0.0 copy-start.6
  323.3 0.0 copy-start.4
  323.3 6.0 %copy.116 = f32[2,1024,768]{2,1,0:T(8,128)} copy(f32[2,1024,768]{2,1,0:T(8,128)} %bitcast.70) | data formatting | bytes 12582912
  329.3 0.0 copy-done.7
  329.3 0.0 copy-done.6
  329.3 0.0 copy-start.3
  329.3 0.7 copy.117
  330.0 0.0 copy-done.4
  330.0 1.0 copy.118
  331.1 0.0 copy-done.3
  331.1 1.0 copy.119
  (57 shorter events, 0.4 us)
Async XLA Ops:
  3.7 1.0 copy-start.1
  4.7 0.7 copy-start.2
  31.5 1.9 copy-start
  289.9 32.0 %copy-start.5 = (f32[96,768]{1,0:T(8,128)S(1)}, f32[96,768]{1,0:T(8,128)}, u32[]{:S(2)}) copy-start(f32[96,768]{1,0:T(8,128)} %get-tuple-element.76) | copy-start | bytes 884740
  322.1 7.2 %copy-start.7 = (f32[96,2304]{1,0:T(8,128)}, f32[96,2304]{1,0:T(8,128)S(1)}, u32[]{:S(2)}) copy-start(f32[96,2304]{1,0:T(8,128)S(1)} %slice_dynamic-update-slice_fusion) | copy-start | bytes 2654212
  323.3 6.0 %copy-start.6 = (f32[96,768]{1,0:T(8,128)S(1)}, f32[96,768]{1,0:T(8,128)}, u32[]{:S(2)}) copy-start(f32[96,768]{1,0:T(8,128)} %get-tuple-element.125) | copy-start | bytes 884740
  323.3 6.7 %copy-start.4 = (f32[96,3072]{1,0:T(8,128)S(1)}, f32[96,3072]{1,0:T(8,128)}, u32[]{:S(2)}) copy-start(f32[96,3072]{1,0:T(8,128)} %get-tuple-element.129) | copy-start | bytes 3538948
  329.3 1.7 copy-start.3

commit v9 on v8

--- a/solution.py
+++ b/solution.py
@@ -808,7 +808,7 @@
         return ref if ref.shape[1]==D else ref.at[:,j*D:(j+1)*D]
     def fetch(ref,j,slot,to_left):
         return pltpu.make_async_copy(block(ref,j),(left if to_left else right).at[slot],(left_sem if to_left else right_sem).at[slot])
-    loads={0:((act,0,0,True),(d2,0,0,False),(act,1,1,True)),1:((act,2,0,True),(pre,0,1,False)),2:((act,3,1,True),),
+    loads={0:((act,0,0,True),(d2,0,0,False)),1:((act,2,0,True),(pre,0,1,False)),2:((act,3,1,True),),
            3:((low,0,0,True),),4:((pre,1,0,False),(att,0,1,True)),5:((pre,2,1,False),),6:((pre,3,0,False),),7:((sl,0,1,False),)}
     needs={0:((act,0,0,True),(d2,0,0,False)),1:((act,1,1,True),),2:((act,2,0,True),),3:((act,3,1,True),),4:((low,0,0,True),(pre,0,1,False)),
            5:((pre,1,0,False),),6:((pre,2,1,False),),7:((pre,3,0,False),),8:((att,0,1,True),(sl,0,1,False))}
@@ -816,6 +816,7 @@
         def move(k=k):
             for one in loads.get(k,()): fetch(*one).start()
             for one in needs[k]: fetch(*one).wait()
+            if k==0: fetch(act,1,1,True).start()
         pl.when(i==k)(move)
     l=jnp.where(i<4,lax.rem(i,2),jnp.where(i<8,0,1))
     r=jnp.where(i<4,0,jnp.where(i<8,lax.rem(i+1,2),1))

time: 337 us -> 337 us (level)
  no operation moved by 1% of the time
where the time goes in v9:
time: 337 us; the launch traced here: 332 us
  Pallas kernels  307 us (91%)
  local copies, waits for them, and re-layouts  20.6 us (6%)
    pallas_call x1, Pallas kernels, attention_backward(): pl.pallas_call(partial(attention_backward_body, shards, reps, shapes), gr...  90.2 us
    pallas_call x1, Pallas kernels, attention_forward(): pl.pallas_call(partial(attention_forward_body, shards, reps), grid_spec=p...  65.5 us
    pallas_call x1, Pallas kernels, middle(): pl.pallas_call(partial(middle_body, T=T, chunk=chunk, sub_rows=sub_rows),...  62.1 us
    pallas_call x1, Pallas kernels, input_grad(): pl.pallas_call(partial(input_grad_body, shards, reps, shapes), grid=(8,),...  32 us
    pallas_call x1, Pallas kernels, weight_grads(): pl.pallas_call(weight_grads_body, grid=(9,), in_specs=[pl.BlockSpec(memor...  30.1 us
    pallas_call x1, Pallas kernels, gather_now(): pl.pallas_call(partial(gather_body, shards, reps, count), in_specs=[pl.Bl...  26.1 us
    unnamed x43, local copies, waits for them, and re-layouts  15.5 us

profile of v9, /device:TPU:9, one launch (start us, length us, event | category | flops | bytes accessed | tf_op | source)
XLA Modules:
  0.0 332.1 jit_solution(3248415218853881832)
XLA Ops:
  0.6 1.4 pack_vectors.1.refs_1_
  2.1 1.6 copy.75.row_ref.refs_4_
  3.7 0.0 copy-start.1
  3.7 1.0 copy-done.1
  4.7 0.0 copy-start.2
  4.7 0.7 copy-done.2
  5.4 26.1 %gather_weights.1 = (bf16[8,96,2304]{2,1,0:T(8,128)(2,1)S(1)}, bf16[8,16,256]{2,1,0:T(8,128)(2,1)S(1)}) custom-call(bf16[96,2304]{1,0:T(8,128)(2,1)S(1)} %copy-done.1, bf16[16,256]{1,0:T(8,128)(2,1)S(1)} %copy-done.2), custom_call_target="tpu_custom_call" | custom-call | tf_op jit(solution)/shard_map/gather_weights/pallas_call | solution.py:179
  31.5 0.0 copy-start
  31.5 1.9 copy-done
  33.4 0.6 copy.90
  34.1 0.1 slice.196
  34.2 0.1 slice.194
  34.3 0.6 pad_maximum_fusion.vec_ref
  34.9 0.1 squeeze.46
  35.0 0.1 squeeze.47
  35.1 0.6 broadcast_in_dim.7.bq_ref.bk_ref.bv_ref
  35.7 65.5 %attention_forward.1 = (bf16[2048,768]{1,0:T(8,128)(2,1)}, bf16[2048,2304]{1,0:T(8,128)(2,1)}, bf16[2048,768]{1,0:T(8,128)(2,1)}, bf16[8,96,3072]{2,1,0:T(8,128)...) custom-call(s32[2]{0:T(128)} %refs_0_.5, f32[2048,768]{1,0:T(8,128)} %bitcast.68, ...), custom_call_target="tpu_custom_call" | custom-call | tf_op jit(solution)/shard_map/attention_forward/pallas_call | solution.py:522
  101.2 62.1 %middle.1 = (f32[2048,768]{1,0:T(8,128)}, f32[2048,768]{1,0:T(8,128)}, bf16[2048,768]{1,0:T(8,128)(2,1)}, bf16[2048,3072]{1,0:T(8,128)(2,1)}, bf16[2048,3072]{1,...) custom-call(s32[2]{0:T(128)} %refs_0_.5, ...), custom_call_target="tpu_custom_call" | custom-call | tf_op jit(solution)/shard_map/middle/pallas_call | solution.py:794
  163.3 0.7 convert_reduce_fusion
  164.0 0.7 convert.18
  164.8 0.1 slice_reduce_fusion.2
  164.9 0.1 convert_element_type.72
  165.0 0.1 convert_element_type.71
  165.1 0.1 convert_element_type.70
  165.2 0.1 convert_element_type.69
  165.3 0.1 convert_element_type.68
  165.4 0.1 convert_element_type.67
  165.6 30.1 %weight_grads.1 = (bf16[3072,768]{1,0:T(8,128)(2,1)}, bf16[768,3072]{1,0:T(8,128)(2,1)}, bf16[768,768]{1,0:T(8,128)(2,1)}) custom-call(bf16[2048,3072]{1,0:T(8,128)(2,1)} %get-tuple-element.60.act, bf16[2048,768]{1,0:T(8,128)(2,1)} %get-tuple-element.61.d2, bf16[2048,768]{1,0:T(8,128)(2,1)} %get-tuple-element.62.low, ...), custom_call_target="tpu_custom_call" | custom-call | tf_op jit(solution)/shard_map/weight_grads/pallas_call | solution.py:832
  195.7 90.2 %attention_backward.1 = (bf16[2048,768]{1,0:T(8,128)(2,1)}, bf16[2048,768]{1,0:T(8,128)(2,1)}, bf16[2048,768]{1,0:T(8,128)(2,1)}, bf16[3,768,768]{2,1,0:T(8,128)...) custom-call(s32[2]{0:T(128)} %refs_0_.5, ...), custom_call_target="tpu_custom_call" | custom-call | tf_op jit(solution)/shard_map/attention_backward/pallas_call | solution.py:677
  285.9 0.8 reduce_sum.9
  286.6 0.1 slice.245
  286.7 0.1 convert_element_type.65
  286.8 0.1 fusion.1
  286.9 0.1 pad_maximum_fusion.2
  287.0 0.1 convert_element_type.66
  287.1 0.1 concatenate.20
  287.3 0.8 slice_dynamic-update-slice_fusion.17
  288.1 1.8 fusion
  289.8 0.0 copy-start.5
  289.9 32.0 %input_grad.1 = (f32[2048,768]{1,0:T(8,128)}, f32[96,768]{1,0:T(8,128)S(1)}, f32[96,768]{1,0:T(8,128)S(1)}, f32[16,256]{1,0:T(8,128)S(1)}) custom-call(f32[2048,768]{1,0:T(8,128)} %get-tuple-element.56.bs_ref, bf16[2048,768]{1,0:T(8,128)(2,1)} %get-tuple-element.68.dq_ref, bf16[2048,768]{1,0:T(8,128)(2,1)} %get-tuple-element.69.dk_ref, ...), custom_call_target="tpu_custom_call" | custom-call | tf_op jit(solution)/shard_map/input_grad/pallas_call | solution.py:860
  321.9 0.0 copy-done.5
  322.1 0.0 copy-start.7
  322.1 0.6 slice_bitcast_fusion.3
  322.7 0.5 slice_bitcast_fusion.4
  323.3 0.0 copy-start.6
  323.3 0.0 copy-start.4
  323.3 6.0 %copy.116 = f32[2,1024,768]{2,1,0:T(8,128)} copy(f32[2,1024,768]{2,1,0:T(8,128)} %bitcast.70) | data formatting | bytes 12582912
  329.3 0.0 copy-done.7
  329.3 0.0 copy-done.6
  329.3 0.0 copy-start.3
  329.3 0.7 copy.117
  330.0 0.0 copy-done.4
  330.0 1.0 copy.118
  331.0 0.0 copy-done.3
  331.0 1.0 copy.119
  (57 shorter events, 0.4 us)
Async XLA Ops:
  3.7 1.0 copy-start.1
  4.7 0.7 copy-start.2
  31.5 1.9 copy-start
  289.8 32.1 %copy-start.5 = (f32[96,768]{1,0:T(8,128)S(1)}, f32[96,768]{1,0:T(8,128)}, u32[]{:S(2)}) copy-start(f32[96,768]{1,0:T(8,128)} %get-tuple-element.76) | copy-start | bytes 884740
  322.1 7.2 %copy-start.7 = (f32[96,2304]{1,0:T(8,128)}, f32[96,2304]{1,0:T(8,128)S(1)}, u32[]{:S(2)}) copy-start(f32[96,2304]{1,0:T(8,128)S(1)} %slice_dynamic-update-slice_fusion) | copy-start | bytes 2654212
  323.3 6.0 %copy-start.6 = (f32[96,768]{1,0:T(8,128)S(1)}, f32[96,768]{1,0:T(8,128)}, u32[]{:S(2)}) copy-start(f32[96,768]{1,0:T(8,128)} %get-tuple-element.125) | copy-start | bytes 884740
  323.3 6.7 %copy-start.4 = (f32[96,3072]{1,0:T(8,128)S(1)}, f32[96,3072]{1,0:T(8,128)}, u32[]{:S(2)}) copy-start(f32[96,3072]{1,0:T(8,128)} %get-tuple-element.129) | copy-start | bytes 3538948
  329.3 1.7 copy-start.3
